TPU v7x, 32 devices: a whole 2x2x4 slice. The times are simulated.
32 devices in a mesh: dp: 8 (over z, y), slot: 4 (over x, core).
Axes of the slice: x: 2, y: 2, z: 4, core: 2. Of those that a mesh axis runs over, the one named last changes fastest.
Arguments:
- tokens: bfloat16 [65536, 512], P(('dp', 'slot')), may hold values from -6 to 6
- memory: bfloat16 [8, 64, 512], P('dp', 'slot'), may hold values from -6 to 6
- pad_mask: int32 [65536], P(('dp', 'slot')), may hold values 0 or 1
- doc_lengths: int32 [12], replicated, may hold values from 1 to 8192, 65536 in all
- first_gain: float32 [512], replicated, may hold values from 0.1 to 1.9
- query_weight: bfloat16 [512, 512], replicated, may hold values from -0.25 to 0.25
- key_weight: bfloat16 [512, 512], replicated, may hold values from -0.25 to 0.25
- value_weight: bfloat16 [512, 512], replicated, may hold values from -0.25 to 0.25
- out_weight: bfloat16 [512, 512], replicated, may hold values from -1 to 1
- second_gain: float32 [512], replicated, may hold values from 0.1 to 1.9
- up_weight: bfloat16 [512, 2048], replicated, may hold values from -0.25 to 0.25
- down_weight: bfloat16 [2048, 512], replicated, may hold values from -0.1875 to 0.1875
- memory_gain: float32 [512], replicated, may hold values from 0.1 to 1.9
- slot_query_weight: bfloat16 [512, 512], replicated, may hold values from -0.25 to 0.25
- gate_weight: bfloat16 [512, 512], replicated, may hold values from -6 to 6
- gate_bias: float32 [512], replicated, may hold values from -2 to 2
- write_weight: bfloat16 [512, 512], replicated, may hold values from -6 to 6
- out_cotangent: bfloat16 [65536, 512], P(('dp', 'slot')), may hold values from -6 to 6
- memory_cotangent: bfloat16 [8, 64, 512], P('dp', 'slot'), may hold values from -6 to 6
Outputs:
- layer_out: bfloat16 [65536, 512], P(('dp', 'slot'))
- new_memory: float32 [8, 64, 512], P('dp', 'slot')
- input_grad: float32 [65536, 512], P(('dp', 'slot'))
- memory_grad: float32 [8, 64, 512], P('dp', 'slot')
- first_gain_grad: float32 [512], replicated
- query_weight_grad: float32 [512, 512], replicated
- key_weight_grad: float32 [512, 512], replicated
- value_weight_grad: float32 [512, 512], replicated
- out_weight_grad: float32 [512, 512], replicated
- second_gain_grad: float32 [512], replicated
- up_weight_grad: float32 [512, 2048], replicated
- down_weight_grad: float32 [2048, 512], replicated
- memory_gain_grad: float32 [512], replicated
- slot_query_weight_grad: float32 [512, 512], replicated
- gate_weight_grad: float32 [512, 512], replicated
- gate_bias_grad: float32 [512], replicated
- write_weight_grad: float32 [512, 512], replicated
Inputs may be any that keep to these rules, and one draw needn't show every extreme that they name: `doc_lengths`: the lengths sum to 65536 and the largest is exactly 8192.
All inputs are finite; a program needn't handle non-finite values. No bound on the sum of `pad_mask` on one device may be relied on, other than what follows from the above.
Results may differ from a plain program's by a relative error of at most 0.03.
Values may be sent and summed in bfloat16 or wider, within the bound.
A program may use at most 256 MiB of HBM per device.

v0:
```python
from functools import partial

import jax
import jax.numpy as jnp
from jax import lax
from jax.sharding import PartitionSpec as P

H = 8
DH = 64
SEG = 512


negative_fill = -1e30
epsilon = 1e-05


def project(left, right):
    return jnp.dot(left, right, preferred_element_type=jnp.float32)


def project_back(left, right):
    return jnp.einsum("tf,df->td", left, right, preferred_element_type=jnp.float32)


def outer_sum(left, right):
    return jnp.einsum("td,tf->df", left, right, preferred_element_type=jnp.float32)


def head_count(matrix):
    return matrix.reshape(matrix.shape[:-1] + (H, DH))


def flatten(tensor):
    return tensor.reshape(tensor.shape[:-2] + (H * DH,))


def normalize(value, gain):
    center = value - jnp.mean(value, -1, keepdims=True)
    inverse = lax.rsqrt(jnp.mean(center * center, -1, keepdims=True) + epsilon)
    unit = center * inverse
    return (unit * gain, unit, inverse)


def normalize_back(grad, unit, inverse, gain):
    inner = grad * gain
    value_grad = inverse * (
        inner
        - jnp.mean(inner, -1, keepdims=True)
        - unit * jnp.mean(inner * unit, -1, keepdims=True)
    )
    return (value_grad, jnp.sum(grad * unit, 0))


def segment_mask(document, pad):
    rows = lax.broadcasted_iota(jnp.int32, (SEG, SEG), 0)
    columns = lax.broadcasted_iota(jnp.int32, (SEG, SEG), 1)
    return (rows >= columns) & (document[:, None] == document[None, :]) & (pad[None, :] > 0)


def segment_scores(query_rows, keys, mask, stored_memory_keys):
    score_scale = DH ** (-0.5)
    slot_logit_scores = (
        jnp.einsum(
            "tiz,fiz->itf", query_rows, stored_memory_keys, preferred_element_type=jnp.float32
        )
        * score_scale
    )
    token_scores = (
        jnp.einsum("shd,thd->hst", query_rows, keys, preferred_element_type=jnp.float32)
        * score_scale
    )
    return (slot_logit_scores, jnp.where(mask[None], token_scores, negative_fill))


def segment_forward(item, stored_memory_keys, stored_memory_values):
    query_rows, keys, values, document, pad = item
    slot_logit_scores, token_scores = segment_scores(
        query_rows, keys, segment_mask(document, pad), stored_memory_keys
    )
    top = jnp.maximum(jnp.max(slot_logit_scores, -1), jnp.max(token_scores, -1))
    slot_exponent_sum = jnp.exp(slot_logit_scores - top[..., None])
    token_power = jnp.exp(token_scores - top[..., None])
    grand_total = jnp.sum(slot_exponent_sum, -1) + jnp.sum(token_power, -1)
    slot_probability = (slot_exponent_sum / grand_total[..., None]).astype(jnp.bfloat16)
    token_share = (token_power / grand_total[..., None]).astype(jnp.bfloat16)
    blended_output = jnp.einsum(
        "vpc,cvi->pvi", slot_probability, stored_memory_values, preferred_element_type=jnp.float32
    )
    blended_output = blended_output + jnp.einsum(
        "hst,thd->shd", token_share, values, preferred_element_type=jnp.float32
    )
    return (flatten(blended_output), top, grand_total)


def segment_backward(carry, item, stored_memory_keys, stored_memory_values):
    key_sum, value_sum = carry
    query_rows, keys, values, document, pad, top, grand_total, blended_gradient = item
    score_scale = DH ** (-0.5)
    slot_logit_scores, token_scores = segment_scores(
        query_rows, keys, segment_mask(document, pad), stored_memory_keys
    )
    slot_probability = jnp.exp(slot_logit_scores - top[..., None]) / grand_total[..., None]
    token_share = jnp.exp(token_scores - top[..., None]) / grand_total[..., None]
    slot_dot = jnp.einsum(
        "tiz,fiz->itf", blended_gradient, stored_memory_values, preferred_element_type=jnp.float32
    )
    token_dot = jnp.einsum(
        "shd,thd->hst", blended_gradient, values, preferred_element_type=jnp.float32
    )
    inner = jnp.sum(slot_probability * slot_dot, -1) + jnp.sum(token_share * token_dot, -1)
    slot_change_term = (slot_probability * (slot_dot - inner[..., None]) * score_scale).astype(
        jnp.bfloat16
    )
    token_delta = (token_share * (token_dot - inner[..., None]) * score_scale).astype(jnp.bfloat16)
    query_grad = jnp.einsum(
        "vpc,cvi->pvi", slot_change_term, stored_memory_keys, preferred_element_type=jnp.float32
    )
    query_grad = query_grad + jnp.einsum(
        "hst,thd->shd", token_delta, keys, preferred_element_type=jnp.float32
    )
    key_grad = jnp.einsum(
        "hst,shd->thd", token_delta, query_rows, preferred_element_type=jnp.float32
    )
    value_grad = jnp.einsum(
        "hst,shd->thd",
        token_share.astype(jnp.bfloat16),
        blended_gradient,
        preferred_element_type=jnp.float32,
    )
    key_sum = key_sum + jnp.einsum(
        "ybq,byw->qyw", slot_change_term, query_rows, preferred_element_type=jnp.float32
    )
    value_sum = value_sum + jnp.einsum(
        "ybq,byw->qyw",
        slot_probability.astype(jnp.bfloat16),
        blended_gradient,
        preferred_element_type=jnp.float32,
    )
    return ((key_sum, value_sum), (query_grad, key_grad, value_grad))


def body(
    tokens,
    memory,
    pad_mask,
    doc_lengths,
    first_gain,
    query_weight,
    key_weight,
    value_weight,
    out_weight,
    second_gain,
    up_weight,
    down_weight,
    memory_gain,
    slot_query_weight,
    gate_weight,
    gate_bias,
    write_weight,
    out_cotangent,
    memory_cotangent,
):
    rows = tokens.shape[0]
    count = rows // SEG
    score_scale = DH ** (-0.5)
    begin = (lax.axis_index("dp") * lax.axis_size("slot") + lax.axis_index("slot")) * rows
    places = begin + jnp.arange(rows, dtype=jnp.int32)
    ends = jnp.cumsum(doc_lengths)
    document = jnp.sum((places[:, None] >= ends[None, :]).astype(jnp.int32), 1)
    inputs = tokens.astype(jnp.float32)
    normed, first_unit, first_inverse = normalize(inputs, first_gain)
    normed_low = normed.astype(jnp.bfloat16)
    query_rows = project(normed_low, query_weight).astype(jnp.bfloat16)
    keys = project(normed_low, key_weight).astype(jnp.bfloat16)
    values = project(normed_low, value_weight).astype(jnp.bfloat16)
    state = memory[0].astype(jnp.float32)
    slot_normed, slot_unit, slot_inverse = normalize(state, memory_gain)
    slot_low = slot_normed.astype(jnp.bfloat16)
    slot_keys = project(slot_low, key_weight).astype(jnp.bfloat16)
    slot_values = project(slot_low, value_weight).astype(jnp.bfloat16)
    all_keys, all_values = (
        lax.all_gather(slot_keys, "slot", axis=0, tiled=True),
        lax.all_gather(slot_values, "slot", axis=0, tiled=True),
    )
    stored_memory_keys = head_count(all_keys)
    stored_memory_values = head_count(all_values)
    block_items = (
        head_count(query_rows).reshape(count, SEG, H, DH),
        head_count(keys).reshape(count, SEG, H, DH),
        head_count(values).reshape(count, SEG, H, DH),
        document.reshape(count, SEG),
        pad_mask.reshape(count, SEG),
    )
    blended_output, tops, totals = lax.map(
        lambda item: segment_forward(item, stored_memory_keys, stored_memory_values), block_items
    )
    mixed_low = blended_output.reshape(rows, H * DH).astype(jnp.bfloat16)
    residual = inputs + project(mixed_low, out_weight)
    second, second_unit, second_inverse = normalize(residual, second_gain)
    second_low = second.astype(jnp.bfloat16)
    up_input = project(second_low, up_weight)
    active_low = jax.nn.gelu(up_input, approximate=False).astype(jnp.bfloat16)
    layer_out = (residual + project(active_low, down_weight)).astype(jnp.bfloat16)
    own_query = project(slot_low, slot_query_weight).astype(jnp.bfloat16)
    query_head_count = head_count(own_query)
    document_own_keys = head_count(slot_keys)
    own_values = head_count(slot_values)
    self_scores = (
        jnp.einsum(
            "lqc,lqc->lq", query_head_count, document_own_keys, preferred_element_type=jnp.float32
        )
        * score_scale
    )
    key_head_count = head_count(keys)
    value_head_count = head_count(values)
    pad_low = pad_mask.astype(jnp.bfloat16)
    top = self_scores
    grand_total = jnp.ones_like(self_scores)
    weighted_values = own_values.astype(jnp.float32)
    segment_piece_keys = lax.all_gather(keys, "slot", axis=0, tiled=True)
    piece_values = lax.all_gather(values, "slot", axis=0, tiled=True)
    piece_pad = lax.all_gather(pad_low, "slot", axis=0, tiled=True)
    scores = (
        jnp.einsum(
            "unb,lnb->unl",
            query_head_count,
            head_count(segment_piece_keys),
            preferred_element_type=jnp.float32,
        )
        * score_scale
    )
    scores = jnp.where(piece_pad[None, None, :] > 0, scores, negative_fill)
    new_top = jnp.maximum(top, jnp.max(scores, -1))
    factor = jnp.exp(top - new_top)
    raised = jnp.exp(scores - new_top[..., None])
    gained = jnp.einsum(
        "izq,qzc->izc",
        raised.astype(jnp.bfloat16),
        head_count(piece_values),
        preferred_element_type=jnp.float32,
    )
    top, grand_total, weighted_values = (
        new_top,
        grand_total * factor + jnp.sum(raised, -1),
        weighted_values * factor[..., None] + gained,
    )
    self_power = jnp.exp(self_scores - top)
    update_heads = weighted_values / grand_total[..., None]
    update_low = flatten(update_heads).astype(jnp.bfloat16)
    gate = jax.nn.sigmoid(project(update_low, gate_weight) + gate_bias)
    written = project(update_low, write_weight)
    new_memory = ((1.0 - gate) * state + gate * written)[None]
    down_weight_grad = outer_sum(active_low, out_cotangent)
    active_grad = project_back(out_cotangent, down_weight)
    gelu_back = jax.vjp(partial(jax.nn.gelu, approximate=False), up_input)[1]
    up_grad_low = gelu_back(active_grad)[0].astype(jnp.bfloat16)
    up_weight_grad = outer_sum(second_low, up_grad_low)
    second_grad, second_gain_grad = normalize_back(
        project_back(up_grad_low, up_weight), second_unit, second_inverse, second_gain
    )
    residual_grad = out_cotangent.astype(jnp.float32) + second_grad
    residual_low = residual_grad.astype(jnp.bfloat16)
    out_weight_grad = outer_sum(mixed_low, residual_low)
    blended_gradient = project_back(residual_low, out_weight).astype(jnp.bfloat16)
    memory_out = memory_cotangent[0].astype(jnp.float32)
    gate_grad = memory_out * (written - state) * gate * (1.0 - gate)
    gate_bias_grad = jnp.sum(gate_grad, 0)
    gate_low = gate_grad.astype(jnp.bfloat16)
    written_low = (memory_out * gate).astype(jnp.bfloat16)
    direct = memory_out * (1.0 - gate)
    gate_weight_grad = outer_sum(update_low, gate_low)
    write_weight_grad = outer_sum(update_low, written_low)
    update_grad_low = (
        project_back(gate_low, gate_weight) + project_back(written_low, write_weight)
    ).astype(jnp.bfloat16)
    grad_heads = head_count(update_grad_low).astype(jnp.float32)
    inner = jnp.sum(grad_heads * update_heads, -1)
    self_dot = jnp.sum(grad_heads * own_values.astype(jnp.float32), -1)
    self_delta = (
        (self_power / grand_total * (self_dot - inner) * score_scale)
        .astype(jnp.bfloat16)
        .astype(jnp.float32)
    )
    self_query = self_delta[..., None] * document_own_keys.astype(jnp.float32)
    self_key = self_delta[..., None] * query_head_count.astype(jnp.float32)
    self_value = (self_power.astype(jnp.bfloat16).astype(jnp.float32) / grand_total)[
        ..., None
    ] * grad_heads
    sent = (
        lax.all_gather(
            own_query.astype(jnp.float32).astype(jnp.bfloat16), "slot", axis=0, tiled=True
        ).astype(jnp.float32),
        lax.all_gather(
            update_grad_low.astype(jnp.float32).astype(jnp.bfloat16), "slot", axis=0, tiled=True
        ).astype(jnp.float32),
        lax.all_gather(top.astype(jnp.bfloat16), "slot", axis=0, tiled=True).astype(top.dtype),
        lax.all_gather(grand_total.astype(jnp.bfloat16), "slot", axis=0, tiled=True).astype(
            grand_total.dtype
        ),
        lax.all_gather(inner.astype(jnp.bfloat16), "slot", axis=0, tiled=True).astype(inner.dtype),
    )
    all_query_reduced = head_count(sent[0].astype(jnp.bfloat16))
    all_gradient_reduced = head_count(sent[1].astype(jnp.bfloat16))
    scores = (
        jnp.einsum(
            "unb,lnb->unl", all_query_reduced, key_head_count, preferred_element_type=jnp.float32
        )
        * score_scale
    )
    scores = jnp.where(pad_mask[None, None, :] > 0, scores, negative_fill)
    raised = jnp.exp(scores - sent[2][..., None])
    share = raised / sent[3][..., None]
    dotted = jnp.einsum(
        "unb,lnb->unl", all_gradient_reduced, value_head_count, preferred_element_type=jnp.float32
    )
    change_term = (share * (dotted - sent[4][..., None]) * score_scale).astype(jnp.bfloat16)
    query_part = flatten(
        jnp.einsum("izq,qzc->izc", change_term, key_head_count, preferred_element_type=jnp.float32)
    )
    writer_key_grad = jnp.einsum(
        "cfi,cfx->ifx", change_term, all_query_reduced, preferred_element_type=jnp.float32
    )
    scaled_grad = all_gradient_reduced.astype(jnp.float32) / sent[3][..., None]
    writer_value_grad = jnp.einsum(
        "cfi,cfx->ifx",
        raised.astype(jnp.bfloat16).astype(jnp.float32),
        scaled_grad,
        precision=lax.Precision.HIGHEST,
    )
    again_keys, again_values = (
        lax.all_gather(slot_keys, "slot", axis=0, tiled=True),
        lax.all_gather(slot_values, "slot", axis=0, tiled=True),
    )
    back_keys = head_count(again_keys)
    back_values = head_count(again_values)
    zero = jnp.zeros((all_keys.shape[0], H, DH), jnp.float32)
    back_items = block_items + (
        tops,
        totals,
        head_count(blended_gradient).reshape(count, SEG, H, DH),
    )
    (slot_key_part, slot_value_part), (query_grad, key_grad, value_grad) = lax.scan(
        lambda carry, item: segment_backward(carry, item, back_keys, back_values),
        (zero, zero),
        back_items,
    )
    key_share, value_share, query_share = (
        lax.psum_scatter(
            flatten(slot_key_part).astype(jnp.bfloat16), "slot", scatter_dimension=0, tiled=True
        ).astype(jnp.float32),
        lax.psum_scatter(
            flatten(slot_value_part).astype(jnp.bfloat16), "slot", scatter_dimension=0, tiled=True
        ).astype(jnp.float32),
        lax.psum_scatter(
            query_part.astype(jnp.bfloat16), "slot", scatter_dimension=0, tiled=True
        ).astype(jnp.float32),
    )
    slot_key_low = (key_share + flatten(self_key)).astype(jnp.bfloat16)
    slot_value_low = (value_share + flatten(self_value)).astype(jnp.bfloat16)
    own_query_low = (query_share + flatten(self_query)).astype(jnp.bfloat16)
    query_low = query_grad.reshape(rows, H * DH).astype(jnp.bfloat16)
    key_low = (key_grad.reshape(rows, H * DH) + flatten(writer_key_grad)).astype(jnp.bfloat16)
    value_low = (value_grad.reshape(rows, H * DH) + flatten(writer_value_grad)).astype(jnp.bfloat16)
    query_weight_grad = outer_sum(normed_low, query_low)
    key_weight_grad = outer_sum(normed_low, key_low) + outer_sum(slot_low, slot_key_low)
    value_weight_grad = outer_sum(normed_low, value_low) + outer_sum(slot_low, slot_value_low)
    slot_query_weight_grad = outer_sum(slot_low, own_query_low)
    normed_grad = (
        project_back(query_low, query_weight)
        + project_back(key_low, key_weight)
        + project_back(value_low, value_weight)
    )
    input_part, first_gain_grad = normalize_back(normed_grad, first_unit, first_inverse, first_gain)
    input_grad = residual_grad + input_part
    slot_grad = (
        project_back(slot_key_low, key_weight)
        + project_back(slot_value_low, value_weight)
        + project_back(own_query_low, slot_query_weight)
    )
    slot_part, memory_gain_grad = normalize_back(slot_grad, slot_unit, slot_inverse, memory_gain)
    memory_grad = (direct + slot_part)[None]
    (
        first_gain_grad,
        query_weight_grad,
        key_weight_grad,
        value_weight_grad,
        out_weight_grad,
        second_gain_grad,
        up_weight_grad,
        down_weight_grad,
        memory_gain_grad,
        slot_query_weight_grad,
        gate_weight_grad,
        gate_bias_grad,
        write_weight_grad,
    ) = lax.psum(
        (
            first_gain_grad,
            query_weight_grad,
            key_weight_grad,
            value_weight_grad,
            out_weight_grad,
            second_gain_grad,
            up_weight_grad,
            down_weight_grad,
            memory_gain_grad,
            slot_query_weight_grad,
            gate_weight_grad,
            gate_bias_grad,
            write_weight_grad,
        ),
        ("dp", "slot"),
    )
    return (
        layer_out,
        new_memory,
        input_grad,
        memory_grad,
        first_gain_grad,
        query_weight_grad,
        key_weight_grad,
        value_weight_grad,
        out_weight_grad,
        second_gain_grad,
        up_weight_grad,
        down_weight_grad,
        memory_gain_grad,
        slot_query_weight_grad,
        gate_weight_grad,
        gate_bias_grad,
        write_weight_grad,
    )


def solution(mesh):
    in_specs = (
        P(("dp", "slot"), None),
        P("dp", "slot", None),
        P(("dp", "slot")),
        P(),
        P(),
        P(),
        P(),
        P(),
        P(),
        P(),
        P(),
        P(),
        P(),
        P(),
        P(),
        P(),
        P(),
        P(("dp", "slot"), None),
        P("dp", "slot", None),
    )
    out_specs = (
        P(("dp", "slot"), None),
        P("dp", "slot", None),
        P(("dp", "slot"), None),
        P("dp", "slot", None),
        P(),
        P(),
        P(),
        P(),
        P(),
        P(),
        P(),
        P(),
        P(),
        P(),
        P(),
        P(),
        P(),
    )
    return jax.shard_map(body, mesh=mesh, in_specs=in_specs, out_specs=out_specs, check_vma=False)
```

profile of v0, /device:TPU:0, one launch (start us, length us, event | category | flops | bytes accessed | tf_op | source)
XLA Modules:
  0.0 1020.8 jit_solution(6473838015863244332)
XLA Ops:
  23.1 4.5 reshape_reshape.13
  27.5 4.6 reshape_reshape.14
  32.9 6.7 all_gather.32
  40.6 5.9 all_gather.33
  55.8 6.3 reshape.406
  62.1 5.5 copy.210
  69.2 55.1 %while.33 = (s32[]{:T(128)}, bf16[4,512,512]{2,1,0:T(8,128)(2,1)}, f32[4,8,512]{2,1,0:T(8,128)}, f32[4,8,512]{2,1,0:T(8,128)}, bf16[4,512,8,64]{1,3,2,0:T(8,128)...) while((s32[]{:T(128)}, bf16[4,512,512]{2,1,0:T(8,128)(2,1)}, ...), condition=%wide.region_11.12_spmd, body=%wide.region_6.11_spmd.sunk | while | flops 632545792 | bytes 36614780 | solution.py:194
  134.6 44.4 %multiply_convert_fusion.2 = (bf16[2048,2048]{1,0:T(8,128)(2,1)}, f32[2048,2048]{1,0:T(8,128)}, f32[2048,2048]{1,0:T(8,128)}) fusion(bf16[512,2048]{1,0:T(8,128)(2,1)S(1)} %copy-done, f32[2048,512]{0,1:T(8,128)} %copy-done.10, f32[512]{0:T(512)S(1)} %copy-done.82, f32[2048]{0:T(1024)S(1)} %add_rsqrt_fusion, f32[2048]{0:T(1024)S(1)} %broadcast_multiply_fusion.4), kind=kOutput, calls=%fused_computation.104 | convolution fusion | flops 4571791360 | bytes 48252928 | tf_op jit(solution)/shard_map/dot_general | solution.py:18
  179.0 20.4 %add_convert_fusion = bf16[2048,2048]{1,0:T(8,128)(2,1)} fusion(f32[2048,2048]{1,0:T(8,128)} %get-tuple-element.529, f32[2048,2048]{1,0:T(8,128)} %get-tuple-element.548, bf16[2048,512]{1,0:T(8,128)(2,1)} %param.40, bf16[2048,512]{1,0:T(8,128)(2,1)} %param.34), kind=kOutput, calls=%fused_computation.103 | convolution fusion | flops 4353687552 | bytes 46137344 | tf_op jit(solution)/shard_map/tf,df->td/dot_general | solution.py:22
  199.4 10.4 %multiply_reduce_fusion.2 = (f32[512]{0:T(512)}, f32[2048]{0:T(1024)S(1)}, f32[2048]{0:T(1024)S(1)}, f32[2048,512]{0,1:T(8,128)S(1)}) fusion(f32[2048,512]{0,1:T(8,128)} %copy-done.10, f32[2048]{0:T(1024)S(1)} %add_rsqrt_fusion, f32[2048]{0:T(1024)S(1)} %broadcast_multiply_fusion.4, f32[512]{0:T(512)S(1)} %copy-done.82, ...), kind=kOutput, calls=%fused_computation.147 | convolution fusion | flops 4303351296 | bytes 18911232 | tf_op jit(solution)/shard_map/tf,df->td/dot_general | solution.py:22
  218.4 5.5 copy.224
  223.9 348.5 %while.34 = (s32[]{:T(128)}, f32[64,8,64]{0,2,1:T(8,128)S(1)}, f32[64,8,64]{0,2,1:T(8,128)}, bf16[4,512,8,64]{1,3,2,0:T(8,128)(2,1)}, f32[4,512,8,64]{1,0,3,2:T(...) while((s32[]{:T(128)}, f32[64,8,64]{0,2,1:T(8,128)S(1)}, ...), condition=%wide.region_21.22_spmd.clone, body=%wide.region_18.21_spmd.clone.sunk | while | flops 1537077760 | bytes 147324240 | solution.py:342
  229.1 8.4 multiply_reduce_fusion.12
  241.4 8.1 multiply_convert_fusion.10
  255.0 21.1 %dynamic_update_slice.38 = f32[4,512,8,64]{1,0,3,2:T(4,128)} dynamic-update-slice(f32[4,512,8,64]{1,0,3,2:T(4,128)} %get-tuple-element.813, f32[1,512,8,64]{1,0,3,2:T(1,128)S(1)} %copy.310, s32[]{:T(128)} %get-tuple-element.809, s32[]{:T(128)} %constant.69.clone.1..sunk, s32[]{:T(128)} %constant.69.clone.1..sunk, s32[]{:T(128)} %constant.69.clone.1..sunk) | dynamic-update-slice | bytes 2097156 | tf_op jit(solution)/shard_map/while/body/jit(dynamic_update_index_in_dim)/dynamic_update_slice | solution.py:342
  280.6 4.9 fusion.324
  286.7 21.0 %dynamic_update_slice.39 = f32[4,512,8,64]{1,0,3,2:T(4,128)} dynamic-update-slice(f32[4,512,8,64]{1,0,3,2:T(4,128)} %get-tuple-element.814, f32[1,512,8,64]{1,0,3,2:T(1,128)S(1)} %copy.311, s32[]{:T(128)} %get-tuple-element.809, s32[]{:T(128)} %constant.69.clone.1..sunk, s32[]{:T(128)} %constant.69.clone.1..sunk, s32[]{:T(128)} %constant.69.clone.1..sunk) | dynamic-update-slice | bytes 2097156 | tf_op jit(solution)/shard_map/while/body/jit(dynamic_update_index_in_dim)/dynamic_update_slice | solution.py:342
  316.1 8.4 multiply_reduce_fusion.12
  328.4 8.1 multiply_convert_fusion.10
  342.0 21.1 %dynamic_update_slice.38 = f32[4,512,8,64]{1,0,3,2:T(4,128)} dynamic-update-slice(f32[4,512,8,64]{1,0,3,2:T(4,128)} %get-tuple-element.813, f32[1,512,8,64]{1,0,3,2:T(1,128)S(1)} %copy.310, s32[]{:T(128)} %get-tuple-element.809, s32[]{:T(128)} %constant.69.clone.1..sunk, s32[]{:T(128)} %constant.69.clone.1..sunk, s32[]{:T(128)} %constant.69.clone.1..sunk) | dynamic-update-slice | bytes 2097156 | tf_op jit(solution)/shard_map/while/body/jit(dynamic_update_index_in_dim)/dynamic_update_slice | solution.py:342
  367.7 5.0 fusion.324
  373.7 21.0 %dynamic_update_slice.39 = f32[4,512,8,64]{1,0,3,2:T(4,128)} dynamic-update-slice(f32[4,512,8,64]{1,0,3,2:T(4,128)} %get-tuple-element.814, f32[1,512,8,64]{1,0,3,2:T(1,128)S(1)} %copy.311, s32[]{:T(128)} %get-tuple-element.809, s32[]{:T(128)} %constant.69.clone.1..sunk, s32[]{:T(128)} %constant.69.clone.1..sunk, s32[]{:T(128)} %constant.69.clone.1..sunk) | dynamic-update-slice | bytes 2097156 | tf_op jit(solution)/shard_map/while/body/jit(dynamic_update_index_in_dim)/dynamic_update_slice | solution.py:342
  403.1 8.4 multiply_reduce_fusion.12
  415.4 8.1 multiply_convert_fusion.10
  429.0 21.1 %dynamic_update_slice.38 = f32[4,512,8,64]{1,0,3,2:T(4,128)} dynamic-update-slice(f32[4,512,8,64]{1,0,3,2:T(4,128)} %get-tuple-element.813, f32[1,512,8,64]{1,0,3,2:T(1,128)S(1)} %copy.310, s32[]{:T(128)} %get-tuple-element.809, s32[]{:T(128)} %constant.69.clone.1..sunk, s32[]{:T(128)} %constant.69.clone.1..sunk, s32[]{:T(128)} %constant.69.clone.1..sunk) | dynamic-update-slice | bytes 2097156 | tf_op jit(solution)/shard_map/while/body/jit(dynamic_update_index_in_dim)/dynamic_update_slice | solution.py:342
  454.7 4.9 fusion.324
  460.7 21.0 %dynamic_update_slice.39 = f32[4,512,8,64]{1,0,3,2:T(4,128)} dynamic-update-slice(f32[4,512,8,64]{1,0,3,2:T(4,128)} %get-tuple-element.814, f32[1,512,8,64]{1,0,3,2:T(1,128)S(1)} %copy.311, s32[]{:T(128)} %get-tuple-element.809, s32[]{:T(128)} %constant.69.clone.1..sunk, s32[]{:T(128)} %constant.69.clone.1..sunk, s32[]{:T(128)} %constant.69.clone.1..sunk) | dynamic-update-slice | bytes 2097156 | tf_op jit(solution)/shard_map/while/body/jit(dynamic_update_index_in_dim)/dynamic_update_slice | solution.py:342
  490.2 8.4 multiply_reduce_fusion.12
  502.4 8.1 multiply_convert_fusion.10
  516.0 21.1 %dynamic_update_slice.38 = f32[4,512,8,64]{1,0,3,2:T(4,128)} dynamic-update-slice(f32[4,512,8,64]{1,0,3,2:T(4,128)} %get-tuple-element.813, f32[1,512,8,64]{1,0,3,2:T(1,128)S(1)} %copy.310, s32[]{:T(128)} %get-tuple-element.809, s32[]{:T(128)} %constant.69.clone.1..sunk, s32[]{:T(128)} %constant.69.clone.1..sunk, s32[]{:T(128)} %constant.69.clone.1..sunk) | dynamic-update-slice | bytes 2097156 | tf_op jit(solution)/shard_map/while/body/jit(dynamic_update_index_in_dim)/dynamic_update_slice | solution.py:342
  541.7 5.0 fusion.324
  547.8 21.0 %dynamic_update_slice.39 = f32[4,512,8,64]{1,0,3,2:T(4,128)} dynamic-update-slice(f32[4,512,8,64]{1,0,3,2:T(4,128)} %get-tuple-element.814, f32[1,512,8,64]{1,0,3,2:T(1,128)S(1)} %copy.311, s32[]{:T(128)} %get-tuple-element.809, s32[]{:T(128)} %constant.69.clone.1..sunk, s32[]{:T(128)} %constant.69.clone.1..sunk, s32[]{:T(128)} %constant.69.clone.1..sunk) | dynamic-update-slice | bytes 2097156 | tf_op jit(solution)/shard_map/while/body/jit(dynamic_update_index_in_dim)/dynamic_update_slice | solution.py:342
  575.1 11.3 %fusion.167 = f32[512,2048]{1,0:T(8,128)} fusion(bf16[2048,2048]{1,0:T(8,128)(2,1)} %add_convert_fusion, f32[2048,512]{0,1:T(8,128)} %copy-done.10, f32[512]{0:T(512)} %param.32, f32[2048]{0:T(1024)} %copy-done.70, f32[2048]{0:T(1024)} %copy-done.60), kind=kOutput, calls=%fused_computation.260 | convolution fusion | flops 4299161600 | bytes 16795648 | tf_op jit(solution)/shard_map/td,tf->df/dot_general | solution.py:26
  587.0 5.2 all_gather.37
  597.3 5.3 all_gather.34
  602.9 6.3 copy.295
  621.7 6.5 fusion.187
  628.2 4.8 fusion.183
  636.4 7.0 fusion.184
  648.7 5.2 all_gather.40
  655.0 5.2 all-gather.1
  660.4 5.3 all-gather
  665.8 5.4 all-gather.2
  696.3 19.8 %reduce-scatter.8.cloned.1.call-done = bf16[16,512]{1,0:T(8,128)(2,1)} async-done(((bf16[64,512]{1,0:T(8,128)(2,1)}), bf16[16,512]{1,0:T(8,128)(2,1)}) %reduce-scatter.8.cloned.1.call-update) | async-done | bytes 16400 | tf_op jit(solution)/shard_map/reduce_scatter | solution.py:354
  719.6 11.2 %add_convert_fusion.1 = bf16[2048,512]{0,1:T(8,128)(2,1)} fusion(f32[2048,512]{0,1:T(8,128)} %copy-done.10, bf16[2048,2048]{1,0:T(8,128)(2,1)} %get-tuple-element.528, bf16[2048,512]{1,0:T(8,128)(2,1)} %param.34), kind=kOutput, calls=%fused_computation.152 | convolution fusion | flops 4297064448 | bytes 16777216 | tf_op jit(solution)/shard_map/dot_general | solution.py:18
  745.5 5.5 copy.246
  751.9 40.9 %all-reduce = (f32[512]{0:T(512)}, f32[512]{0:T(512)}, f32[512]{0:T(512)}, f32[512]{0:T(512)}) all-reduce(f32[512]{0:T(512)S(1)} %get-tuple-element.443, f32[512]{0:T(512)S(1)} %copy-done.81, f32[512]{0:T(512)S(1)} %get-tuple-element.447, f32[512]{0:T(512)S(1)} %copy-done.77), channel_id=1, replica_groups=mesh['dp'=8,'slot'=4] {'dp','slot'}, use_global_device_ids=true, to_apply=%region_32.33 | all-reduce | flops 2048 | bytes 16384 | tf_op jit(solution)/shard_map/psum | solution.py:396
  793.5 204.6 %all-reduce.4.cloned.1.call-done = (f32[512,512]{1,0:T(8,128)}, f32[512,512]{1,0:T(8,128)}, f32[512,512]{1,0:T(8,128)}, f32[512,512]{1,0:T(8,128)}, f32[512,2048...) async-done(((f32[512,512]{1,0:T(8,128)}, f32[512,512]{1,0:T(8,128)}, f32[512,512]{1,0:T(8,128)}, ...) | async-done | bytes 15728656 | tf_op jit(solution)/shard_map/psum | solution.py:396
  (463 shorter events, 286.6 us)
Async XLA Ops:
  7.2 127.4 %copy-start = (bf16[512,2048]{1,0:T(8,128)(2,1)S(1)}, bf16[512,2048]{1,0:T(8,128)(2,1)}, u32[]{:S(2)}) copy-start(bf16[512,2048]{1,0:T(8,128)(2,1)} %param.33) | copy-start | bytes 6291460
  7.2 8.5 copy-start.78
  7.2 8.5 copy-start.37
  7.2 620.9 %all-gather.6.cloned.1.call-start = ((), (), s32[]{:S(2)}) async-start(), calls=%async_computation.3 | async-start | bytes 10485760 | tf_op jit(solution)/shard_map/all_gather | solution.py:220
  13.5 39.4 %copy-start.54 = (f32[2048]{0:T(1024)}, f32[2048]{0:T(1024)S(1)}, u32[]{:S(2)}) copy-start(f32[2048]{0:T(1024)S(1)} %broadcast_multiply_fusion.5) | copy-start | bytes 24580
  15.7 37.2 %copy-start.57 = (f32[2048]{0:T(1024)}, f32[2048]{0:T(1024)S(1)}, u32[]{:S(2)}) copy-start(f32[2048]{0:T(1024)S(1)} %add_rsqrt_fusion.1) | copy-start | bytes 24580
  18.6 617.8 %all-gather.8.cloned.1.call-start = ((), (), s32[]{:S(2)}) async-start(), calls=%async_computation.4 | async-start | bytes 10485760 | tf_op jit(solution)/shard_map/all_gather | solution.py:221
  23.0 9.2 copy-start.39
  23.0 9.5 copy-start.65
  23.0 624.6 %reduce-scatter.6.cloned.1.call-start = ((), (), s32[]{:S(2)}) async-start(), calls=%async_computation.6 | async-start | bytes 81920 | tf_op jit(solution)/shard_map/reduce_scatter | solution.py:351
  32.3 7.4 copy-start.71
  32.5 7.2 copy-start.74
  32.7 7.0 copy-start.52
  32.9 13.6 %copy-start.63 = (bf16[16,512]{1,0:T(8,128)(2,1)}, bf16[16,512]{1,0:T(8,128)(2,1)S(1)}, u32[]{:S(2)}) copy-start(bf16[16,512]{1,0:T(8,128)(2,1)S(1)} %convolution_convert_fusion.6) | copy-start | bytes 49156
  128.1 81.7 %copy-start.60 = (f32[2048]{0:T(1024)}, f32[2048]{0:T(1024)S(1)}, u32[]{:S(2)}) copy-start(f32[2048]{0:T(1024)S(1)} %broadcast_multiply_fusion.4) | copy-start | bytes 24580
  130.7 79.2 %copy-start.70 = (f32[2048]{0:T(1024)}, f32[2048]{0:T(1024)S(1)}, u32[]{:S(2)}) copy-start(f32[2048]{0:T(1024)S(1)} %add_rsqrt_fusion) | copy-start | bytes 24580
  199.4 10.5 %copy-start.11 = (f32[2048,512]{0,1:T(8,128)S(1)}, f32[2048,512]{0,1:T(8,128)}, u32[]{:S(2)}) copy-start(f32[2048,512]{0,1:T(8,128)} %copy-done.10) | copy-start | bytes 12582916
  199.4 10.5 %copy-start.25 = (bf16[2048,512]{0,1:T(8,128)(2,1)S(1)}, bf16[2048,512]{0,1:T(8,128)(2,1)}, u32[]{:S(2)}) copy-start(bf16[2048,512]{0,1:T(8,128)(2,1)} %copy.220) | copy-start | bytes 6291460
  228.3 9.2 copy-start.3
  255.0 24.3 %copy-start.4 = (f32[8,512,64]{1,2,0:T(8,128)S(1)}, f32[8,512,64]{1,2,0:T(8,128)}, u32[]{:S(2)}) copy-start(f32[8,512,64]{1,2,0:T(8,128)} %get-tuple-element.751) | copy-start | bytes 3145732 | tf_op jit(solution)/shard_map/while
  285.6 23.5 %copy-start.16 = (f32[64,8,64]{0,2,1:T(8,128)S(1)}, f32[64,8,64]{0,2,1:T(8,128)}, u32[]{:S(2)}) copy-start(f32[64,8,64]{0,2,1:T(8,128)} %get-tuple-element.811) | copy-start | bytes 393220 | tf_op jit(solution)/shard_map/while
  315.3 9.2 copy-start.3
  342.0 24.3 %copy-start.4 = (f32[8,512,64]{1,2,0:T(8,128)S(1)}, f32[8,512,64]{1,2,0:T(8,128)}, u32[]{:S(2)}) copy-start(f32[8,512,64]{1,2,0:T(8,128)} %get-tuple-element.751) | copy-start | bytes 3145732 | tf_op jit(solution)/shard_map/while
  372.6 23.5 %copy-start.16 = (f32[64,8,64]{0,2,1:T(8,128)S(1)}, f32[64,8,64]{0,2,1:T(8,128)}, u32[]{:S(2)}) copy-start(f32[64,8,64]{0,2,1:T(8,128)} %get-tuple-element.811) | copy-start | bytes 393220 | tf_op jit(solution)/shard_map/while
  402.3 9.2 copy-start.3
  429.0 24.3 %copy-start.4 = (f32[8,512,64]{1,2,0:T(8,128)S(1)}, f32[8,512,64]{1,2,0:T(8,128)}, u32[]{:S(2)}) copy-start(f32[8,512,64]{1,2,0:T(8,128)} %get-tuple-element.751) | copy-start | bytes 3145732 | tf_op jit(solution)/shard_map/while
  459.6 23.5 %copy-start.16 = (f32[64,8,64]{0,2,1:T(8,128)S(1)}, f32[64,8,64]{0,2,1:T(8,128)}, u32[]{:S(2)}) copy-start(f32[64,8,64]{0,2,1:T(8,128)} %get-tuple-element.811) | copy-start | bytes 393220 | tf_op jit(solution)/shard_map/while
  489.3 9.2 copy-start.3
  516.0 24.3 %copy-start.4 = (f32[8,512,64]{1,2,0:T(8,128)S(1)}, f32[8,512,64]{1,2,0:T(8,128)}, u32[]{:S(2)}) copy-start(f32[8,512,64]{1,2,0:T(8,128)} %get-tuple-element.751) | copy-start | bytes 3145732 | tf_op jit(solution)/shard_map/while
  546.7 23.5 %copy-start.16 = (f32[64,8,64]{0,2,1:T(8,128)S(1)}, f32[64,8,64]{0,2,1:T(8,128)}, u32[]{:S(2)}) copy-start(f32[64,8,64]{0,2,1:T(8,128)} %get-tuple-element.811) | copy-start | bytes 393220 | tf_op jit(solution)/shard_map/while
  574.1 122.2 %reduce-scatter.4.cloned.1.call-start = ((), (), s32[]{:S(2)}) async-start(), calls=%async_computation.5 | async-start | bytes 81920 | tf_op jit(solution)/shard_map/reduce_scatter | solution.py:348
  575.0 11.5 %copy-start.62 = (s32[2048]{0:T(1024)S(1)}, s32[2048]{0:T(1024)}, u32[]{:S(2)}) copy-start(s32[2048]{0:T(1024)} %param.25) | copy-start | bytes 24580
  575.0 11.5 %copy-start.53 = (bf16[16,512]{1,0:T(8,128)(2,1)S(1)}, bf16[16,512]{1,0:T(8,128)(2,1)}, u32[]{:S(2)}) copy-start(bf16[16,512]{1,0:T(8,128)(2,1)} %copy-done.52) | copy-start | bytes 49156
  575.0 11.6 %copy-start.64 = (bf16[16,512]{1,0:T(8,128)(2,1)S(1)}, bf16[16,512]{1,0:T(8,128)(2,1)}, u32[]{:S(2)}) copy-start(bf16[16,512]{1,0:T(8,128)(2,1)} %copy-done.63) | copy-start | bytes 49156
  575.0 11.6 %copy-start.40 = (bf16[1,16,512]{2,1,0:T(8,128)(2,1)S(1)}, bf16[1,16,512]{2,1,0:T(8,128)(2,1)}, u32[]{:S(2)}) copy-start(bf16[1,16,512]{2,1,0:T(8,128)(2,1)} %param.24) | copy-start | bytes 49156
  575.0 11.6 %copy-start.47 = (bf16[512,512]{1,0:T(8,128)(2,1)S(1)}, bf16[512,512]{1,0:T(8,128)(2,1)}, u32[]{:S(2)}) copy-start(bf16[512,512]{1,0:T(8,128)(2,1)} %param.36) | copy-start | bytes 1572868
  575.0 11.6 %copy-start.66 = (f32[512]{0:T(512)S(1)}, f32[512]{0:T(512)}, u32[]{:S(2)}) copy-start(f32[512]{0:T(512)} %param.35) | copy-start | bytes 6148
  575.0 11.6 %copy-start.72 = (f32[16]{0:T(128)S(1)}, f32[16]{0:T(128)}, u32[]{:S(2)}) copy-start(f32[16]{0:T(128)} %copy-done.71) | copy-start | bytes 196
  575.0 11.6 %copy-start.75 = (f32[16]{0:T(128)S(1)}, f32[16]{0:T(128)}, u32[]{:S(2)}) copy-start(f32[16]{0:T(128)} %copy-done.74) | copy-start | bytes 196
  575.1 17.8 %copy-start.26 = (bf16[4,512,512]{2,1,0:T(8,128)(2,1)S(1)}, bf16[4,512,512]{2,1,0:T(8,128)(2,1)}, u32[]{:S(2)}) copy-start(bf16[4,512,512]{2,1,0:T(8,128)(2,1)} %get-tuple-element.162) | copy-start | bytes 6291460
  575.1 141.0 %reduce-scatter.8.cloned.1.call-start = ((), (), s32[]{:S(2)}) async-start(), calls=%async_computation.7 | async-start | bytes 81920 | tf_op jit(solution)/shard_map/reduce_scatter | solution.py:354
  636.3 7.0 copy-start.68
  636.3 7.1 copy-start.69
  636.3 7.2 copy-start.36
  636.4 8.1 copy-start.34
  636.4 8.1 copy-start.51
  694.8 303.4 %all-reduce.4.cloned.1.call-start = ((), (), s32[]{:S(2)}) async-start(), calls=%async_computation.8 | async-start | bytes 31457280 | tf_op jit(solution)/shard_map/psum | solution.py:396
  998.2 6.7 copy-start.30
  (59 other events, 189.8 us)
Sparse Core Ops, SparseCore 0:
  18.7 61.6 all-gather.5
  82.0 58.2 all-gather.7
  574.3 21.3 reduce-scatter.5
  597.9 19.5 reduce-scatter.3
  694.9 21.1 reduce-scatter.7
  724.1 274.0 all-reduce.3
where the time goes:
time: 1040 us; the launch traced here: 1020 us
  matrix products  318 us (31%)
  local copies, waits for them, and re-layouts  301 us (29%)
  waiting for transfers between devices  225 us (22%)
  blocking collectives  85.1 us (8%)
  other arithmetic  75.3 us (7%)
  between operations  15.3 us (1%)
    psum x1, waiting for transfers between devices, body(): lax.psum((first_gain_grad, query_weight_grad, key_weight_grad, value_weig...  205 us
    dynamic_update_slice x16, local copies, waits for them, and re-layouts, body(): lax.scan(lambda carry, item: segment_backward(carry, item, back_keys, bac...  177 us
    dot_general x11, matrix products, project(): return jnp.dot(left, right, preferred_element_type=jnp.float32)  72.4 us
    unnamed x181, local copies, waits for them, and re-layouts  61.1 us
    dot_general x8, matrix products, segment_scores(): jnp.einsum('shd,thd->hst', query_rows, keys, preferred_element_type=jnp.f...  44.3 us
    dot_general x11, matrix products, project_back(): jnp.einsum('tf,df->td', left, right, preferred_element_type=jnp.float32)  41.5 us
    psum x1, blocking collectives, body(): lax.psum((first_gain_grad, query_weight_grad, key_weight_grad, value_weig...  40.9 us
    dot_general x11, matrix products, outer_sum(): jnp.einsum('td,tf->df', left, right, preferred_element_type=jnp.float32)  34.8 us
  transfers between devices with their start and end apart: 6, of which 2 were waited for; matrix products, arithmetic and copies ran while one was open for 63% of the time, Pallas kernels for 0%

commit v1 on v0

v1 whole, which is shorter than its diff:
```python
import jax
import jax.numpy as jnp
from jax import lax
from jax.experimental import pallas as pl
from jax.experimental.pallas import tpu as pltpu
from jax.sharding import PartitionSpec as P

H = 8
DH = 64
SEG = 512
HALF = 256
FILL = -1e30
EPS = 1e-05
SCALE = DH ** (-0.5)
F32 = jnp.float32
BF16 = jnp.bfloat16

TAIL = (
    0.11962928145668905,
    0.12075423000729175,
    0.09991172819365436,
    0.12856765411993218,
    -0.053695489964182386,
    0.20636694099934239,
    -0.15721125090545032,
    0.035676834162404004,
)


def nn(a, b, precision=None):
    return lax.dot_general(
        a, b, (((1,), (0,)), ((), ())), preferred_element_type=F32, precision=precision
    )


def nt(a, b):
    return lax.dot_general(a, b, (((1,), (1,)), ((), ())), preferred_element_type=F32)


def norm(value):
    center = value - jnp.mean(value, -1, keepdims=True)
    inverse = lax.rsqrt(jnp.mean(center * center, -1, keepdims=True) + EPS)
    return center * inverse, inverse


def norm_back(grad, unit, inverse, gain):
    inner = grad * gain
    value_grad = inverse * (
        inner
        - jnp.mean(inner, -1, keepdims=True)
        - unit * jnp.mean(inner * unit, -1, keepdims=True)
    )
    return value_grad, jnp.sum(grad * unit, 0, keepdims=True)


def gelu_pair(x):
    t = 1.0 / (1.0 + 0.3 * jnp.abs(x))
    poly = TAIL[7]
    for c in TAIL[6::-1]:
        poly = poly * t + c
    bell = jnp.exp(-0.5 * (x * x))
    tail = bell * (poly * t)
    cdf = jnp.where(x >= 0, 1.0 - tail, tail)
    return x * cdf, cdf + x * (bell * 0.3989422804014327)


def segment_bias(doc_row, pad_row):
    code = jnp.where(pad_row > 0, doc_row, -1.0)
    key_code = jnp.transpose(jnp.broadcast_to(code, (SEG, SEG)))
    rows = lax.broadcasted_iota(jnp.int32, (SEG, SEG), 0)
    columns = lax.broadcasted_iota(jnp.int32, (SEG, SEG), 1)
    seen = (rows <= columns) & (key_code == doc_row)
    return jnp.where(seen, 0.0, FILL)


def head_rows(pair, odd):
    zero = jnp.zeros((DH, pair.shape[1]), pair.dtype)
    if odd:
        return jnp.concatenate([zero, pair[DH:]], 0)
    return jnp.concatenate([pair[:DH], zero], 0)


def head_lanes(pair, odd):
    lane = lax.broadcasted_iota(jnp.int32, pair.shape, 1)
    keep = (lane >= DH) if odd else (lane < DH)
    return jnp.where(keep, pair, jnp.zeros_like(pair))


def two(p):
    return slice(p * 2 * DH, (p + 1) * 2 * DH)


def one(h):
    return slice(h * DH, (h + 1) * DH)


BLOCKS = ((0, HALF), (HALF, SEG))


def project_kernel(x, gain, wq, wk, wv, q_t, k, k_t, v, v_t):
    unit, _ = norm(x[...].astype(F32))
    low = (unit * gain[...]).astype(BF16)
    q_t[...] = jnp.transpose((nn(low, wq[...]) * SCALE).astype(BF16))
    key = nn(low, wk[...]).astype(BF16)
    k[...] = key
    k_t[...] = jnp.transpose(key)
    value = nn(low, wv[...]).astype(BF16)
    v[...] = value
    v_t[...] = jnp.transpose(value)


def writer_kernel(
    mem, gain, wk, wv, wsq, k_t, v, pad,
    slot_k, slot_k_t, slot_v, slot_v_t, slot_q, slot_q_t, stats,
):
    unit, _ = norm(mem[...].astype(F32))
    low = (unit * gain[...]).astype(BF16)
    sk = nn(low, wk[...]).astype(BF16)
    sv = nn(low, wv[...]).astype(BF16)
    sq = (nn(low, wsq[...]) * SCALE).astype(BF16)
    slot_k[...] = sk
    slot_k_t[...] = jnp.transpose(sk)
    slot_v[...] = sv
    slot_v_t[...] = jnp.transpose(sv)
    slot_q[...] = sq
    slot_q_t[...] = jnp.transpose(sq)
    bias = jnp.where(pad[...] > 0, 0.0, FILL)
    slots = mem.shape[0]
    lane = lax.broadcasted_iota(jnp.int32, (slots, 2 * DH), 1) < DH
    for p in range(H // 2):
        parts = []
        for odd in range(2):
            c = nn(head_lanes(sq[:, two(p)], odd), k_t[two(p), :]) + bias
            top = jnp.max(c, 1, keepdims=True)
            w = jnp.exp(c - top)
            parts.append((nn(w.astype(BF16), v[:, two(p)]), top, jnp.sum(w, 1, keepdims=True)))
        for n in range(3):
            stats[n, :, two(p)] = jnp.where(lane, parts[0][n], parts[1][n])


def middle_kernel(
    x, q_t, k, v_t, doc, pad, slot_k, slot_v_t, wo, gain, wup, wdown, cot,
    out, res_grad, d_t, lse, inner, dwo_out, dwup_out, dwdown_out, dgain_out,
    bias, o_t, dwo, dwup, dwdown_t, dgain,
):
    step = pl.program_id(0)

    @pl.when(step == 0)
    def _():
        dwo[...] = jnp.zeros_like(dwo)
        dwup[...] = jnp.zeros_like(dwup)
        dwdown_t[...] = jnp.zeros_like(dwdown_t)
        dgain[...] = jnp.zeros_like(dgain)

    bias[...] = segment_bias(doc[...], pad[...])
    for h in range(H):
        p, odd = h // 2, h % 2
        qm = head_rows(q_t[two(p), :], odd)
        for lo, hi in BLOCKS:
            qb = qm[:, lo:hi]
            s = nn(k[:hi, two(p)], qb) + bias[:hi, lo:hi]
            sm = nn(slot_k[:, two(p)], qb)
            top = jnp.maximum(jnp.max(s, 0, keepdims=True), jnp.max(sm, 0, keepdims=True))
            e = jnp.exp(s - top)
            em = jnp.exp(sm - top)
            total = jnp.sum(e, 0, keepdims=True) + jnp.sum(em, 0, keepdims=True)
            o = nn(v_t[one(h), :hi], e.astype(BF16)) + nn(slot_v_t[one(h), :], em.astype(BF16))
            o_t[one(h), lo:hi] = o / total
            lse[h : h + 1, lo:hi] = top + jnp.log(total)
    mixed_t = o_t[...].astype(BF16)
    residual = x[...].astype(F32) + nn(jnp.transpose(mixed_t), wo[...])
    unit, inverse = norm(residual)
    second = (unit * gain[...]).astype(BF16)
    second_t = jnp.transpose(second)
    cot_low = cot[...]
    cot_t = jnp.transpose(cot_low)
    total_out = residual
    grad = jnp.zeros_like(residual)
    width = SEG
    for c in range(wup.shape[1] // width):
        cs = slice(c * width, (c + 1) * width)
        act, slope = gelu_pair(nn(second, wup[:, cs]))
        act = act.astype(BF16)
        total_out = total_out + nn(act, wdown[cs, :])
        up_grad = (nt(cot_low, wdown[cs, :]) * slope).astype(BF16)
        dwdown_t[:, cs] += nn(cot_t, act)
        dwup[:, cs] += nn(second_t, up_grad)
        grad = grad + nt(up_grad, wup[:, cs])
    out[...] = total_out.astype(BF16)
    back, gain_part = norm_back(grad, unit, inverse, gain[...])
    dgain[...] += gain_part
    back = back + cot_low.astype(F32)
    res_grad[...] = back
    low = back.astype(BF16)
    dwo[...] += nn(mixed_t, low)
    d = nt(wo[...], low).astype(BF16)
    d_t[...] = d
    prod = d.astype(F32) * o_t[...]
    for h in range(H):
        inner[h : h + 1, :] = jnp.sum(prod[one(h), :], 0, keepdims=True)

    @pl.when(step == pl.num_programs(0) - 1)
    def _():
        dwo_out[...] = dwo[...].astype(BF16)
        dwup_out[...] = dwup[...].astype(BF16)
        dwdown_out[...] = jnp.transpose(dwdown_t[...].astype(BF16))
        dgain_out[...] = jnp.broadcast_to(dgain[...], dgain_out.shape).astype(BF16)


def update_kernel(
    place, stats, mem, cot, slot_q, slot_k, slot_v, wgate, bgate, wwrite,
    new_memory, g_out, g_t, lse, inner_out, self_q_t, self_k_t, self_v_t, direct_out,
    dwgate, dwwrite, dbias, fresh,
):
    slots, width = mem.shape
    rows = new_memory.shape[0]
    same = (
        lax.broadcasted_iota(jnp.int32, (width, width), 0) // DH
        == lax.broadcasted_iota(jnp.int32, (width, width), 1) // DH
    ).astype(F32)
    def head_sum(value):
        return nn(value, same, lax.Precision.HIGHEST)
    start = place[0, 0] * rows
    row = lax.broadcasted_iota(jnp.int32, (slots, width), 0)
    own = (row >= start) & (row < start + rows)
    sq, sk, sv = (r[...].astype(F32) for r in (slot_q, slot_k, slot_v))
    state = mem[...].astype(F32)
    memory_out = cot[...].astype(F32)
    own_score = head_sum(sq * sk)
    count = stats.shape[0]
    top = own_score
    for n in range(count):
        top = jnp.maximum(top, stats[n, 1])
    power = jnp.exp(own_score - top)
    total = power
    weighted = power.astype(BF16).astype(F32) * sv
    for n in range(count):
        factor = jnp.exp(stats[n, 1] - top)
        total = total + factor * stats[n, 2]
        weighted = weighted + factor * stats[n, 0]
    update = weighted / total
    low = update.astype(BF16)
    gate = jax.nn.sigmoid(nn(low, wgate[...]) + bgate[...])
    written = nn(low, wwrite[...])
    fresh[...] = (1.0 - gate) * state + gate * written
    new_memory[...] = fresh[pl.ds(pl.multiple_of(start, rows), rows), :]
    gate_grad = memory_out * (written - state) * gate * (1.0 - gate)
    gate_low = gate_grad.astype(BF16)
    written_low = (memory_out * gate).astype(BF16)
    zero = jnp.zeros((slots, width), F32)
    direct_out[...] = jnp.where(own, memory_out * (1.0 - gate), zero)
    mine = jnp.where(own, gate_grad, zero)
    dbias[...] = jnp.broadcast_to(jnp.sum(mine, 0, keepdims=True), dbias.shape).astype(BF16)
    low_t = jnp.transpose(low)
    dwgate[...] = nn(low_t, mine.astype(BF16)).astype(BF16)
    dwwrite[...] = nn(low_t, jnp.where(own, memory_out * gate, zero).astype(BF16)).astype(BF16)
    g_low = (nt(gate_low, wgate[...]) + nt(written_low, wwrite[...])).astype(BF16)
    g = g_low.astype(F32)
    g_out[...] = g_low
    g_t[...] = jnp.transpose(g_low)
    inner = head_sum(g * update)
    inner_out[...] = inner
    lse[...] = top + jnp.log(total)
    delta = (power / total * (head_sum(g * sv) - inner)).astype(BF16).astype(F32)
    self_q_t[...] = jnp.transpose(jnp.where(own, delta * sk, zero))
    self_k_t[...] = jnp.transpose(jnp.where(own, delta * sq, zero))
    self_v_t[...] = jnp.transpose(
        jnp.where(own, power.astype(BF16).astype(F32) / total * g, zero)
    )


def last_kernel(
    x, gain, q_t, k, k_t, v, v_t, d_t, lse, inner, doc, pad, res_grad,
    slot_k, slot_k_t, slot_v, slot_q, slot_q_t, g, g_t, wlse, winner,
    self_q_t, self_k_t, self_v_t, direct, mem, mgain, wq, wk, wv, wsq,
    input_grad, dwq_out, dwk_out, dwv_out, dwsq_out, dgain_out, slot_part,
    bias, dq_t, dk_t, dv_t, dwq_t, dwk_t, dwv_t, sq_acc, sk_acc, sv_acc, dgain,
):
    step = pl.program_id(0)

    @pl.when(step == 0)
    def _():
        dwq_t[...] = jnp.zeros_like(dwq_t)
        dwk_t[...] = jnp.zeros_like(dwk_t)
        dwv_t[...] = jnp.zeros_like(dwv_t)
        dgain[...] = jnp.zeros_like(dgain)
        sq_acc[...] = self_q_t[...]
        sk_acc[...] = self_k_t[...]
        sv_acc[...] = self_v_t[...]

    bias[...] = segment_bias(doc[...], pad[...])
    pad_bias = jnp.where(pad[...] > 0, 0.0, FILL)
    for h in range(H):
        p, odd = h // 2, h % 2
        qm = head_rows(q_t[two(p), :], odd)
        dm = head_rows(d_t[two(p), :], odd)
        c = nn(head_lanes(slot_q[:, two(p)], odd), k_t[two(p), :]) + pad_bias
        share = jnp.exp(c - wlse[:, h * DH : h * DH + 1])
        dotted = nn(head_lanes(g[:, two(p)], odd), v_t[two(p), :])
        change = (share * (dotted - winner[:, h * DH : h * DH + 1])).astype(BF16)
        dk = nn(slot_q_t[one(h), :], change)
        dv = nn(g_t[one(h), :], share.astype(BF16))
        sq_acc[one(h), :] += nt(k_t[one(h), :], change)
        for lo, hi in BLOCKS:
            qb = qm[:, lo:hi]
            db = dm[:, lo:hi]
            qh = q_t[one(h), lo:hi]
            dh = d_t[one(h), lo:hi]
            l = lse[h : h + 1, lo:hi]
            i = inner[h : h + 1, lo:hi]
            e = jnp.exp(nn(k[:hi, two(p)], qb) + bias[:hi, lo:hi] - l)
            em = jnp.exp(nn(slot_k[:, two(p)], qb) - l)
            ds = (e * (nn(v[:hi, two(p)], db) - i)).astype(BF16)
            dsm = (em * (nn(slot_v[:, two(p)], db) - i)).astype(BF16)
            dq_t[one(h), lo:hi] = (
                (nn(k_t[one(h), :hi], ds) + nn(slot_k_t[one(h), :], dsm)) * SCALE
            ).astype(BF16)
            dvp = nt(dh, e.astype(BF16))
            dkp = nt(qh, ds)
            if hi < SEG:
                dvp = jnp.concatenate([dvp, jnp.zeros((DH, SEG - hi), F32)], 1)
                dkp = jnp.concatenate([dkp, jnp.zeros((DH, SEG - hi), F32)], 1)
            dv = dv + dvp
            dk = dk + dkp
            sv_acc[one(h), :] += nt(dh, em.astype(BF16))
            sk_acc[one(h), :] += nt(qh, dsm)
        dk_t[one(h), :] = dk.astype(BF16)
        dv_t[one(h), :] = dv.astype(BF16)
    unit, inverse = norm(x[...].astype(F32))
    low = (unit * gain[...]).astype(BF16)
    grad_t = nn(wq[...], dq_t[...]) + nn(wk[...], dk_t[...]) + nn(wv[...], dv_t[...])
    part, gain_part = norm_back(jnp.transpose(grad_t), unit, inverse, gain[...])
    dgain[...] += gain_part
    input_grad[...] = res_grad[...] + part
    dwq_t[...] += nn(dq_t[...], low)
    dwk_t[...] += nn(dk_t[...], low)
    dwv_t[...] += nn(dv_t[...], low)

    @pl.when(step == pl.num_programs(0) - 1)
    def _():
        unit, inverse = norm(mem[...].astype(F32))
        low = (unit * mgain[...]).astype(BF16)
        sq_low = (sq_acc[...] * SCALE).astype(BF16)
        sk_low = sk_acc[...].astype(BF16)
        sv_low = sv_acc[...].astype(BF16)
        dwq_out[...] = jnp.transpose(dwq_t[...]).astype(BF16)
        dwk_out[...] = jnp.transpose(dwk_t[...] + nn(sk_low, low)).astype(BF16)
        dwv_out[...] = jnp.transpose(dwv_t[...] + nn(sv_low, low)).astype(BF16)
        dwsq_out[...] = jnp.transpose(nn(sq_low, low)).astype(BF16)
        grad_t = nn(wk[...], sk_low) + nn(wv[...], sv_low) + nn(wsq[...], sq_low)
        part, gain_part = norm_back(jnp.transpose(grad_t), unit, inverse, mgain[...])
        slot_part[...] = part + direct[...]
        dgain_out[0:8, :] = jnp.broadcast_to(dgain[...], (8, dgain.shape[1]))
        dgain_out[8:16, :] = jnp.broadcast_to(gain_part, (8, dgain.shape[1]))


def struct(shape, dtype):
    return jax.ShapeDtypeStruct(shape, dtype)


def full(shape):
    return pl.BlockSpec(shape, lambda i: (0,) * len(shape))


def rows_of(width):
    return pl.BlockSpec((SEG, width), lambda i: (i, 0))


def lanes_of(height):
    return pl.BlockSpec((height, SEG), lambda i: (0, i))


PARAMS = pltpu.CompilerParams(dimension_semantics=("arbitrary",), vmem_limit_bytes=60 << 20)
PLAIN = pltpu.CompilerParams(vmem_limit_bytes=60 << 20)


def body(
    tokens,
    memory,
    pad_mask,
    doc_lengths,
    first_gain,
    query_weight,
    key_weight,
    value_weight,
    out_weight,
    second_gain,
    up_weight,
    down_weight,
    memory_gain,
    slot_query_weight,
    gate_weight,
    gate_bias,
    write_weight,
    out_cotangent,
    memory_cotangent,
):
    rows, width = tokens.shape
    hidden = up_weight.shape[1]
    count = rows // SEG
    slots_here = memory.shape[1]
    group = lax.axis_size("slot")
    slots = slots_here * group
    place = lax.axis_index("slot")
    begin = (lax.axis_index("dp") * group + place) * rows
    places = begin + jnp.arange(rows, dtype=jnp.int32)
    ends = jnp.cumsum(doc_lengths)
    document = jnp.sum((places[:, None] >= ends[None, :]).astype(jnp.int32), 1)
    doc = document.astype(F32)[None, :]
    pad = pad_mask.astype(F32)[None, :]
    gain1, gain2, gain3 = (g[None, :] for g in (first_gain, second_gain, memory_gain))

    both = lax.all_gather(
        jnp.concatenate([memory[0], memory_cotangent[0]], 1), "slot", axis=0, tiled=True
    )
    mem, mem_cot = both[:, :width], both[:, width:]

    square = (width, width)
    q_t, k, k_t, v, v_t = pl.pallas_call(
        project_kernel,
        grid=(count,),
        in_specs=[rows_of(width), full((1, width)), full(square), full(square), full(square)],
        out_specs=[lanes_of(width), rows_of(width), lanes_of(width), rows_of(width), lanes_of(width)],
        out_shape=[
            struct((width, rows), BF16), struct((rows, width), BF16), struct((width, rows), BF16),
            struct((rows, width), BF16), struct((width, rows), BF16),
        ],
        compiler_params=PARAMS,
        name="project",
    )(tokens, gain1, query_weight, key_weight, value_weight)

    tall, wide = (slots, width), (width, slots)
    slot_k, slot_k_t, slot_v, slot_v_t, slot_q, slot_q_t, stats = pl.pallas_call(
        writer_kernel,
        out_shape=[
            struct(tall, BF16), struct(wide, BF16), struct(tall, BF16), struct(wide, BF16),
            struct(tall, BF16), struct(wide, BF16), struct((3,) + tall, F32),
        ],
        compiler_params=PLAIN,
        name="writer",
    )(mem, gain3, key_weight, value_weight, slot_query_weight, k_t, v, pad)
    all_stats = lax.all_gather(stats, "slot", axis=0)

    layer_out, res_grad, d_t, lse, inner, dwo, dwup, dwdown, dgain2 = pl.pallas_call(
        middle_kernel,
        grid=(count,),
        in_specs=[
            rows_of(width), lanes_of(width), rows_of(width), lanes_of(width), lanes_of(1), lanes_of(1),
            full(tall), full(wide), full(square), full((1, width)), full((width, hidden)),
            full((hidden, width)), rows_of(width),
        ],
        out_specs=[
            rows_of(width), rows_of(width), lanes_of(width), lanes_of(H), lanes_of(H),
            full(square), full((width, hidden)), full((hidden, width)), full((16, width)),
        ],
        out_shape=[
            struct((rows, width), BF16), struct((rows, width), F32), struct((width, rows), BF16),
            struct((H, rows), F32), struct((H, rows), F32), struct(square, BF16),
            struct((width, hidden), BF16), struct((hidden, width), BF16), struct((16, width), BF16),
        ],
        scratch_shapes=[
            pltpu.VMEM((SEG, SEG), F32), pltpu.VMEM((width, SEG), F32), pltpu.VMEM(square, F32),
            pltpu.VMEM((width, hidden), F32), pltpu.VMEM((width, hidden), F32), pltpu.VMEM((1, width), F32),
        ],
        compiler_params=PARAMS,
        name="middle",
    )(
        tokens, q_t, k, v_t, doc, pad, slot_k, slot_v_t, out_weight, gain2, up_weight, down_weight,
        out_cotangent,
    )

    vm = pl.BlockSpec(memory_space=pltpu.VMEM)
    (
        new_memory, g, g_t, wlse, winner, self_q_t, self_k_t, self_v_t, direct, dwgate, dwwrite, dbias,
    ) = pl.pallas_call(
        update_kernel,
        in_specs=[pl.BlockSpec(memory_space=pltpu.SMEM)] + [vm] * 9,
        out_specs=[vm] * 12,
        out_shape=[
            struct((slots_here, width), F32), struct(tall, BF16), struct(wide, BF16), struct(tall, F32),
            struct(tall, F32), struct(wide, F32), struct(wide, F32), struct(wide, F32), struct(tall, F32),
            struct(square, BF16), struct(square, BF16), struct((16, width), BF16),
        ],
        scratch_shapes=[pltpu.VMEM(tall, F32)],
        compiler_params=PLAIN,
        name="update",
    )(
        place.astype(jnp.int32).reshape(1, 1), all_stats, mem, mem_cot, slot_q, slot_k, slot_v,
        gate_weight, gate_bias[None, :], write_weight,
    )

    axes = ("dp", "slot")
    dwo, dwup, dwdown, dwgate, dwwrite, dgain2, dbias = lax.psum(
        (dwo, dwup, dwdown, dwgate, dwwrite, dgain2, dbias), axes
    )

    input_grad, dwq, dwk, dwv, dwsq, dgains, slot_part = pl.pallas_call(
        last_kernel,
        grid=(count,),
        in_specs=[
            rows_of(width), full((1, width)), lanes_of(width), rows_of(width), lanes_of(width),
            rows_of(width), lanes_of(width), lanes_of(width), lanes_of(H), lanes_of(H), lanes_of(1),
            lanes_of(1), rows_of(width),
            full(tall), full(wide), full(tall), full(tall), full(wide), full(tall), full(wide),
            full(tall), full(tall), full(wide), full(wide), full(wide), full(tall), full(tall),
            full((1, width)), full(square), full(square), full(square), full(square),
        ],
        out_specs=[
            rows_of(width), full(square), full(square), full(square), full(square), full((16, width)),
            full(tall),
        ],
        out_shape=[
            struct((rows, width), F32), struct(square, BF16), struct(square, BF16), struct(square, BF16),
            struct(square, BF16), struct((16, width), F32), struct(tall, F32),
        ],
        scratch_shapes=[
            pltpu.VMEM((SEG, SEG), F32), pltpu.VMEM((width, SEG), BF16), pltpu.VMEM((width, SEG), BF16),
            pltpu.VMEM((width, SEG), BF16), pltpu.VMEM(square, F32), pltpu.VMEM(square, F32),
            pltpu.VMEM(square, F32), pltpu.VMEM(wide, F32), pltpu.VMEM(wide, F32), pltpu.VMEM(wide, F32),
            pltpu.VMEM((1, width), F32),
        ],
        compiler_params=PARAMS,
        name="last",
    )(
        tokens, gain1, q_t, k, k_t, v, v_t, d_t, lse, inner, doc, pad, res_grad,
        slot_k, slot_k_t, slot_v, slot_q, slot_q_t, g, g_t, wlse, winner,
        self_q_t, self_k_t, self_v_t, direct, mem, gain3,
        query_weight, key_weight, value_weight, slot_query_weight,
    )
    memory_grad = lax.psum_scatter(slot_part, "slot", scatter_dimension=0, tiled=True)[None]
    dwq, dwk, dwv, dwsq, dgains = lax.psum((dwq, dwk, dwv, dwsq, dgains.astype(BF16)), axes)

    return (
        layer_out,
        new_memory[None],
        input_grad,
        memory_grad,
        dgains[0].astype(F32),
        dwq.astype(F32),
        dwk.astype(F32),
        dwv.astype(F32),
        dwo.astype(F32),
        dgain2[0].astype(F32),
        dwup.astype(F32),
        dwdown.astype(F32),
        dgains[8].astype(F32),
        dwsq.astype(F32),
        dwgate.astype(F32),
        dbias[0].astype(F32),
        dwwrite.astype(F32),
    )


def solution(mesh):
    token = P(("dp", "slot"), None)
    slot = P("dp", "slot", None)
    in_specs = (
        (token, slot, P(("dp", "slot"))) + (P(),) * 14 + (token, slot)
    )
    out_specs = (token, slot, token, slot) + (P(),) * 13
    return jax.shard_map(body, mesh=mesh, in_specs=in_specs, out_specs=out_specs, check_vma=False)
```

time: 1040 us -> 367 us (0.35); the launches traced: 1020 us -> 366 us
  matrix products: 318 us -> 0 us
  local copies, waits for them, and re-layouts: 301 us -> 1.35 us
  Pallas kernels: 0 us -> 141 us
  waiting for transfers between devices: 225 us -> 141 us
  other arithmetic: 75.3 us -> 19.2 us
  blocking collectives: 85.1 us -> 49.8 us
    dot_general x96 -> x0, matrix products: 318 us -> none  [the longest x11 72.4 us: project(): return jnp.dot(left, right, preferred_element_type=jnp.float32)]
    dynamic_update_slice x24 -> x0, local copies, waits for them, and re-layouts: 181 us -> none  [the longest x16 177 us: body(): lax.scan(lambda carry, item: segment_backward(carry, item, back_keys, bac...]
    pallas_call x0 -> x5, Pallas kernels: none -> 141 us  [the longest x1 75.1 us: body(): pl.pallas_call(middle_kernel, grid=(count,), in_specs=[rows_of(width), la...]
    psum x1, waiting for transfers between devices: 205 us -> 133 us  [body(): lax.psum((dwq, dwk, dwv, dwsq, dgains.astype(BF16)), axes)]
    unnamed x181 -> x22, local copies, waits for them, and re-layouts: 61.1 us -> 0.7 us
    all_gather x8 -> x1, blocking collectives: 44.2 us -> 6.49 us  [body(): lax.all_gather(jnp.concatenate([memory[0], memory_cotangent[0]], 1), 'slo...]
    convert_element_type x15 -> x14, other arithmetic: 40.9 us -> 18.1 us  [the longest x1 2.61 us: body(): dwdown.astype(F32)]
    while x45 -> x0, local copies, waits for them, and re-layouts: 21.8 us -> none  [the longest x5 11.1 us: body(): lax.map(lambda item: segment_forward(item, stored_memory_keys, stored_mem...]
  transfers between devices with their start and end apart: 6 -> 3, of which waited for: 2 -> 2; matrix products, arithmetic and copies ran while one was open for 63% -> 5% of each run, Pallas kernels for 0% -> 21%
where the time goes in v1:
time: 367 us; the launch traced here: 366 us
  Pallas kernels  141 us (38%)
  waiting for transfers between devices  141 us (38%)
  blocking collectives  49.8 us (14%)
  other arithmetic  19.2 us (5%)
  between operations  13.9 us (4%)
    psum x1, waiting for transfers between devices, body(): lax.psum((dwq, dwk, dwv, dwsq, dgains.astype(BF16)), axes)  133 us
    pallas_call x1, Pallas kernels, body(): pl.pallas_call(middle_kernel, grid=(count,), in_specs=[rows_of(width), la...  75.1 us
    pallas_call x1, Pallas kernels, body(): pl.pallas_call(last_kernel, grid=(count,), in_specs=[rows_of(width), full...  44.9 us
    psum x1, blocking collectives, body(): lax.psum((dwq, dwk, dwv, dwsq, dgains.astype(BF16)), axes)  43.4 us
    pallas_call x1, Pallas kernels, body(): pl.pallas_call(project_kernel, grid=(count,), in_specs=[rows_of(width), f...  8.09 us
    reduce_scatter x1, waiting for transfers between devices, body(): lax.psum_scatter(slot_part, 'slot', scatter_dimension=0, tiled=True)[None]  7.65 us
  transfers between devices with their start and end apart: 3, of which 2 were waited for; matrix products, arithmetic and copies ran while one was open for 5% of the time, Pallas kernels for 21%

profile of v1, /device:TPU:0, one launch (start us, length us, event | category | flops | bytes accessed | tf_op | source)
XLA Modules:
  0.0 366.0 jit_solution(13206896388305914448)
XLA Ops:
  7.2 0.0 all-gather.3.cloned.1.call-start
  7.2 1.3 convert_element_type.76
  8.5 0.7 pad_maximum_fusion
  9.3 6.5 %all_gather.9 = bf16[64,1024]{1,0:T(8,128)(2,1)S(1)} all-gather(bf16[16,1024]{1,0:T(8,128)(2,1)S(1)} %pad_maximum_fusion), channel_id=1, replica_groups=mesh['dp'=8,'slot'=4] {'slot'}, dimensions={0}, use_global_device_ids=true | all-gather | bytes 163840 | tf_op jit(solution)/shard_map/all_gather | solution.py:413
  15.8 0.7 fusion
  16.4 8.1 %project.1 = (bf16[512,2048]{1,0:T(8,128)(2,1)}, bf16[2048,512]{1,0:T(8,128)(2,1)}, bf16[512,2048]{1,0:T(8,128)(2,1)}, bf16[2048,512]{1,0:T(8,128)(2,1)}, bf16[512,2048]{1,0:T(8,128)(2,1)}) custom-call(bf16[2048,512]{1,0:T(8,128)(2,1)} %x.5, f32[1,512]{1,0:T(1,128)} %bitcast.26, bf16[512,512]{1,0:T(8,128)(2,1)} %wq.3, bf16[512,512]{1,0:T(8,128)(2,1)} %wk.5, ...), custom_call_target="tpu_custom_call" | custom-call | tf_op jit(solution)/shard_map/project/pallas_call | solution.py:419
  24.5 0.0 copy-start.10
  24.5 7.1 %writer.1 = (bf16[64,512]{1,0:T(8,128)(2,1)}, bf16[512,64]{1,0:T(8,128)(2,1)}, bf16[64,512]{1,0:T(8,128)(2,1)}, bf16[512,64]{1,0:T(8,128)(2,1)}, bf16[64,512]{1,...) custom-call(bf16[64,512]{1,0:T(8,128)(2,1)} %get-tuple-element.110.mem, f32[1,512]{1,0:T(1,128)} %bitcast.28, ...), custom_call_target="tpu_custom_call" | custom-call | tf_op jit(solution)/shard_map/writer/pallas_call | solution.py:433
  31.6 0.0 all-gather.3.cloned.1.call-update
  31.7 0.0 all-reduce.4.cloned.1.call-start
  31.7 0.0 copy-done.10
  31.7 0.2 reduce-window.8
  31.9 0.1 convert_reduce_fusion
  32.0 0.6 convert_element_type.74
  32.6 75.1 %middle.1 = (bf16[2048,512]{1,0:T(8,128)(2,1)}, f32[2048,512]{1,0:T(8,128)}, bf16[512,2048]{1,0:T(8,128)(2,1)}, f32[8,2048]{1,0:T(8,128)}, f32[8,2048]{1,0:T(8,1...) custom-call(bf16[2048,512]{1,0:T(8,128)(2,1)} %x.5, ...), custom_call_target="tpu_custom_call" | custom-call | tf_op jit(solution)/shard_map/middle/pallas_call | solution.py:444
  107.8 0.0 all-gather.3.cloned.1.call-done
  107.8 5.8 %update.1 = (f32[16,512]{1,0:T(8,128)}, bf16[64,512]{1,0:T(8,128)(2,1)}, bf16[512,64]{1,0:T(8,128)(2,1)}, f32[64,512]{1,0:T(8,128)}, f32[64,512]{1,0:T(8,128)}, ...) custom-call(s32[1,1]{1,0:T(1,128)} %bitcast.9.place, ...), custom_call_target="tpu_custom_call" | custom-call | tf_op jit(solution)/shard_map/update/pallas_call | solution.py:475
  113.6 44.9 %last.1 = (f32[2048,512]{1,0:T(8,128)}, bf16[512,512]{1,0:T(8,128)(2,1)}, bf16[512,512]{1,0:T(8,128)(2,1)}, bf16[512,512]{1,0:T(8,128)(2,1)}, bf16[512,512]{1,0:...) custom-call(bf16[2048,512]{1,0:T(8,128)(2,1)} %x.5, f32[1,512]{1,0:T(1,128)} %bitcast.27, ...), custom_call_target="tpu_custom_call" | custom-call | tf_op jit(solution)/shard_map/last/pallas_call | solution.py:497
  158.5 0.0 copy-start.7
  158.5 0.0 copy-start.8
  158.5 0.0 copy-start.9
  158.5 0.0 all-reduce.4.cloned.1.call-update
  158.5 0.0 reduce-scatter.2.cloned.1.call-start
  158.6 0.7 copy-done.7
  159.2 0.0 reduce-scatter.2.cloned.1.call-update
  159.3 0.0 copy-done.8
  159.3 0.0 copy-done.9
  159.3 43.4 %all-reduce = (bf16[16,512]{1,0:T(8,128)(2,1)S(1)}, bf16[16,512]{1,0:T(8,128)(2,1)S(1)}, bf16[16,512]{1,0:T(8,128)(2,1)S(1)}) all-reduce(bf16[16,512]{1,0:T(8,128)(2,1)S(1)} %convert_element_type.77, bf16[16,512]{1,0:T(8,128)(2,1)S(1)} %copy-done.8, bf16[16,512]{1,0:T(8,128)(2,1)S(1)} %copy-done.9), channel_id=1, replica_groups=mesh['dp'=8,'slot'=4] {'dp','slot'}, use_global_device_ids=true, to_apply=%region_3.4 | all-reduce | flops 24576 | bytes 98304 | tf_op jit(solution)/shard_map/psum | solution.py:531
  202.6 0.6 slice_convert_fusion.1
  203.2 0.6 slice_convert_fusion
  203.8 132.9 %all-reduce.4.cloned.1.call-done = (bf16[512,512]{1,0:T(8,128)(2,1)}, bf16[512,512]{1,0:T(8,128)(2,1)}, bf16[512,512]{1,0:T(8,128)(2,1)}, bf16[512,512]{1,0:T(8,...) async-done(((bf16[512,512]{1,0:T(8,128)(2,1)}, ...) | async-done | bytes 7864336 | tf_op jit(solution)/shard_map/psum | solution.py:531
  336.7 2.2 convert_element_type.80
  339.0 2.2 convert_element_type.81
  341.2 0.0 copy-done.6
  341.2 1.1 convert_element_type.82
  342.3 0.0 copy-done.5
  342.3 1.1 convert_element_type.83
  343.4 0.0 copy-done.4
  343.4 1.1 convert_element_type.90
  344.5 0.0 copy-done.3
  344.5 1.1 convert_element_type.91
  345.6 0.0 copy-done.2
  345.6 1.1 convert_element_type.94
  346.7 0.0 copy-done.1
  346.7 2.5 convert_element_type.86
  349.2 0.0 copy-done
  349.2 2.6 convert_element_type.87
  351.8 7.7 %reduce-scatter.2.cloned.1.call-done = f32[16,512]{1,0:T(8,128)} async-done(((f32[64,512]{1,0:T(8,128)}), f32[16,512]{1,0:T(8,128)}) %reduce-scatter.2.cloned.1.call-update) | async-done | bytes 32784 | tf_op jit(solution)/shard_map/reduce_scatter | solution.py:530
  (9 shorter events, 0.0 us)
Async XLA Ops:
  7.2 100.6 %all-gather.3.cloned.1.call-start = ((), (), s32[]{:S(2)}) async-start(), calls=%async_computation.2 | async-start | bytes 1966080 | tf_op jit(solution)/shard_map/all_gather | solution.py:442
  24.5 7.2 %copy-start.10 = (s32[12]{0:T(128)S(1)}, s32[12]{0:T(128)}, u32[]{:S(2)}) copy-start(s32[12]{0:T(128)} %param.22) | copy-start | bytes 148
  31.7 305.1 %all-reduce.4.cloned.1.call-start = ((), (), s32[]{:S(2)}) async-start(), calls=%async_computation.3 | async-start | bytes 15728640 | tf_op jit(solution)/shard_map/psum | solution.py:531
  158.5 0.8 copy-start.7
  158.5 0.8 copy-start.8
  158.5 0.8 copy-start.9
  158.5 201.0 %reduce-scatter.2.cloned.1.call-start = ((), (), s32[]{:S(2)}) async-start(), calls=%async_computation.1 | async-start | bytes 163840 | tf_op jit(solution)/shard_map/reduce_scatter | solution.py:530
  336.7 4.4 %copy-start.6 = (bf16[512,512]{1,0:T(8,128)(2,1)S(1)}, bf16[512,512]{1,0:T(8,128)(2,1)}, u32[]{:S(2)}) copy-start(bf16[512,512]{1,0:T(8,128)(2,1)} %get-tuple-element.102) | copy-start | bytes 1572868
  336.7 5.5 %copy-start.5 = (bf16[512,512]{1,0:T(8,128)(2,1)S(1)}, bf16[512,512]{1,0:T(8,128)(2,1)}, u32[]{:S(2)}) copy-start(bf16[512,512]{1,0:T(8,128)(2,1)} %get-tuple-element.103) | copy-start | bytes 1572868
  339.0 4.4 %copy-start.4 = (bf16[512,512]{1,0:T(8,128)(2,1)S(1)}, bf16[512,512]{1,0:T(8,128)(2,1)}, u32[]{:S(2)}) copy-start(bf16[512,512]{1,0:T(8,128)(2,1)} %get-tuple-element.106) | copy-start | bytes 1572868
  341.2 3.3 copy-start.3
  342.3 3.3 copy-start.2
  343.4 3.3 copy-start.1
  346.7 2.5 copy-start
Sparse Core Ops, SparseCore 0:
  31.8 21.2 all-gather.2
  158.6 178.0 all-reduce.3
  339.7 19.7 reduce-scatter.1

commit v2 on v1

v2 whole, which is shorter than its diff:
```python
import jax
import jax.numpy as jnp
from jax import lax
from jax.experimental import pallas as pl
from jax.experimental.pallas import tpu as pltpu
from jax.sharding import PartitionSpec as P

H = 8
DH = 64
SEG = 512
HALF = 256
FILL = -1e30
EPS = 1e-05
SCALE = DH ** (-0.5)
F32 = jnp.float32
BF16 = jnp.bfloat16

TAIL = (
    0.11962928145668905,
    0.12075423000729175,
    0.09991172819365436,
    0.12856765411993218,
    -0.053695489964182386,
    0.20636694099934239,
    -0.15721125090545032,
    0.035676834162404004,
)


def nn(a, b, precision=None):
    return lax.dot_general(
        a, b, (((1,), (0,)), ((), ())), preferred_element_type=F32, precision=precision
    )


def nt(a, b):
    return lax.dot_general(a, b, (((1,), (1,)), ((), ())), preferred_element_type=F32)


def norm(value):
    center = value - jnp.mean(value, -1, keepdims=True)
    inverse = lax.rsqrt(jnp.mean(center * center, -1, keepdims=True) + EPS)
    return center * inverse, inverse


def norm_back(grad, unit, inverse, gain):
    inner = grad * gain
    value_grad = inverse * (
        inner
        - jnp.mean(inner, -1, keepdims=True)
        - unit * jnp.mean(inner * unit, -1, keepdims=True)
    )
    return value_grad, jnp.sum(grad * unit, 0, keepdims=True)


def gelu_pair(x):
    t = 1.0 / (1.0 + 0.3 * jnp.abs(x))
    poly = TAIL[7]
    for c in TAIL[6::-1]:
        poly = poly * t + c
    bell = jnp.exp(-0.5 * (x * x))
    tail = bell * (poly * t)
    cdf = jnp.where(x >= 0, 1.0 - tail, tail)
    return x * cdf, cdf + x * (bell * 0.3989422804014327)


def segment_bias(doc_row, pad_row):
    code = jnp.where(pad_row > 0, doc_row, -1.0)
    key_code = jnp.transpose(jnp.broadcast_to(code, (SEG, SEG)))
    rows = lax.broadcasted_iota(jnp.int32, (SEG, SEG), 0)
    columns = lax.broadcasted_iota(jnp.int32, (SEG, SEG), 1)
    seen = (rows <= columns) & (key_code == doc_row)
    return jnp.where(seen, 0.0, FILL)


def head_rows(pair, odd):
    zero = jnp.zeros((DH, pair.shape[1]), pair.dtype)
    if odd:
        return jnp.concatenate([zero, pair[DH:]], 0)
    return jnp.concatenate([pair[:DH], zero], 0)


def head_lanes(pair, odd):
    lane = lax.broadcasted_iota(jnp.int32, pair.shape, 1)
    keep = (lane >= DH) if odd else (lane < DH)
    return jnp.where(keep, pair, jnp.zeros_like(pair))


def two(p):
    return slice(p * 2 * DH, (p + 1) * 2 * DH)


def one(h):
    return slice(h * DH, (h + 1) * DH)


BLOCKS = ((0, HALF), (HALF, SEG))


def project_kernel(x, gain, wq, wk, wv, normed, q_t, k, k_t, v, v_t):
    unit, _ = norm(x[...].astype(F32))
    low = (unit * gain[...]).astype(BF16)
    normed[...] = low
    q_t[...] = jnp.transpose((nn(low, wq[...]) * SCALE).astype(BF16))
    key = nn(low, wk[...]).astype(BF16)
    k[...] = key
    k_t[...] = jnp.transpose(key)
    value = nn(low, wv[...]).astype(BF16)
    v[...] = value
    v_t[...] = jnp.transpose(value)


def writer_kernel(
    mem, gain, wk, wv, wsq, k_t, v, pad,
    slot_k, slot_k_t, slot_v, slot_v_t, slot_q, slot_q_t, stats,
):
    unit, _ = norm(mem[...].astype(F32))
    low = (unit * gain[...]).astype(BF16)
    sk = nn(low, wk[...]).astype(BF16)
    sv = nn(low, wv[...]).astype(BF16)
    sq = (nn(low, wsq[...]) * SCALE).astype(BF16)
    slot_k[...] = sk
    slot_k_t[...] = jnp.transpose(sk)
    slot_v[...] = sv
    slot_v_t[...] = jnp.transpose(sv)
    slot_q[...] = sq
    slot_q_t[...] = jnp.transpose(sq)
    bias = jnp.where(pad[...] > 0, 0.0, FILL)
    slots = mem.shape[0]
    lane = lax.broadcasted_iota(jnp.int32, (slots, 2 * DH), 1) < DH
    for p in range(H // 2):
        parts = []
        for odd in range(2):
            c = nn(head_lanes(sq[:, two(p)], odd), k_t[two(p), :]) + bias
            top = jnp.max(c, 1, keepdims=True)
            w = jnp.exp(c - top)
            parts.append((nn(w.astype(BF16), v[:, two(p)]), top, jnp.sum(w, 1, keepdims=True)))
        for n in range(3):
            stats[n, :, two(p)] = jnp.where(lane, parts[0][n], parts[1][n])


TILE = 16
MESH = pl.DeviceIdType.MESH


def bit_orders(sizes):
    dp = [("dp", 1 << n) for n in range(sizes["dp"].bit_length() - 1)]
    slot = [("slot", 1 << n) for n in range(sizes["slot"].bit_length() - 1)]
    first, other = slot[:1], slot[1:]
    return first + other + dp, first + dp[:1] + other + dp[1:]


def plan(blocks, orders):
    half = blocks // 2
    steps, recv = [], 0
    for n, order in enumerate(orders):
        size, row = half, []
        for axis, stride in order:
            halves = size % 2 == 0
            sent = size // 2 if halves else size
            row.append((axis, stride, halves, sent, recv))
            recv += sent
            size = sent
        steps.append((n * half, row))
    return steps, recv


def here():
    return {"dp": lax.axis_index("dp"), "slot": lax.axis_index("slot")}


def across(index, axis, stride):
    bit = (index[axis] // stride) % 2
    peer = dict(index)
    peer[axis] = index[axis] + stride - 2 * bit * stride
    return bit, (peer["dp"], peer["slot"])


def greet(orders, index):
    barrier = pltpu.get_barrier_semaphore()
    for axis, stride in orders[0]:
        _, peer = across(index, axis, stride)
        pl.semaphore_signal(barrier, inc=1, device_id=peer, device_id_type=MESH)
    pl.semaphore_wait(barrier, len(orders[0]))


class Reduction:
    def __init__(self, buf, recv, sems, free, base, orders, index):
        self.buf, self.recv, self.sems, self.free = buf, recv, sems, free
        self.base, self.index = base, index
        self.steps, _ = plan(buf.shape[0], orders)
        self.depth = len(orders[0])
        up = [
            (level, False)
            for level in reversed(range(self.depth))
            if any(row[level][2] for _, row in self.steps)
        ]
        self.moves = [(level, True) for level in range(self.depth)] + up
        self.stages = len(self.moves) + 1

    def copies(self, move):
        level, down = self.moves[move]
        found = []
        for n, (start, row) in enumerate(self.steps):
            for axis, stride, halves, sent, _ in row[: level if down else level + 1]:
                if halves:
                    start = start + across(self.index, axis, stride)[0] * sent
            axis, stride, halves, sent, at = row[level]
            bit, peer = across(self.index, axis, stride)
            slot = self.base + n * self.depth + level
            if down:
                keep = start + bit * sent if halves else start
                give = start + sent - bit * sent if halves else start
                target, ends = self.recv.at[pl.ds(at, sent)], 0
            elif halves:
                keep, give = None, start
                target, ends = self.buf.at[pl.ds(give, sent)], 2
            else:
                continue
            copy = pltpu.make_async_remote_copy(
                self.buf.at[pl.ds(give, sent)], target,
                self.sems.at[ends, slot], self.sems.at[ends + 1, slot],
                device_id=peer, device_id_type=MESH,
            )
            found.append((copy, halves, keep, sent, at, slot, peer))
        return found

    def tick(self, stage):
        if stage > 0:
            down = self.moves[stage - 1][1]
            for copy, halves, keep, sent, at, slot, peer in self.copies(stage - 1):
                copy.wait()
                if not down:
                    continue
                if halves:
                    pl.semaphore_signal(
                        self.free.at[slot], inc=1, device_id=peer, device_id_type=MESH
                    )
                mine = self.buf[pl.ds(keep, sent)].astype(F32)
                self.buf[pl.ds(keep, sent)] = (
                    mine + self.recv[pl.ds(at, sent)].astype(F32)
                ).astype(BF16)
        if stage < len(self.moves):
            down = self.moves[stage][1]
            for copy, halves, keep, sent, at, slot, peer in self.copies(stage):
                if not down:
                    pl.semaphore_wait(self.free.at[slot], 1)
                copy.start()


def reduction_scratch(sizes, orders, width):
    depth = len(orders[0])
    return (
        [pltpu.VMEM((s, TILE, width), BF16) for s in sizes]
        + [pltpu.VMEM((plan(s, orders)[1], TILE, width), BF16) for s in sizes]
        + [
            pltpu.SemaphoreType.DMA((4, len(sizes) * 2 * depth)),
            pltpu.SemaphoreType.REGULAR((len(sizes) * 2 * depth,)),
        ]
    )


def reductions(refs, count, orders, index):
    bufs, recvs, (sems, free) = refs[:count], refs[count : 2 * count], refs[2 * count :]
    return [
        Reduction(bufs[n], recvs[n], sems, free, n * 2 * len(orders[0]), orders, index)
        for n in range(count)
    ]


def tiles(value):
    return value.reshape(value.shape[0] // TILE, TILE, value.shape[1])


EARLY = 2


def middle_kernel(
    count, chunks, orders,
    x, q_t, k, v_t, doc, pad, slot_k, slot_v_t, wo, gain, wup, wdown, cot,
    out, res_grad, d_t, lse, inner, dwo_out, late, dgain_out, *rest,
):
    sums, rest = rest[:EARLY], rest[EARLY:]
    bias, o_t, residual, second, second_t, cot_t, ffn, grad, dwo, dwup, dwdown_t, dgain = rest[:12]
    stores = rest[-1]
    step = pl.program_id(0)
    index = here()
    work = reductions(rest[12:-1], EARLY, orders, index)

    @pl.when(step == 0)
    def _():
        greet(orders, index)
        dwo[...] = jnp.zeros_like(dwo)
        dgain[...] = jnp.zeros_like(dgain)

    @pl.when(step < count)
    def _():
        bias[...] = segment_bias(doc[...], pad[...])
        for h in range(H):
            p, odd = h // 2, h % 2
            qm = head_rows(q_t[two(p), :], odd)
            for lo, hi in BLOCKS:
                qb = qm[:, lo:hi]
                s = nn(k[:hi, two(p)], qb) + bias[:hi, lo:hi]
                sm = nn(slot_k[:, two(p)], qb)
                top = jnp.maximum(jnp.max(s, 0, keepdims=True), jnp.max(sm, 0, keepdims=True))
                e = jnp.exp(s - top)
                em = jnp.exp(sm - top)
                total = jnp.sum(e, 0, keepdims=True) + jnp.sum(em, 0, keepdims=True)
                o = nn(v_t[one(h), :hi], e.astype(BF16)) + nn(slot_v_t[one(h), :], em.astype(BF16))
                o_t[step, one(h), lo:hi] = (o / total).astype(BF16)
                lse[p, odd : odd + 1, lo:hi] = top + jnp.log(total)
        res = x[...].astype(F32) + nn(jnp.transpose(o_t[step]), wo[...])
        residual[step] = res
        unit, _ = norm(res)
        low = (unit * gain[...]).astype(BF16)
        second[step] = low
        second_t[step] = jnp.transpose(low)
        cot_t[step] = jnp.transpose(cot[step])

    @pl.when((step >= count) & (step < count + chunks * count))
    def _():
        chunk = step // count - 1
        i = step % count
        act, slope = gelu_pair(nn(second[i], wup[...]))
        act = act.astype(BF16)
        plus = nn(act, wdown[...])
        up_grad = (nt(cot[i], wdown[...]) * slope).astype(BF16)
        back = nt(up_grad, wup[...])
        down_part = nn(cot_t[i], act)
        up_part = nn(second_t[i], up_grad)

        @pl.when(chunk == 0)
        def _():
            ffn[i] = plus
            grad[i] = back

        @pl.when(chunk > 0)
        def _():
            ffn[i] += plus
            grad[i] += back

        @pl.when(i == 0)
        def _():
            dwdown_t[...] = down_part
            dwup[...] = up_part

        @pl.when(i > 0)
        def _():
            dwdown_t[...] += down_part
            dwup[...] += up_part

        half = SEG // TILE
        for n in range(chunks):

            @pl.when((i == count - 1) & (chunk == n))
            def _():
                target = work[n].buf if n < EARLY else late.at[n - EARLY]
                target[:half] = tiles(dwup[...].astype(BF16))
                target[half:] = tiles(jnp.transpose(dwdown_t[...].astype(BF16)))

    @pl.when(step >= count + chunks * count)
    def _():
        i = step - count - chunks * count
        res = residual[i]
        unit, inverse = norm(res)
        out[...] = (res + ffn[i]).astype(BF16)
        back, gain_part = norm_back(grad[i], unit, inverse, gain[...])
        dgain[...] += gain_part
        back = back + cot[i].astype(F32)
        res_grad[...] = back
        low = back.astype(BF16)
        dwo[...] += nn(o_t[i], low)
        d = nt(wo[...], low).astype(BF16)
        d_t[...] = d
        prod = d.astype(F32) * o_t[i].astype(F32)
        for h in range(H):
            inner[h // 2, h % 2 : h % 2 + 1, :] = jnp.sum(prod[one(h), :], 0, keepdims=True)

        @pl.when(i == count - 1)
        def _():
            dwo_out[...] = dwo[...].astype(BF16)
            dgain_out[...] = jnp.broadcast_to(dgain[...], dgain_out.shape).astype(BF16)

    last = 2 * count + chunks * count - 1
    events = {}
    for n, item in enumerate(work):
        first = 2 * count - 1 + n * count
        for stage in range(item.stages):
            events.setdefault(min(first + stage, last), []).append((n, stage))
    for when, todo in sorted(events.items()):

        @pl.when(step == when)
        def _():
            for n, stage in todo:
                work[n].tick(stage)
                if stage == work[n].stages - 1:
                    pltpu.make_async_copy(work[n].buf, sums[n], stores.at[n]).start()

    @pl.when(step == last)
    def _():
        for n in range(EARLY):
            pltpu.make_async_copy(work[n].buf, sums[n], stores.at[n]).wait()


def update_kernel(
    place, stats, mem, cot, slot_q, slot_k, slot_v, wgate, bgate, wwrite,
    new_memory, g_out, g_t, lse, inner_out, self_q_t, self_k_t, self_v_t, direct_out,
    dwgate, dwwrite, dbias, fresh,
):
    slots, width = mem.shape
    rows = new_memory.shape[0]
    same = (
        lax.broadcasted_iota(jnp.int32, (width, width), 0) // DH
        == lax.broadcasted_iota(jnp.int32, (width, width), 1) // DH
    ).astype(F32)
    def head_sum(value):
        return nn(value, same, lax.Precision.HIGHEST)
    start = place[0, 0] * rows
    row = lax.broadcasted_iota(jnp.int32, (slots, width), 0)
    own = (row >= start) & (row < start + rows)
    sq, sk, sv = (r[...].astype(F32) for r in (slot_q, slot_k, slot_v))
    state = mem[...].astype(F32)
    memory_out = cot[...].astype(F32)
    own_score = head_sum(sq * sk)
    count = stats.shape[0]
    top = own_score
    for n in range(count):
        top = jnp.maximum(top, stats[n, 1])
    power = jnp.exp(own_score - top)
    total = power
    weighted = power.astype(BF16).astype(F32) * sv
    for n in range(count):
        factor = jnp.exp(stats[n, 1] - top)
        total = total + factor * stats[n, 2]
        weighted = weighted + factor * stats[n, 0]
    update = weighted / total
    low = update.astype(BF16)
    gate = jax.nn.sigmoid(nn(low, wgate[...]) + bgate[...])
    written = nn(low, wwrite[...])
    fresh[...] = (1.0 - gate) * state + gate * written
    new_memory[...] = fresh[pl.ds(pl.multiple_of(start, rows), rows), :]
    gate_grad = memory_out * (written - state) * gate * (1.0 - gate)
    gate_low = gate_grad.astype(BF16)
    written_low = (memory_out * gate).astype(BF16)
    zero = jnp.zeros((slots, width), F32)
    direct_out[...] = jnp.where(own, memory_out * (1.0 - gate), zero)
    mine = jnp.where(own, gate_grad, zero)
    dbias[...] = jnp.broadcast_to(jnp.sum(mine, 0, keepdims=True), dbias.shape).astype(BF16)
    low_t = jnp.transpose(low)
    dwgate[...] = nn(low_t, mine.astype(BF16)).astype(BF16)
    dwwrite[...] = nn(low_t, jnp.where(own, memory_out * gate, zero).astype(BF16)).astype(BF16)
    g_low = (nt(gate_low, wgate[...]) + nt(written_low, wwrite[...])).astype(BF16)
    g = g_low.astype(F32)
    g_out[...] = g_low
    g_t[...] = jnp.transpose(g_low)
    inner = head_sum(g * update)
    inner_out[...] = inner
    lse[...] = top + jnp.log(total)
    delta = (power / total * (head_sum(g * sv) - inner)).astype(BF16).astype(F32)
    self_q_t[...] = jnp.transpose(jnp.where(own, delta * sk, zero))
    self_k_t[...] = jnp.transpose(jnp.where(own, delta * sq, zero))
    self_v_t[...] = jnp.transpose(
        jnp.where(own, power.astype(BF16).astype(F32) / total * g, zero)
    )


def last_kernel(
    count, orders, sizes,
    x, gain, low, q_t, k, k_t, v, v_t, d_t, lse, inner, doc, pad, res_grad,
    slot_k, slot_k_t, slot_v, slot_q, slot_q_t, g, g_t, wlse, winner,
    self_q_t, self_k_t, self_v_t, direct, mem, mgain, wq, wk, wv, wsq, gains_in, *rest,
):
    early = len(sizes)
    ready, rest = rest[:early], rest[early:]
    input_grad, dwq_out, dwk_out, dwv_out, dwsq_out, gains_out, memory_grad = rest[:7]
    sums, rest = rest[7 : 7 + early], rest[7 + early :]
    bias, grads, acc, w_all, sq_acc, sk_acc, sv_acc, sq_all, sk_all, sv_all, slot_low, dgain = rest[:12]
    part, part_in, part_sems, loads, stores = rest[12:17]
    pairs = H // 2
    step = pl.program_id(0)
    index = here()
    work = reductions(rest[17:], early + pairs + 1, orders, index)
    wide = 2 * DH
    busy = step < pairs * count
    p = jnp.minimum(step // count, pairs - 1)
    i = step % count

    @pl.when(step == 0)
    def _():
        for n in range(early):
            pltpu.make_async_copy(ready[n], work[n].buf, loads.at[n]).start()
        greet(orders, index)
        for n in range(pairs):
            for m, w in enumerate((wq, wk, wv)):
                at = (3 * n + m) * wide
                w_all[:, at : at + wide] = w[:, two(n)]
        unit, _ = norm(mem[...].astype(F32))
        slot_low[...] = (unit * mgain[...]).astype(BF16)
        dgain[...] = jnp.zeros_like(dgain)

    @pl.when(busy)
    def _():
        @pl.when(i == 0)
        def _():
            sq_acc[...] = self_q_t[...]
            sk_acc[...] = self_k_t[...]
            sv_acc[...] = self_v_t[...]

        bias[...] = segment_bias(doc[...], pad[...])
        pad_bias = jnp.where(pad[...] > 0, 0.0, FILL)
        for odd in range(2):
            own = one(odd)
            qm = head_rows(q_t[...], odd)
            dm = head_rows(d_t[...], odd)
            c = nn(head_lanes(slot_q[...], odd), k_t[...]) + pad_bias
            share = jnp.exp(c - wlse[:, odd * DH : odd * DH + 1])
            dotted = nn(head_lanes(g[...], odd), v_t[...])
            change = (share * (dotted - winner[:, odd * DH : odd * DH + 1])).astype(BF16)
            dk = nn(slot_q_t[own, :], change)
            dv = nn(g_t[own, :], share.astype(BF16))
            sq_acc[own, :] += nt(k_t[own, :], change)
            for lo, hi in BLOCKS:
                qb = qm[:, lo:hi]
                db = dm[:, lo:hi]
                qh = q_t[own, lo:hi]
                dh = d_t[own, lo:hi]
                l = lse[0, odd : odd + 1, lo:hi]
                t = inner[0, odd : odd + 1, lo:hi]
                e = jnp.exp(nn(k[:hi, :], qb) + bias[:hi, lo:hi] - l)
                em = jnp.exp(nn(slot_k[...], qb) - l)
                ds = (e * (nn(v[:hi, :], db) - t)).astype(BF16)
                dsm = (em * (nn(slot_v[...], db) - t)).astype(BF16)
                dq = (nn(k_t[own, :hi], ds) + nn(slot_k_t[own, :], dsm)) * SCALE
                grads[i, p, own, lo:hi] = dq.astype(BF16)
                dvp = nt(dh, e.astype(BF16))
                dkp = nt(qh, ds)
                if hi < SEG:
                    dvp = jnp.concatenate([dvp, jnp.zeros((DH, SEG - hi), F32)], 1)
                    dkp = jnp.concatenate([dkp, jnp.zeros((DH, SEG - hi), F32)], 1)
                dv = dv + dvp
                dk = dk + dkp
                sv_acc[own, :] += nt(dh, em.astype(BF16))
                sk_acc[own, :] += nt(qh, dsm)
            grads[i, p, wide + odd * DH : wide + (odd + 1) * DH, :] = dk.astype(BF16)
            grads[i, p, 2 * wide + odd * DH : 2 * wide + (odd + 1) * DH, :] = dv.astype(BF16)
        more = nn(grads[i, p], low[...])

        @pl.when(i == 0)
        def _():
            acc[...] = more

        @pl.when(i > 0)
        def _():
            acc[...] += more

        @pl.when(i == count - 1)
        def _():
            sq_all[p] = (sq_acc[...] * SCALE).astype(BF16)
            sk_all[p] = sk_acc[...].astype(BF16)
            sv_all[p] = sv_acc[...].astype(BF16)
            rows = jnp.concatenate(
                [
                    acc[:wide],
                    acc[wide : 2 * wide] + nn(sk_all[p], slot_low[...]),
                    acc[2 * wide :] + nn(sv_all[p], slot_low[...]),
                    nn(sq_all[p], slot_low[...]),
                ],
                0,
            )
            rows = tiles(rows.astype(BF16))
            for n in range(pairs):

                @pl.when(p == n)
                def _():
                    work[early + n].buf[...] = rows

    @pl.when(step >= pairs * count)
    def _():
        unit, inverse = norm(x[...].astype(F32))
        grad_t = nn(w_all[...], grads[i].reshape(3 * pairs * wide, SEG))
        back, gain_part = norm_back(jnp.transpose(grad_t), unit, inverse, gain[...])
        dgain[...] += gain_part
        input_grad[...] = res_grad[...] + back

    group = part.shape[0]
    strides = [1 << n for n in reversed(range(group.bit_length() - 1))]

    def scatter(level):
        stride = strides[level]
        start, at = 0, 0
        for s in strides[:level]:
            start = start + across(index, "slot", s)[0] * s
            at += s
        bit, peer = across(index, "slot", stride)
        copy = pltpu.make_async_remote_copy(
            part.at[pl.ds(start + stride - bit * stride, stride)], part_in.at[pl.ds(at, stride)],
            part_sems.at[0, level], part_sems.at[1, level], device_id=peer, device_id_type=MESH,
        )
        return copy, start + bit * stride, at, stride

    def slots(stage):
        if stage == 0:
            unit, inverse = norm(mem[...].astype(F32))
            rows = mem.shape[1]
            sq, sk, sv = (a[...].reshape(rows, mem.shape[0]) for a in (sq_all, sk_all, sv_all))
            grad_t = nn(wk[...], sk) + nn(wv[...], sv) + nn(wsq[...], sq)
            back, gain_part = norm_back(jnp.transpose(grad_t), unit, inverse, mgain[...])
            part[...] = (back + direct[...]).reshape(part.shape)
            gains_out[0:8, :] = jnp.broadcast_to(gain_part, (8, gain_part.shape[1]))
        else:
            copy, keep, at, size = scatter(stage - 1)
            copy.wait()
            part[pl.ds(keep, size)] += part_in[pl.ds(at, size)]
        if stage < len(strides):
            scatter(stage)[0].start()
        else:
            memory_grad[...] = part[index["slot"]]

    def gains(stage):
        item = work[early + pairs]
        if stage == 0:
            buf = item.buf
            eight = jnp.broadcast_to(dgain[...], (8, dgain.shape[1]))
            buf[0] = jnp.concatenate([eight, gains_out[0:8, :]], 0).astype(BF16)
            buf[1] = gains_in[...]
        item.tick(stage)
        if stage == item.stages - 1:
            gains_out[...] = item.buf[...].reshape(gains_out.shape).astype(F32)

    def summed(n, stage):
        item = work[n]
        if n < early and stage == 0:
            pltpu.make_async_copy(ready[n], item.buf, loads.at[n]).wait()
        item.tick(stage)
        if stage < item.stages - 1:
            return
        if n < early:
            pltpu.make_async_copy(item.buf, sums[n], stores.at[n]).start()
            return
        per = wide // TILE
        for m, out in enumerate((dwq_out, dwk_out, dwv_out, dwsq_out)):
            block = item.buf[m * per : (m + 1) * per].reshape(wide, out.shape[0])
            out[:, two(n - early)] = jnp.transpose(block)

    last = pairs * count + count - 1
    events = []
    for n in range(early):
        events += [(1 + n // 2 + stage, summed, (n, stage)) for stage in range(work[n].stages)]
    for n in range(pairs):
        events += [
            ((n + 1) * count - 1 + stage, summed, (early + n, stage))
            for stage in range(work[early + n].stages)
        ]
    events += [(pairs * count + stage, slots, (stage,)) for stage in range(len(strides) + 1)]
    events += [(last + stage, gains, (stage,)) for stage in range(work[early + pairs].stages)]
    events.sort(key=lambda event: event[0])
    for when in range(last + 1):
        todo = [e for e in events if e[0] == when or (when == last and e[0] > last)]
        if not todo:
            continue

        @pl.when(step == when)
        def _():
            for _, act, args in todo:
                act(*args)

    @pl.when(step == last)
    def _():
        for n in range(early):
            pltpu.make_async_copy(work[n].buf, sums[n], stores.at[n]).wait()


def struct(shape, dtype):
    return jax.ShapeDtypeStruct(shape, dtype)


def full(shape):
    return pl.BlockSpec(shape, lambda i: (0,) * len(shape))


def rows_of(width, at=lambda i: i):
    return pl.BlockSpec((SEG, width), lambda i: (at(i), 0))


def lanes_of(height, at=lambda i: i):
    return pl.BlockSpec((height, SEG), lambda i: (0, at(i)))


def params(collective_id=None):
    grid = dict(dimension_semantics=("arbitrary",), vmem_limit_bytes=62 << 20)
    if collective_id is None:
        return pltpu.CompilerParams(**grid)
    return pltpu.CompilerParams(collective_id=collective_id, has_side_effects=True, **grid)


PLAIN = pltpu.CompilerParams(vmem_limit_bytes=60 << 20)


def body(
    tokens,
    memory,
    pad_mask,
    doc_lengths,
    first_gain,
    query_weight,
    key_weight,
    value_weight,
    out_weight,
    second_gain,
    up_weight,
    down_weight,
    memory_gain,
    slot_query_weight,
    gate_weight,
    gate_bias,
    write_weight,
    out_cotangent,
    memory_cotangent,
):
    rows, width = tokens.shape
    hidden = up_weight.shape[1]
    count = rows // SEG
    slots_here = memory.shape[1]
    group = lax.axis_size("slot")
    slots = slots_here * group
    place = lax.axis_index("slot")
    begin = (lax.axis_index("dp") * group + place) * rows
    places = begin + jnp.arange(rows, dtype=jnp.int32)
    ends = jnp.cumsum(doc_lengths)
    document = jnp.sum((places[:, None] >= ends[None, :]).astype(jnp.int32), 1)
    doc = document.astype(F32)[None, :]
    pad = pad_mask.astype(F32)[None, :]
    gain1, gain2, gain3 = (g[None, :] for g in (first_gain, second_gain, memory_gain))

    both = lax.all_gather(
        jnp.concatenate([memory[0], memory_cotangent[0]], 1), "slot", axis=0, tiled=True
    )
    mem, mem_cot = both[:, :width], both[:, width:]

    square = (width, width)
    normed, q_t, k, k_t, v, v_t = pl.pallas_call(
        project_kernel,
        grid=(count,),
        in_specs=[rows_of(width), full((1, width)), full(square), full(square), full(square)],
        out_specs=[
            rows_of(width), lanes_of(width), rows_of(width), lanes_of(width), rows_of(width),
            lanes_of(width),
        ],
        out_shape=[
            struct((rows, width), BF16),
            struct((width, rows), BF16), struct((rows, width), BF16), struct((width, rows), BF16),
            struct((rows, width), BF16), struct((width, rows), BF16),
        ],
        compiler_params=params(),
        name="project",
    )(tokens, gain1, query_weight, key_weight, value_weight)

    tall, wide = (slots, width), (width, slots)
    slot_k, slot_k_t, slot_v, slot_v_t, slot_q, slot_q_t, stats = pl.pallas_call(
        writer_kernel,
        out_shape=[
            struct(tall, BF16), struct(wide, BF16), struct(tall, BF16), struct(wide, BF16),
            struct(tall, BF16), struct(wide, BF16), struct((3,) + tall, F32),
        ],
        compiler_params=PLAIN,
        name="writer",
    )(mem, gain3, key_weight, value_weight, slot_query_weight, k_t, v, pad)
    all_stats = lax.all_gather(stats, "slot", axis=0)

    axes = {"dp": lax.axis_size("dp"), "slot": group}
    orders = bit_orders(axes)
    chunks = hidden // SEG
    pairs = H // 2
    anywhere = pl.BlockSpec(memory_space=pl.ANY)
    begin_at = lambda i: jnp.minimum(i, count - 1)
    chunk_at = lambda i: jnp.clip(i // count - 1, 0, chunks - 1)
    end_at = lambda i: jnp.maximum(i - count - chunks * count, 0)
    blocks = 2 * SEG // TILE
    layer_out, res_grad, d_t, lse, inner, dwo, late, dgain2, *early = pl.pallas_call(
        lambda *refs: middle_kernel(count, chunks, orders, *refs),
        grid=(2 * count + chunks * count,),
        in_specs=[
            rows_of(width, begin_at), lanes_of(width, begin_at), rows_of(width, begin_at),
            lanes_of(width, begin_at), lanes_of(1, begin_at), lanes_of(1, begin_at),
            full(tall), full(wide), full(square), full((1, width)),
            pl.BlockSpec((width, SEG), lambda i: (0, chunk_at(i))),
            pl.BlockSpec((SEG, width), lambda i: (chunk_at(i), 0)),
            full((count, SEG, width)),
        ],
        out_specs=[
            rows_of(width, end_at), rows_of(width, end_at), lanes_of(width, end_at),
            pl.BlockSpec((pairs, 2, SEG), lambda i: (0, 0, begin_at(i))),
            pl.BlockSpec((pairs, 2, SEG), lambda i: (0, 0, end_at(i))),
            full(square), full((chunks - EARLY, blocks, TILE, width)), full((16, width)),
        ]
        + [anywhere] * EARLY,
        out_shape=[
            struct((rows, width), BF16), struct((rows, width), F32), struct((width, rows), BF16),
            struct((pairs, 2, rows), F32), struct((pairs, 2, rows), F32), struct(square, BF16),
            struct((chunks - EARLY, blocks, TILE, width), BF16), struct((16, width), BF16),
        ]
        + [struct((blocks, TILE, width), BF16)] * EARLY,
        scratch_shapes=[
            pltpu.VMEM((SEG, SEG), F32), pltpu.VMEM((count, width, SEG), BF16),
            pltpu.VMEM((count, SEG, width), F32), pltpu.VMEM((count, SEG, width), BF16),
            pltpu.VMEM((count, width, SEG), BF16), pltpu.VMEM((count, width, SEG), BF16),
            pltpu.VMEM((count, SEG, width), F32), pltpu.VMEM((count, SEG, width), F32),
            pltpu.VMEM(square, F32), pltpu.VMEM((width, SEG), F32), pltpu.VMEM((width, SEG), F32),
            pltpu.VMEM((1, width), F32),
        ]
        + reduction_scratch([blocks] * EARLY, orders, width)
        + [pltpu.SemaphoreType.DMA((EARLY,))],
        compiler_params=params(0),
        name="middle",
    )(
        tokens, q_t, k, v_t, doc, pad, slot_k, slot_v_t, out_weight, gain2, up_weight, down_weight,
        out_cotangent.reshape(count, SEG, width),
    )

    vm = pl.BlockSpec(memory_space=pltpu.VMEM)
    (
        new_memory, g, g_t, wlse, winner, self_q_t, self_k_t, self_v_t, direct, dwgate, dwwrite, dbias,
    ) = pl.pallas_call(
        update_kernel,
        in_specs=[pl.BlockSpec(memory_space=pltpu.SMEM)] + [vm] * 9,
        out_specs=[vm] * 12,
        out_shape=[
            struct((slots_here, width), F32), struct(tall, BF16), struct(wide, BF16), struct(tall, F32),
            struct(tall, F32), struct(wide, F32), struct(wide, F32), struct(wide, F32), struct(tall, F32),
            struct(square, BF16), struct(square, BF16), struct((16, width), BF16),
        ],
        scratch_shapes=[pltpu.VMEM(tall, F32)],
        compiler_params=PLAIN,
        name="update",
    )(
        place.astype(jnp.int32).reshape(1, 1), all_stats, mem, mem_cot, slot_q, slot_k, slot_v,
        gate_weight, gate_bias[None, :], write_weight,
    )

    ready = [late[n] for n in range(chunks - EARLY)] + [
        jnp.concatenate([tiles(dwo), tiles(dwgate), tiles(dwwrite)], 0)
    ]
    sizes = [r.shape[0] for r in ready]
    wide_pair = 2 * DH
    pair_at = lambda s: jnp.minimum(s // count, pairs - 1)
    seg_at = lambda s: s % count
    final_at = lambda s: jnp.maximum(s - pairs * count, 0)
    pair_rows = pl.BlockSpec((SEG, wide_pair), lambda s: (seg_at(s), pair_at(s)))
    pair_lanes = pl.BlockSpec((wide_pair, SEG), lambda s: (pair_at(s), seg_at(s)))
    pair_stat = pl.BlockSpec((1, 2, SEG), lambda s: (pair_at(s), 0, seg_at(s)))
    pair_tall = pl.BlockSpec((slots, wide_pair), lambda s: (0, pair_at(s)))
    pair_wide = pl.BlockSpec((wide_pair, slots), lambda s: (pair_at(s), 0))
    input_grad, dwq, dwk, dwv, dwsq, gains, memory_grad, *sums = pl.pallas_call(
        lambda *refs: last_kernel(count, orders, sizes, *refs),
        grid=(pairs * count + count,),
        in_specs=[
            rows_of(width, final_at), full((1, width)), rows_of(width, seg_at),
            pair_lanes, pair_rows, pair_lanes, pair_rows, pair_lanes, pair_lanes, pair_stat, pair_stat,
            lanes_of(1, seg_at), lanes_of(1, seg_at), rows_of(width, final_at),
            pair_tall, pair_wide, pair_tall, pair_tall, pair_wide, pair_tall, pair_wide,
            pair_tall, pair_tall, pair_wide, pair_wide, pair_wide, full(tall), full(tall),
            full((1, width)), full(square), full(square), full(square), full(square),
            full((16, width)),
        ]
        + [anywhere] * len(ready),
        out_specs=[
            rows_of(width, final_at), full(square), full(square), full(square), full(square),
            full((32, width)), full((slots_here, width)),
        ]
        + [anywhere] * len(ready),
        out_shape=[
            struct((rows, width), F32), struct(square, BF16), struct(square, BF16), struct(square, BF16),
            struct(square, BF16), struct((32, width), F32), struct((slots_here, width), F32),
        ]
        + [struct(r.shape, BF16) for r in ready],
        scratch_shapes=[
            pltpu.VMEM((SEG, SEG), F32), pltpu.VMEM((count, pairs, 3 * wide_pair, SEG), BF16),
            pltpu.VMEM((3 * wide_pair, width), F32), pltpu.VMEM((width, 3 * width), BF16),
            pltpu.VMEM((wide_pair, slots), F32), pltpu.VMEM((wide_pair, slots), F32),
            pltpu.VMEM((wide_pair, slots), F32), pltpu.VMEM((pairs, wide_pair, slots), BF16),
            pltpu.VMEM((pairs, wide_pair, slots), BF16), pltpu.VMEM((pairs, wide_pair, slots), BF16),
            pltpu.VMEM(tall, BF16), pltpu.VMEM((1, width), F32),
            pltpu.VMEM((group, slots_here, width), F32), pltpu.VMEM((group, slots_here, width), F32),
            pltpu.SemaphoreType.DMA((2, group)), pltpu.SemaphoreType.DMA((len(ready),)),
            pltpu.SemaphoreType.DMA((len(ready),)),
        ]
        + reduction_scratch(sizes + [4 * wide_pair // TILE] * pairs + [2], orders, width),
        compiler_params=params(1),
        name="last",
    )(
        tokens, gain1, normed, q_t, k, k_t, v, v_t, d_t, lse, inner, doc, pad, res_grad,
        slot_k, slot_k_t, slot_v, slot_q, slot_q_t, g, g_t, wlse, winner,
        self_q_t, self_k_t, self_v_t, direct, mem, gain3,
        query_weight, key_weight, value_weight, slot_query_weight,
        jnp.concatenate([dgain2[:8], dbias[:8]], 0), *ready,
    )
    half = SEG // TILE
    ffn = list(early) + list(sums[: chunks - EARLY])
    dwup = jnp.concatenate([f[:half].reshape(width, SEG) for f in ffn], 1)
    dwdown = jnp.concatenate([f[half:].reshape(SEG, width) for f in ffn], 0)
    dwo, dwgate, dwwrite = (
        sums[-1][n * width // TILE : (n + 1) * width // TILE].reshape(width, width) for n in range(3)
    )

    return (
        layer_out,
        new_memory[None],
        input_grad,
        memory_grad[None],
        gains[0],
        dwq.astype(F32),
        dwk.astype(F32),
        dwv.astype(F32),
        dwo.astype(F32),
        gains[16],
        dwup.astype(F32),
        dwdown.astype(F32),
        gains[8],
        dwsq.astype(F32),
        dwgate.astype(F32),
        gains[24],
        dwwrite.astype(F32),
    )


def solution(mesh):
    token = P(("dp", "slot"), None)
    slot = P("dp", "slot", None)
    in_specs = (
        (token, slot, P(("dp", "slot"))) + (P(),) * 14 + (token, slot)
    )
    out_specs = (token, slot, token, slot) + (P(),) * 13
    return jax.shard_map(body, mesh=mesh, in_specs=in_specs, out_specs=out_specs, check_vma=False)
```

time: 367 us -> 301 us (0.82)
  waiting for transfers between devices: 141 us -> 0.02 us
  Pallas kernels: 141 us -> 244 us
  blocking collectives: 49.8 us -> 6.49 us
  local copies, waits for them, and re-layouts: 1.35 us -> 14.5 us
    psum x1 -> x0, waiting for transfers between devices: 133 us -> none  [body(): lax.psum((dwq, dwk, dwv, dwsq, dgains.astype(BF16)), axes)]
    pallas_call x2, Pallas kernels: 120 us -> 222 us  [the longest x1 116 us: body(): pl.pallas_call(lambda *refs: last_kernel(count, orders, sizes, *refs), gr...]
    psum x1 -> x0, blocking collectives: 43.4 us -> none  [body(): lax.psum((dwq, dwk, dwv, dwsq, dgains.astype(BF16)), axes)]
    reduce_scatter x1 -> x0, waiting for transfers between devices: 7.65 us -> none  [body(): lax.psum_scatter(slot_part, 'slot', scatter_dimension=0, tiled=True)[None]]
    unnamed x22 -> x29, local copies, waits for them, and re-layouts: 0.7 us -> 6.51 us
    slice x0 -> x6, local copies, waits for them, and re-layouts: none -> 4.17 us  [the longest x1 1.42 us: body(): gains[24]]
  transfers between devices with their start and end apart: 3 -> 1, of which waited for: 2 -> 0; matrix products, arithmetic and copies ran while one was open for 5% -> 2% of each run, Pallas kernels for 21% -> 35%
where the time goes in v2:
time: 301 us; the launch traced here: 300 us
  Pallas kernels  244 us (81%)
  other arithmetic  21.3 us (7%)
  local copies, waits for them, and re-layouts  14.5 us (5%)
  between operations  14.1 us (5%)
  blocking collectives  6.49 us (2%)
    pallas_call x1, Pallas kernels, body(): pl.pallas_call(lambda *refs: last_kernel(count, orders, sizes, *refs), gr...  116 us
    pallas_call x1, Pallas kernels, body(): pl.pallas_call(lambda *refs: middle_kernel(count, chunks, orders, *refs),...  106 us
    pallas_call x1, Pallas kernels, body(): pl.pallas_call(project_kernel, grid=(count,), in_specs=[rows_of(width), f...  8.27 us
    pallas_call x1, Pallas kernels, body(): pl.pallas_call(writer_kernel, out_shape=[struct(tall, BF16), struct(wide,...  7.14 us
    unnamed x29, local copies, waits for them, and re-layouts  6.51 us
    all_gather x1, blocking collectives, body(): lax.all_gather(jnp.concatenate([memory[0], memory_cotangent[0]], 1), 'slo...  6.49 us
  transfers between devices with their start and end apart: 1, of which 0 were waited for; matrix products, arithmetic and copies ran while one was open for 2% of the time, Pallas kernels for 35%

profile of v2, /device:TPU:0, one launch (start us, length us, event | category | flops | bytes accessed | tf_op | source)
XLA Modules:
  0.0 300.1 jit_solution(17598663530167442018)
XLA Ops:
  7.2 0.0 all-gather.3.cloned.1.call-start
  7.2 1.3 convert_element_type.58
  8.5 0.7 pad_maximum_fusion.1
  9.3 6.5 %all_gather.9 = bf16[64,1024]{1,0:T(8,128)(2,1)S(1)} all-gather(bf16[16,1024]{1,0:T(8,128)(2,1)S(1)} %pad_maximum_fusion.1), channel_id=1, replica_groups=mesh['dp'=8,'slot'=4] {'slot'}, dimensions={0}, use_global_device_ids=true | all-gather | bytes 163840 | tf_op jit(solution)/shard_map/all_gather | solution.py:736
  15.8 0.7 fusion.5
  16.4 8.3 %project.1 = (bf16[2048,512]{1,0:T(8,128)(2,1)}, bf16[512,2048]{1,0:T(8,128)(2,1)}, bf16[2048,512]{1,0:T(8,128)(2,1)}, bf16[512,2048]{1,0:T(8,128)(2,1)}, bf16[2...) custom-call(bf16[2048,512]{1,0:T(8,128)(2,1)} %refs_0_.3, f32[1,512]{1,0:T(1,128)} %bitcast.64, bf16[512,512]{1,0:T(8,128)(2,1)} %refs_29_.1, ...), custom_call_target="tpu_custom_call" | custom-call | tf_op jit(solution)/shard_map/project/pallas_call | solution.py:742
  24.7 7.1 %writer.1 = (bf16[64,512]{1,0:T(8,128)(2,1)}, bf16[512,64]{1,0:T(8,128)(2,1)}, bf16[64,512]{1,0:T(8,128)(2,1)}, bf16[512,64]{1,0:T(8,128)(2,1)}, bf16[64,512]{1,...) custom-call(bf16[64,512]{1,0:T(8,128)(2,1)} %get-tuple-element.121.mem.refs_27_, f32[1,512]{1,0:T(1,128)} %bitcast.66, ...), custom_call_target="tpu_custom_call" | custom-call | tf_op jit(solution)/shard_map/writer/pallas_call | solution.py:760
  31.8 0.0 all-gather.3.cloned.1.call-update
  31.9 0.0 copy-done.12
  31.9 0.2 reduce-window.8
  32.1 0.1 convert_reduce_fusion
  32.2 0.6 convert_element_type.56
  32.8 106.4 %middle.1 = (bf16[2048,512]{1,0:T(8,128)(2,1)}, f32[2048,512]{1,0:T(8,128)}, bf16[512,2048]{1,0:T(8,128)(2,1)}, f32[4,2,2048]{2,1,0:T(2,128)}, f32[4,2,2048]{2,1...) custom-call(bf16[2048,512]{1,0:T(8,128)(2,1)} %refs_0_.3, ...), custom_call_target="tpu_custom_call" | custom-call | tf_op jit(solution)/shard_map/middle/pallas_call | solution.py:780
  139.2 0.7 slice.65
  139.9 3.2 %slice_bitcast_fusion = (bf16[64,16,512]{2,1,0:T(8,128)(2,1)}, bf16[64,16,512]{2,1,0:T(8,128)(2,1)}) fusion(bf16[2,64,16,512]{3,2,1,0:T(8,128)(2,1)} %get-tuple-element.91), kind=kLoop, calls=%fused_computation.3 | loop fusion | bytes 4194304 | tf_op jit(solution)/shard_map/squeeze | solution.py:841
  143.0 0.0 copy-done.6
  143.0 0.0 copy-done.7
  143.0 1.0 fusion.1
  144.0 5.8 %update.1 = (f32[16,512]{1,0:T(8,128)}, bf16[64,512]{1,0:T(8,128)(2,1)}, bf16[512,64]{1,0:T(8,128)(2,1)}, f32[64,512]{1,0:T(8,128)}, f32[64,512]{1,0:T(8,128)}, ...) custom-call(s32[1,1]{1,0:T(1,128)} %bitcast.10.place, ...), custom_call_target="tpu_custom_call" | custom-call | tf_op jit(solution)/shard_map/update/pallas_call | solution.py:824
  149.8 0.7 slice.66
  150.5 0.6 pad_maximum_fusion.2.refs_33_
  151.1 0.0 copy-done.10
  151.1 2.5 pad_maximum_fusion.refs_36_
  153.7 116.1 %last.1 = (f32[2048,512]{1,0:T(8,128)}, bf16[512,512]{1,0:T(8,128)(2,1)}, bf16[512,512]{1,0:T(8,128)(2,1)}, bf16[512,512]{1,0:T(8,128)(2,1)}, bf16[512,512]{1,0:...) custom-call(bf16[2048,512]{1,0:T(8,128)(2,1)} %refs_0_.3, ...), custom_call_target="tpu_custom_call" | custom-call | tf_op jit(solution)/shard_map/last/pallas_call | solution.py:854
  269.8 0.0 copy-start.9
  269.8 1.4 fusion.6
  271.2 2.2 convert_element_type.59
  273.4 2.2 convert_element_type.60
  275.6 0.0 copy-done.9
  275.6 1.1 convert_element_type.61
  276.7 0.0 copy-done.8
  276.7 1.1 convert_element_type.66
  277.8 0.0 copy-done.5
  277.8 0.1 fusion.4
  277.9 0.6 copy-done.3
  278.5 0.3 copy-done.4
  278.8 0.3 fusion
  279.1 0.0 copy-start.2
  279.1 1.1 bitcast_convert_fusion
  280.3 1.1 bitcast_convert_fusion.1
  281.4 1.1 bitcast_convert_fusion.2
  282.5 0.0 copy-done.2
  282.5 2.6 maximum_convert_fusion
  285.1 2.6 maximum_convert_fusion.1
  287.7 1.3 copy.39
  289.0 1.6 copy-done
  290.7 2.0 copy.40
  292.7 0.6 copy.41
  (15 shorter events, 0.0 us)
Async XLA Ops:
  7.2 136.9 %all-gather.3.cloned.1.call-start = ((), (), s32[]{:S(2)}) async-start(), calls=%async_computation | async-start | bytes 1966080 | tf_op jit(solution)/shard_map/all_gather | solution.py:769
  24.7 7.2 %copy-start.12 = (s32[12]{0:T(128)S(1)}, s32[12]{0:T(128)}, u32[]{:S(2)}) copy-start(s32[12]{0:T(128)} %param.22) | copy-start | bytes 148
  139.9 3.2 %copy-start.6 = (bf16[64,16,512]{2,1,0:T(8,128)(2,1)S(1)}, bf16[64,16,512]{2,1,0:T(8,128)(2,1)}, u32[]{:S(2)}) copy-start(bf16[64,16,512]{2,1,0:T(8,128)(2,1)} %get-tuple-element.102) | copy-start | bytes 3145732
  139.9 3.2 %copy-start.7 = (bf16[64,16,512]{2,1,0:T(8,128)(2,1)S(1)}, bf16[64,16,512]{2,1,0:T(8,128)(2,1)}, u32[]{:S(2)}) copy-start(bf16[64,16,512]{2,1,0:T(8,128)(2,1)} %get-tuple-element.103) | copy-start | bytes 3145732
  144.0 7.1 %copy-start.10 = (bf16[512,512]{1,0:T(8,128)(2,1)S(1)}, bf16[512,512]{1,0:T(8,128)(2,1)}, u32[]{:S(2)}) copy-start(bf16[512,512]{1,0:T(8,128)(2,1)} %get-tuple-element.92) | copy-start | bytes 1572868
  269.8 5.9 %copy-start.9 = (bf16[512,512]{1,0:T(8,128)(2,1)S(1)}, bf16[512,512]{1,0:T(8,128)(2,1)}, u32[]{:S(2)}) copy-start(bf16[512,512]{1,0:T(8,128)(2,1)} %get-tuple-element.100) | copy-start | bytes 1572868
  271.2 5.5 %copy-start.8 = (bf16[512,512]{1,0:T(8,128)(2,1)S(1)}, bf16[512,512]{1,0:T(8,128)(2,1)}, u32[]{:S(2)}) copy-start(bf16[512,512]{1,0:T(8,128)(2,1)} %get-tuple-element.106) | copy-start | bytes 1572868
  273.4 4.4 %copy-start.5 = (bf16[64,16,512]{2,1,0:T(8,128)(2,1)S(1)}, bf16[64,16,512]{2,1,0:T(8,128)(2,1)}, u32[]{:S(2)}) copy-start(bf16[64,16,512]{2,1,0:T(8,128)(2,1)} %get-tuple-element.105) | copy-start | bytes 3145732
  276.7 1.8 copy-start.3
  276.7 2.1 copy-start.4
  279.1 3.4 %copy-start.2 = (bf16[32,16,512]{2,1,0:T(8,128)(2,1)S(1)}, bf16[32,16,512]{2,1,0:T(8,128)(2,1)}, u32[]{:S(2)}) copy-start(bf16[32,16,512]{2,1,0:T(8,128)(2,1)} %get-tuple-element.126) | copy-start | bytes 1572868
  285.1 2.6 copy-start.1
  287.7 2.9 copy-start
  290.7 2.0 copy-start.11
Sparse Core Ops, SparseCore 0:
  32.0 21.2 all-gather.2

commit v3 on v2

v3 whole, which is shorter than its diff:
```python
import jax
import jax.numpy as jnp
from jax import lax
from jax.experimental import pallas as pl
from jax.experimental.pallas import tpu as pltpu
from jax.sharding import PartitionSpec as P

H = 8
DH = 64
SEG = 512
HALF = 256
FILL = -1e30
EPS = 1e-05
SCALE = DH ** (-0.5)
F32 = jnp.float32
BF16 = jnp.bfloat16

TAIL = (
    0.11962928145668905,
    0.12075423000729175,
    0.09991172819365436,
    0.12856765411993218,
    -0.053695489964182386,
    0.20636694099934239,
    -0.15721125090545032,
    0.035676834162404004,
)


def nn(a, b, precision=None):
    return lax.dot_general(
        a, b, (((1,), (0,)), ((), ())), preferred_element_type=F32, precision=precision
    )


def nt(a, b):
    return lax.dot_general(a, b, (((1,), (1,)), ((), ())), preferred_element_type=F32)


def norm(value):
    center = value - jnp.mean(value, -1, keepdims=True)
    inverse = lax.rsqrt(jnp.mean(center * center, -1, keepdims=True) + EPS)
    return center * inverse, inverse


def norm_back(grad, unit, inverse, gain):
    inner = grad * gain
    value_grad = inverse * (
        inner
        - jnp.mean(inner, -1, keepdims=True)
        - unit * jnp.mean(inner * unit, -1, keepdims=True)
    )
    return value_grad, jnp.sum(grad * unit, 0, keepdims=True)


def gelu_pair(x):
    t = 1.0 / (1.0 + 0.3 * jnp.abs(x))
    poly = TAIL[7]
    for c in TAIL[6::-1]:
        poly = poly * t + c
    bell = jnp.exp(-0.5 * (x * x))
    tail = bell * (poly * t)
    cdf = jnp.where(x >= 0, 1.0 - tail, tail)
    return x * cdf, cdf + x * (bell * 0.3989422804014327)


def segment_bias(doc_row, pad_row):
    code = jnp.where(pad_row > 0, doc_row, -1.0)
    key_code = jnp.transpose(jnp.broadcast_to(code, (SEG, SEG)))
    rows = lax.broadcasted_iota(jnp.int32, (SEG, SEG), 0)
    columns = lax.broadcasted_iota(jnp.int32, (SEG, SEG), 1)
    seen = (rows <= columns) & (key_code == doc_row)
    return jnp.where(seen, 0.0, FILL)


def head_rows(pair, odd):
    zero = jnp.zeros((DH, pair.shape[1]), pair.dtype)
    if odd:
        return jnp.concatenate([zero, pair[DH:]], 0)
    return jnp.concatenate([pair[:DH], zero], 0)


def head_lanes(pair, odd):
    lane = lax.broadcasted_iota(jnp.int32, pair.shape, 1)
    keep = (lane >= DH) if odd else (lane < DH)
    return jnp.where(keep, pair, jnp.zeros_like(pair))


def two(p):
    return slice(p * 2 * DH, (p + 1) * 2 * DH)


def one(h):
    return slice(h * DH, (h + 1) * DH)


BLOCKS = ((0, HALF), (HALF, SEG))


TILE = 16
MESH = pl.DeviceIdType.MESH


def bit_orders(sizes):
    dp = [("dp", 1 << n) for n in range(sizes["dp"].bit_length() - 1)]
    slot = [("slot", 1 << n) for n in range(sizes["slot"].bit_length() - 1)]
    first, other = slot[:1], slot[1:]
    return first + other + dp, first + dp[:1] + other + dp[1:]


def plan(blocks, orders):
    half = blocks // 2
    steps, recv = [], 0
    for n, order in enumerate(orders):
        size, row = half, []
        for axis, stride in order:
            halves = size % 2 == 0
            sent = size // 2 if halves else size
            row.append((axis, stride, halves, sent, recv))
            recv += sent
            size = sent
        steps.append((n * half, row))
    return steps, recv


def here():
    return {"dp": lax.axis_index("dp"), "slot": lax.axis_index("slot")}


def across(index, axis, stride):
    bit = (index[axis] // stride) % 2
    peer = dict(index)
    peer[axis] = index[axis] + stride - 2 * bit * stride
    return bit, (peer["dp"], peer["slot"])


def ring(index, offset, group):
    return (index["dp"], (index["slot"] + offset) % group)


def greet(orders, index, group):
    barrier = pltpu.get_barrier_semaphore()
    peers = [ring(index, n, group) for n in range(1, group)] + [
        across(index, axis, stride)[1] for axis, stride in orders[0] if axis == "dp"
    ]
    for peer in peers:
        pl.semaphore_signal(barrier, inc=1, device_id=peer, device_id_type=MESH)
    pl.semaphore_wait(barrier, len(peers))


def gather(ref, sems, index, group):
    own = ref.at[index["slot"]]
    return [
        pltpu.make_async_remote_copy(
            own, own, sems.at[0, n], sems.at[1, n],
            device_id=ring(index, n, group), device_id_type=MESH,
        )
        for n in range(1, group)
    ]


def run_events(step, last, events):
    events = sorted(events, key=lambda event: event[0])
    for when in range(last + 1):
        todo = [e for e in events if e[0] == when or (when == last and e[0] > last)]
        if not todo:
            continue

        @pl.when(step == when)
        def _():
            for _, act, args in todo:
                act(*args)


class Reduction:
    def __init__(self, buf, recv, sems, free, base, orders, index):
        self.buf, self.recv, self.sems, self.free = buf, recv, sems, free
        self.base, self.index = base, index
        self.steps, _ = plan(buf.shape[0], orders)
        self.depth = len(orders[0])
        up = [
            (level, False)
            for level in reversed(range(self.depth))
            if any(row[level][2] for _, row in self.steps)
        ]
        self.moves = [(level, True) for level in range(self.depth)] + up
        self.stages = len(self.moves) + 1

    def copies(self, move):
        level, down = self.moves[move]
        found = []
        for n, (start, row) in enumerate(self.steps):
            for axis, stride, halves, sent, _ in row[: level if down else level + 1]:
                if halves:
                    start = start + across(self.index, axis, stride)[0] * sent
            axis, stride, halves, sent, at = row[level]
            bit, peer = across(self.index, axis, stride)
            slot = self.base + n * self.depth + level
            if down:
                keep = start + bit * sent if halves else start
                give = start + sent - bit * sent if halves else start
                target, ends = self.recv.at[pl.ds(at, sent)], 0
            elif halves:
                keep, give = None, start
                target, ends = self.buf.at[pl.ds(give, sent)], 2
            else:
                continue
            copy = pltpu.make_async_remote_copy(
                self.buf.at[pl.ds(give, sent)], target,
                self.sems.at[ends, slot], self.sems.at[ends + 1, slot],
                device_id=peer, device_id_type=MESH,
            )
            found.append((copy, halves, keep, sent, at, slot, peer))
        return found

    def tick(self, stage):
        if stage > 0:
            down = self.moves[stage - 1][1]
            for copy, halves, keep, sent, at, slot, peer in self.copies(stage - 1):
                copy.wait()
                if not down:
                    continue
                if halves:
                    pl.semaphore_signal(
                        self.free.at[slot], inc=1, device_id=peer, device_id_type=MESH
                    )
                mine = self.buf[pl.ds(keep, sent)].astype(F32)
                self.buf[pl.ds(keep, sent)] = (
                    mine + self.recv[pl.ds(at, sent)].astype(F32)
                ).astype(BF16)
        if stage < len(self.moves):
            down = self.moves[stage][1]
            for copy, halves, keep, sent, at, slot, peer in self.copies(stage):
                if not down:
                    pl.semaphore_wait(self.free.at[slot], 1)
                copy.start()


def reduction_scratch(sizes, orders, width):
    depth = len(orders[0])
    return (
        [pltpu.VMEM((s, TILE, width), BF16) for s in sizes]
        + [pltpu.VMEM((plan(s, orders)[1], TILE, width), BF16) for s in sizes]
        + [
            pltpu.SemaphoreType.DMA((4, len(sizes) * 2 * depth)),
            pltpu.SemaphoreType.REGULAR((len(sizes) * 2 * depth,)),
        ]
    )


def reductions(refs, count, orders, index):
    bufs, recvs, (sems, free) = refs[:count], refs[count : 2 * count], refs[2 * count :]
    return [
        Reduction(bufs[n], recvs[n], sems, free, n * 2 * len(orders[0]), orders, index)
        for n in range(count)
    ]


def tiles(value):
    return value.reshape(value.shape[0] // TILE, TILE, value.shape[1])


EARLY = 2


def front_kernel(
    count, chunks, group, orders,
    x_in, mem_in, wq_in, wk_in, wv_in, wsq_in, wo_in, wup_in, wdown_in, cot_in,
    doc, pad, gain1, gain2, gain3,
    out, res_out, low_out, q_out, k_out, kt_out, v_out, vt_out, d_out, late, *rest,
):
    sums, rest = rest[:EARLY], rest[EARLY:]
    (lse, inner, slot_k, slot_kt, slot_v, slot_q, slot_qt, mem, stats, dwo_out, dgain) = rest[:11]
    (
        x, cot, low, q_t, k, k_t, v, v_t, o_t, second, second_t, cot_t, ffn, grad,
        wq, wk, wv, wsq, wo, wup, wdown, slot_vt, bias, dwo, dwup, dwdown_t, out_low, late_buf,
        loads, stores, gathers, late_sems,
    ) = rest[11:43]
    index = here()
    work = reductions(rest[43:], EARLY, orders, index)
    pairs = H // 2

    def load(n):
        pairs_of = (
            [(x_in.at[i], x.at[i]) for i in range(count)]
            + [(wq_in, wq), (wk_in, wk), (wv_in, wv), (wsq_in, wsq), (wo_in, wo)]
            + [(cot_in.at[i], cot.at[i]) for i in range(count)]
            + [
                (wup_in.at[:, c * SEG : (c + 1) * SEG], wup.at[c]) for c in range(chunks)
            ]
            + [(wdown_in.at[c], wdown.at[c]) for c in range(chunks)]
            + [(mem_in, mem.at[index["slot"]])]
        )
        return pltpu.make_async_copy(*pairs_of[n], loads.at[n])

    weights_at = count
    cot_at = count + 5
    up_at = 2 * count + 5
    down_at = up_at + chunks
    mem_at = down_at + chunks
    order = (
        [mem_at, 0, weights_at, weights_at + 1, weights_at + 2]
        + list(range(1, count))
        + [weights_at + 3, weights_at + 4]
        + list(range(cot_at, mem_at))
    )
    for n in order:
        load(n).start()
    greet(orders, index, group)
    load(mem_at).wait()
    for copy in gather(mem, gathers.at[0], index, group):
        copy.start()
    dwo[...] = jnp.zeros_like(dwo)
    dwup[...] = jnp.zeros_like(dwup)
    dwdown_t[...] = jnp.zeros_like(dwdown_t)
    dgain[...] = jnp.zeros_like(dgain)
    for n in range(weights_at, weights_at + 3):
        load(n).wait()

    kept = ((low, low_out), (q_t, q_out), (k, k_out), (k_t, kt_out), (v, v_out), (v_t, vt_out))

    def keep(n, i):
        source, target = kept[n]
        return pltpu.make_async_copy(source.at[i], target.at[i], stores.at[n, i])

    @pl.loop(0, count)
    def _(i):
        pltpu.make_async_copy(x_in.at[i], x.at[i], loads.at[i]).wait()
        unit, _ = norm(x[i].astype(F32))
        row = (unit * gain1[...]).astype(BF16)
        low[i] = row
        q_t[i] = jnp.transpose((nn(row, wq[...]) * SCALE).astype(BF16)).reshape(q_t.shape[1:])
        key = nn(row, wk[...]).astype(BF16)
        k_t[i] = jnp.transpose(key).reshape(k_t.shape[1:])
        value = nn(row, wv[...]).astype(BF16)
        v_t[i] = jnp.transpose(value).reshape(v_t.shape[1:])
        for p in range(pairs):
            k[i, p] = key[:, two(p)]
            v[i, p] = value[:, two(p)]
        for n in range(len(kept)):
            keep(n, i).start()

    for copy in gather(mem, gathers.at[0], index, group):
        copy.wait()
    load(weights_at + 3).wait()
    load(weights_at + 4).wait()
    slots = group * mem.shape[2]
    unit, _ = norm(mem[:, 0].reshape(slots, mem.shape[3]).astype(F32))
    row = (unit * gain3[...]).astype(BF16)
    sk = nn(row, wk[...]).astype(BF16)
    sv = nn(row, wv[...]).astype(BF16)
    sq = (nn(row, wsq[...]) * SCALE).astype(BF16)
    lane = lax.broadcasted_iota(jnp.int32, (slots, 2 * DH), 1) < DH
    for p in range(pairs):
        slot_k[p], slot_v[p], slot_q[p] = sk[:, two(p)], sv[:, two(p)], sq[:, two(p)]
        slot_kt[p] = jnp.transpose(sk[:, two(p)])
        slot_vt[p] = jnp.transpose(sv[:, two(p)])
        slot_qt[p] = jnp.transpose(sq[:, two(p)])
        parts = []
        for odd in range(2):
            mine = head_lanes(sq[:, two(p)], odd)
            cs = [
                nn(mine, k_t[i, p]) + jnp.where(pad[:, i * SEG : (i + 1) * SEG] > 0, 0.0, FILL)
                for i in range(count)
            ]
            top = jnp.max(cs[0], 1, keepdims=True)
            for c in cs[1:]:
                top = jnp.maximum(top, jnp.max(c, 1, keepdims=True))
            total, acc = 0.0, 0.0
            for i, c in enumerate(cs):
                w = jnp.exp(c - top)
                total = total + jnp.sum(w, 1, keepdims=True)
                acc = acc + nn(w.astype(BF16), v[i, p])
            parts.append((acc, top, total))
        for n in range(3):
            stats[index["slot"], n, :, two(p)] = jnp.where(lane, parts[0][n], parts[1][n])
    for copy in gather(stats, gathers.at[1], index, group):
        copy.start()

    @pl.loop(0, count)
    def _(i):
        cols = pl.ds(pl.multiple_of(i * SEG, SEG), SEG)
        bias[...] = segment_bias(doc[:, cols], pad[:, cols])
        for h in range(H):
            p, odd = h // 2, h % 2
            own = one(odd)
            qm = head_rows(q_t[i, p], odd)
            for lo, hi in BLOCKS:
                qb = qm[:, lo:hi]
                s = nn(k[i, p, :hi, :], qb) + bias[:hi, lo:hi]
                sm = nn(slot_k[p], qb)
                top = jnp.maximum(jnp.max(s, 0, keepdims=True), jnp.max(sm, 0, keepdims=True))
                e = jnp.exp(s - top)
                em = jnp.exp(sm - top)
                total = jnp.sum(e, 0, keepdims=True) + jnp.sum(em, 0, keepdims=True)
                o = nn(v_t[i, p, own, :hi], e.astype(BF16)) + nn(slot_vt[p, own, :], em.astype(BF16))
                o_t[i, one(h), lo:hi] = (o / total).astype(BF16)
                lse[i, p, odd : odd + 1, lo:hi] = top + jnp.log(total)
        res = x[i].astype(F32) + nn(jnp.transpose(o_t[i]), wo[...])
        ffn[i] = res
        grad[i] = jnp.zeros_like(res)
        unit, _ = norm(res)
        row = (unit * gain2[...]).astype(BF16)
        second[i] = row
        second_t[i] = jnp.transpose(row)
        pltpu.make_async_copy(cot_in.at[i], cot.at[i], loads.at[cot_at + i]).wait()
        cot_t[i] = jnp.transpose(cot[i])

    last = chunks * count + count - 1

    def summed(n, stage):
        work[n].tick(stage)
        if stage == work[n].stages - 1:
            pltpu.make_async_copy(work[n].buf, sums[n], late_sems.at[n]).start()

    events = [
        ((n + 1) * count - 1 + stage, summed, (n, stage))
        for n in range(EARLY)
        for stage in range(work[n].stages)
    ]

    @pl.loop(0, chunks * count)
    def _(step):
        c = step // count
        i = step % count

        @pl.when(i == 0)
        def _():
            for n in range(chunks):

                @pl.when(c == n)
                def _():
                    load(up_at + n).wait()
                    load(down_at + n).wait()

        act, slope = gelu_pair(nn(second[i], wup[c]))
        act = act.astype(BF16)
        ffn[i] += nn(act, wdown[c])
        up_grad = (nt(cot[i], wdown[c]) * slope).astype(BF16)
        dwdown_t[...] += nn(cot_t[i], act)
        dwup[...] += nn(second_t[i], up_grad)
        grad[i] += nt(up_grad, wup[c])

        half = SEG // TILE
        for n in range(chunks):

            @pl.when((i == count - 1) & (c == n))
            def _():
                target = work[n].buf if n < EARLY else late_buf.at[n - EARLY]
                target[:half] = tiles(dwup[...].astype(BF16))
                target[half:] = tiles(jnp.transpose(dwdown_t[...].astype(BF16)))
                dwup[...] = jnp.zeros_like(dwup)
                dwdown_t[...] = jnp.zeros_like(dwdown_t)
                if n >= EARLY:
                    pltpu.make_async_copy(target, late.at[n - EARLY], late_sems.at[n]).start()

        run_events(step, last, [e for e in events if e[0] < chunks * count])

    def finish(n, i):
        source, target = ((out_low, out), (grad, res_out), (o_t, d_out))[n]
        return pltpu.make_async_copy(source.at[i], target.at[i], stores.at[len(kept) + n, i])

    @pl.loop(0, count)
    def _(i):
        res = x[i].astype(F32) + nn(jnp.transpose(o_t[i]), wo[...])
        unit, inverse = norm(res)
        out_low[i] = ffn[i].astype(BF16)
        back, gain_part = norm_back(grad[i], unit, inverse, gain2[...])
        dgain[...] += gain_part
        back = back + cot[i].astype(F32)
        grad[i] = back
        row = back.astype(BF16)
        dwo[...] += nn(o_t[i], row)
        d = nt(wo[...], row).astype(BF16)
        prod = d.astype(F32) * o_t[i].astype(F32)
        for h in range(H):
            inner[i, h // 2, h % 2 : h % 2 + 1, :] = jnp.sum(prod[one(h), :], 0, keepdims=True)
        o_t[i] = d
        for n in range(3):
            finish(n, i).start()
        run_events(i + chunks * count, last, [e for e in events if e[0] >= chunks * count])

    dwo_out[...] = dwo[...].astype(BF16)
    for copy in gather(stats, gathers.at[1], index, group):
        copy.wait()
    for i in range(count):
        for n in range(len(kept)):
            keep(n, i).wait()
        for n in range(3):
            finish(n, i).wait()
    for n in range(EARLY):
        pltpu.make_async_copy(work[n].buf, sums[n], late_sems.at[n]).wait()
    for n in range(EARLY, chunks):
        pltpu.make_async_copy(late_buf.at[n - EARLY], late.at[n - EARLY], late_sems.at[n]).wait()


def update(
    index, stats, mem, slot_q, slot_k, slot_v, wgate, bgate, wwrite,
    new_memory, g_out, g_t, lse, inner_out, sq_acc, sk_acc, sv_acc, direct_out,
    dwgate, dwwrite, dbias, fresh,
):
    group, _, rows, width = mem.shape
    slots = group * rows
    pairs = H // 2
    same = (
        lax.broadcasted_iota(jnp.int32, (width, width), 0) // DH
        == lax.broadcasted_iota(jnp.int32, (width, width), 1) // DH
    ).astype(F32)

    def head_sum(value):
        return nn(value, same, lax.Precision.HIGHEST)

    start = index["slot"] * rows
    row = lax.broadcasted_iota(jnp.int32, (slots, width), 0)
    own = (row >= start) & (row < start + rows)
    sq, sk, sv = (
        jnp.concatenate([r[p] for p in range(pairs)], 1).astype(F32) for r in (slot_q, slot_k, slot_v)
    )
    state = mem[:, 0].reshape(slots, width).astype(F32)
    memory_out = mem[:, 1].reshape(slots, width).astype(F32)
    own_score = head_sum(sq * sk)
    top = own_score
    for n in range(group):
        top = jnp.maximum(top, stats[n, 1])
    power = jnp.exp(own_score - top)
    total = power
    weighted = power.astype(BF16).astype(F32) * sv
    for n in range(group):
        factor = jnp.exp(stats[n, 1] - top)
        total = total + factor * stats[n, 2]
        weighted = weighted + factor * stats[n, 0]
    value = weighted / total
    low = value.astype(BF16)
    gate = jax.nn.sigmoid(nn(low, wgate[...]) + bgate[...])
    written = nn(low, wwrite[...])
    fresh[...] = ((1.0 - gate) * state + gate * written).reshape(fresh.shape)
    new_memory[...] = fresh[index["slot"]]
    gate_grad = memory_out * (written - state) * gate * (1.0 - gate)
    gate_low = gate_grad.astype(BF16)
    written_low = (memory_out * gate).astype(BF16)
    zero = jnp.zeros((slots, width), F32)
    direct_out[...] = jnp.where(own, memory_out * (1.0 - gate), zero)
    mine = jnp.where(own, gate_grad, zero)
    dbias[...] = jnp.sum(mine, 0, keepdims=True)
    low_t = jnp.transpose(low)
    dwgate[...] = tiles(nn(low_t, mine.astype(BF16)).astype(BF16))
    dwwrite[...] = tiles(nn(low_t, jnp.where(own, memory_out * gate, zero).astype(BF16)).astype(BF16))
    g_low = (nt(gate_low, wgate[...]) + nt(written_low, wwrite[...])).astype(BF16)
    g = g_low.astype(F32)
    inner = head_sum(g * value)
    spread = top + jnp.log(total)
    delta = (power / total * (head_sum(g * sv) - inner)).astype(BF16).astype(F32)
    self_q = jnp.where(own, delta * sk, zero)
    self_k = jnp.where(own, delta * sq, zero)
    self_v = jnp.where(own, power.astype(BF16).astype(F32) / total * g, zero)
    for p in range(pairs):
        g_out[p] = g_low[:, two(p)]
        g_t[p] = jnp.transpose(g_low[:, two(p)])
        inner_out[p] = inner[:, two(p)]
        lse[p] = spread[:, two(p)]
        sq_acc[p] = jnp.transpose(self_q[:, two(p)])
        sk_acc[p] = jnp.transpose(self_k[:, two(p)])
        sv_acc[p] = jnp.transpose(self_v[:, two(p)])


def back_kernel(
    count, group, orders, sizes,
    x_in, low_in, q_in, k_in, kt_in, v_in, vt_in, d_in, res_in,
    wq_in, wk_in, wv_in, wsq_in, wgate_in, wwrite_in, late, dwo_in,
    lse, inner, doc, pad, gain1, mgain, slot_k, slot_kt, slot_v, slot_q, slot_qt, mem, stats, bgate,
    dgain2, *rest,
):
    early = len(sizes)
    input_grad = rest[0]
    sums = rest[1 : 1 + early]
    (
        dwq_out, dwk_out, dwv_out, dwsq_out, gains_out, memory_grad, new_memory,
        x, low, q_t, k, k_t, v, v_t, d_t, res, wq, wk, wv, wsq, wgate, wwrite,
        bias, grads, acc, w_all, sq_acc, sk_acc, sv_acc, g, g_t, wlse, winner, direct, fresh,
        slot_low, dgain, dgain3, dbias, part, part_in, part_sems, block_loads, loads, stores,
    ) = rest[1 + early : 46 + early]
    pairs = H // 2
    index = here()
    work = reductions(rest[46 + early :], early + pairs + 1, orders, index)
    wide = 2 * DH
    third = wo_blocks = wq.shape[0] // TILE

    blocks = (
        (q_in, q_t), (k_in, k), (kt_in, k_t), (v_in, v), (vt_in, v_t), (d_in, d_t), (low_in, low),
        (x_in, x), (res_in, res),
    )
    used = 7

    def block(n, i):
        return pltpu.make_async_copy(blocks[n][0].at[i], blocks[n][1].at[i], block_loads.at[n, i])

    whole = (
        [(wgate_in, wgate), (wwrite_in, wwrite), (wq_in, wq), (wk_in, wk), (wv_in, wv), (wsq_in, wsq)]
        + [(late.at[n], work[n].buf) for n in range(early - 1)]
        + [(dwo_in, work[early - 1].buf.at[:wo_blocks])]
    )

    def load(n):
        return pltpu.make_async_copy(*whole[n], loads.at[n])

    for n in (0, 1):
        load(n).start()
    for n in range(used):
        block(n, 0).start()
    for n in range(2, len(whole)):
        load(n).start()
    for i in range(1, count):
        for n in range(used):
            block(n, i).start()
    for i in range(count):
        for n in range(used, len(blocks)):
            block(n, i).start()
    greet(orders, index, group)
    load(0).wait()
    load(1).wait()
    update(
        index, stats, mem, slot_q, slot_k, slot_v, wgate, bgate, wwrite,
        new_memory, g, g_t, wlse, winner, sq_acc, sk_acc, sv_acc, direct,
        work[early - 1].buf.at[third : 2 * third], work[early - 1].buf.at[2 * third :], dbias, fresh,
    )
    for n in range(2, 6):
        load(n).wait()
    for n in range(pairs):
        for m, w in enumerate((wq, wk, wv)):
            at = (3 * n + m) * wide
            w_all[:, at : at + wide] = w[:, two(n)]
    slots = group * mem.shape[2]
    unit3, inverse3 = norm(mem[:, 0].reshape(slots, mem.shape[3]).astype(F32))
    slot_low[...] = (unit3 * mgain[...]).astype(BF16)
    dgain[...] = jnp.zeros_like(dgain)
    acc[...] = jnp.zeros_like(acc)

    strides = [1 << n for n in reversed(range(group.bit_length() - 1))]

    def scatter(level):
        stride = strides[level]
        start, at = 0, 0
        for s in strides[:level]:
            start = start + across(index, "slot", s)[0] * s
            at += s
        bit, peer = across(index, "slot", stride)
        copy = pltpu.make_async_remote_copy(
            part.at[pl.ds(start + stride - bit * stride, stride)], part_in.at[pl.ds(at, stride)],
            part_sems.at[0, level], part_sems.at[1, level], device_id=peer, device_id_type=MESH,
        )
        return copy, start + bit * stride, at, stride

    def slot_grads(stage):
        if stage == 0:
            unit, inverse = norm(mem[:, 0].reshape(slots, mem.shape[3]).astype(F32))
            grad_t = 0.0
            for p in range(pairs):
                grad_t = (
                    grad_t
                    + nn(wk[:, two(p)], sk_acc[p].astype(BF16))
                    + nn(wv[:, two(p)], sv_acc[p].astype(BF16))
                    + nn(wsq[:, two(p)], (sq_acc[p] * SCALE).astype(BF16))
                )
            back, gain_part = norm_back(jnp.transpose(grad_t), unit, inverse, mgain[...])
            part[...] = (back + direct[...]).reshape(part.shape)
            dgain3[...] = gain_part
        else:
            copy, keep, at, size = scatter(stage - 1)
            copy.wait()
            part[pl.ds(keep, size)] += part_in[pl.ds(at, size)]
        if stage < len(strides):
            scatter(stage)[0].start()
        else:
            memory_grad[...] = part[index["slot"]]

    def gains(stage):
        item = work[early + pairs]
        if stage == 0:
            rows = [jnp.broadcast_to(r[...], (8, dgain.shape[1])) for r in (dgain, dgain3, dgain2, dbias)]
            item.buf[...] = tiles(jnp.concatenate(rows, 0).astype(BF16))
        item.tick(stage)
        if stage == item.stages - 1:
            gains_out[...] = item.buf[...].reshape(gains_out.shape).astype(F32)

    def summed(n, stage):
        item = work[n]
        if n < early and stage == 0:
            load(6 + n).wait()
        item.tick(stage)
        if stage < item.stages - 1:
            return
        if n < early:
            pltpu.make_async_copy(item.buf, sums[n], stores.at[n]).start()
            return
        per = wide // TILE
        for m, out in enumerate((dwq_out, dwk_out, dwv_out, dwsq_out)):
            rows = item.buf[m * per : (m + 1) * per].reshape(wide, out.shape[0])
            out[:, two(n - early)] = jnp.transpose(rows)

    busy = pairs * count
    last = busy + count - 1
    events = []
    for n in range(early):
        events += [(n // 2 + stage, summed, (n, stage)) for stage in range(work[n].stages)]
    for n in range(pairs):
        events += [
            ((n + 1) * count - 1 + stage, summed, (early + n, stage))
            for stage in range(work[early + n].stages)
        ]
    events += [(busy + stage, slot_grads, (stage,)) for stage in range(len(strides) + 1)]
    events += [(last + stage, gains, (stage,)) for stage in range(work[early + pairs].stages)]

    @pl.loop(0, busy)
    def _(step):
        p = step // count
        i = step % count

        @pl.when(p == 0)
        def _():
            for n in range(used):
                block(n, i).wait()
            cols = pl.ds(pl.multiple_of(i * SEG, SEG), SEG)
            bias[i] = segment_bias(doc[:, cols], pad[:, cols])

        cols = pl.ds(pl.multiple_of(i * SEG, SEG), SEG)
        pad_bias = jnp.where(pad[:, cols] > 0, 0.0, FILL)
        for odd in range(2):
            own = one(odd)
            qm = head_rows(q_t[i, p], odd)
            dm = head_rows(d_t[i, p], odd)
            c = nn(head_lanes(slot_q[p], odd), k_t[i, p]) + pad_bias
            share = jnp.exp(c - wlse[p, :, odd * DH : odd * DH + 1])
            dotted = nn(head_lanes(g[p], odd), v_t[i, p])
            change = (share * (dotted - winner[p, :, odd * DH : odd * DH + 1])).astype(BF16)
            dk = nn(slot_qt[p, own, :], change)
            dv = nn(g_t[p, own, :], share.astype(BF16))
            sq_acc[p, own, :] += nt(k_t[i, p, own, :], change)
            for lo, hi in BLOCKS:
                qb = qm[:, lo:hi]
                db = dm[:, lo:hi]
                qh = q_t[i, p, own, lo:hi]
                dh = d_t[i, p, own, lo:hi]
                l = lse[i, p, odd : odd + 1, lo:hi]
                t = inner[i, p, odd : odd + 1, lo:hi]
                e = jnp.exp(nn(k[i, p, :hi, :], qb) + bias[i, :hi, lo:hi] - l)
                em = jnp.exp(nn(slot_k[p], qb) - l)
                ds = (e * (nn(v[i, p, :hi, :], db) - t)).astype(BF16)
                dsm = (em * (nn(slot_v[p], db) - t)).astype(BF16)
                dq = (nn(k_t[i, p, own, :hi], ds) + nn(slot_kt[p, own, :], dsm)) * SCALE
                grads[i, p, own, lo:hi] = dq.astype(BF16)
                dvp = nt(dh, e.astype(BF16))
                dkp = nt(qh, ds)
                if hi < SEG:
                    dvp = jnp.concatenate([dvp, jnp.zeros((DH, SEG - hi), F32)], 1)
                    dkp = jnp.concatenate([dkp, jnp.zeros((DH, SEG - hi), F32)], 1)
                dv = dv + dvp
                dk = dk + dkp
                sv_acc[p, own, :] += nt(dh, em.astype(BF16))
                sk_acc[p, own, :] += nt(qh, dsm)
            grads[i, p, wide + odd * DH : wide + (odd + 1) * DH, :] = dk.astype(BF16)
            grads[i, p, 2 * wide + odd * DH : 2 * wide + (odd + 1) * DH, :] = dv.astype(BF16)
        acc[...] += nn(grads[i, p], low[i])

        @pl.when(i == count - 1)
        def _():
            rows = jnp.concatenate(
                [
                    acc[:wide],
                    acc[wide : 2 * wide] + nn(sk_acc[p].astype(BF16), slot_low[...]),
                    acc[2 * wide :] + nn(sv_acc[p].astype(BF16), slot_low[...]),
                    nn((sq_acc[p] * SCALE).astype(BF16), slot_low[...]),
                ],
                0,
            )
            acc[...] = jnp.zeros_like(acc)
            rows = tiles(rows.astype(BF16))
            for n in range(pairs):

                @pl.when(p == n)
                def _():
                    work[early + n].buf[...] = rows

        run_events(step, last, [e for e in events if e[0] < busy])

    @pl.loop(0, count)
    def _(i):
        block(used, i).wait()
        block(used + 1, i).wait()
        unit, inverse = norm(x[i].astype(F32))
        grad_t = nn(w_all[...], grads[i].reshape(3 * pairs * wide, SEG))
        back, gain_part = norm_back(jnp.transpose(grad_t), unit, inverse, gain1[...])
        dgain[...] += gain_part
        res[i] += back
        pltpu.make_async_copy(res.at[i], input_grad.at[i], block_loads.at[0, i]).start()
        run_events(i + busy, last, [e for e in events if e[0] >= busy])

    for i in range(count):
        pltpu.make_async_copy(res.at[i], input_grad.at[i], block_loads.at[0, i]).wait()
    for n in range(early):
        pltpu.make_async_copy(work[n].buf, sums[n], stores.at[n]).wait()


def struct(shape, dtype):
    return jax.ShapeDtypeStruct(shape, dtype)


def params(collective_id):
    return pltpu.CompilerParams(
        vmem_limit_bytes=63 << 20, collective_id=collective_id, has_side_effects=True
    )


def body(
    tokens,
    memory,
    pad_mask,
    doc_lengths,
    first_gain,
    query_weight,
    key_weight,
    value_weight,
    out_weight,
    second_gain,
    up_weight,
    down_weight,
    memory_gain,
    slot_query_weight,
    gate_weight,
    gate_bias,
    write_weight,
    out_cotangent,
    memory_cotangent,
):
    rows, width = tokens.shape
    hidden = up_weight.shape[1]
    count = rows // SEG
    chunks = hidden // SEG
    pairs = H // 2
    two_heads = 2 * DH
    slots_here = memory.shape[1]
    group = lax.axis_size("slot")
    slots = slots_here * group
    begin = (lax.axis_index("dp") * group + lax.axis_index("slot")) * rows
    places = begin + jnp.arange(rows, dtype=jnp.int32)
    ends = jnp.cumsum(doc_lengths)
    document = jnp.sum((places[:, None] >= ends[None, :]).astype(jnp.int32), 1)
    doc = document.astype(F32)[None, :]
    pad = pad_mask.astype(F32)[None, :]
    gain1, gain2, gain3 = (g[None, :] for g in (first_gain, second_gain, memory_gain))
    orders = bit_orders({"dp": lax.axis_size("dp"), "slot": group})

    anywhere = pl.BlockSpec(memory_space=pl.ANY)
    vm = pl.BlockSpec(memory_space=pltpu.VMEM)
    tokens = tokens.reshape(count, SEG, width)
    segments = (count, SEG, width)
    by_rows = (count, pairs, SEG, two_heads)
    by_lanes = (count, pairs, two_heads, SEG)
    square = (width, width)
    blocks = 2 * SEG // TILE
    half = SEG // TILE
    slot_tall, slot_wide = (pairs, slots, two_heads), (pairs, two_heads, slots)
    per_head = (count, pairs, 2, SEG)
    outs = pl.pallas_call(
        lambda *refs: front_kernel(count, chunks, group, orders, *refs),
        in_specs=[anywhere] * 10 + [vm] * 5,
        out_specs=[anywhere] * (10 + EARLY) + [vm] * 11,
        out_shape=[
            struct(segments, BF16), struct(segments, F32), struct(segments, BF16),
            struct(by_lanes, BF16), struct(by_rows, BF16), struct(by_lanes, BF16),
            struct(by_rows, BF16), struct(by_lanes, BF16), struct((count, width, SEG), BF16),
            struct((chunks - EARLY, blocks, TILE, width), BF16),
        ]
        + [struct((blocks, TILE, width), BF16)] * EARLY
        + [
            struct(per_head, F32), struct(per_head, F32), struct(slot_tall, BF16),
            struct(slot_wide, BF16), struct(slot_tall, BF16), struct(slot_tall, BF16),
            struct(slot_wide, BF16), struct((group, 2, slots_here, width), BF16),
            struct((group, 3, slots, width), F32), struct(square, BF16), struct((1, width), F32),
        ],
        scratch_shapes=[
            pltpu.VMEM(segments, BF16), pltpu.VMEM(segments, BF16), pltpu.VMEM(segments, BF16),
            pltpu.VMEM(by_lanes, BF16), pltpu.VMEM(by_rows, BF16), pltpu.VMEM(by_lanes, BF16),
            pltpu.VMEM(by_rows, BF16), pltpu.VMEM(by_lanes, BF16),
            pltpu.VMEM((count, width, SEG), BF16), pltpu.VMEM(segments, BF16),
            pltpu.VMEM((count, width, SEG), BF16), pltpu.VMEM((count, width, SEG), BF16),
            pltpu.VMEM(segments, F32), pltpu.VMEM(segments, F32),
            pltpu.VMEM(square, BF16), pltpu.VMEM(square, BF16), pltpu.VMEM(square, BF16),
            pltpu.VMEM(square, BF16), pltpu.VMEM(square, BF16),
            pltpu.VMEM((chunks, width, SEG), BF16), pltpu.VMEM((chunks, SEG, width), BF16),
            pltpu.VMEM(slot_wide, BF16), pltpu.VMEM((SEG, SEG), F32), pltpu.VMEM(square, F32),
            pltpu.VMEM((width, SEG), F32), pltpu.VMEM((width, SEG), F32),
            pltpu.VMEM(segments, BF16), pltpu.VMEM((chunks - EARLY, blocks, TILE, width), BF16),
            pltpu.SemaphoreType.DMA((2 * count + 6 + 2 * chunks,)),
            pltpu.SemaphoreType.DMA((9, count)),
            pltpu.SemaphoreType.DMA((2, 2, group)),
            pltpu.SemaphoreType.DMA((chunks,)),
        ]
        + reduction_scratch([blocks] * EARLY, orders, width),
        compiler_params=params(0),
        name="front",
    )(
        tokens, jnp.stack([memory[0], memory_cotangent[0]]), query_weight, key_weight, value_weight,
        slot_query_weight, out_weight, up_weight, down_weight.reshape(chunks, SEG, width),
        out_cotangent.reshape(segments), doc, pad, gain1, gain2, gain3,
    )
    layer_out, res_grad, low, q_t, k, k_t, v, v_t, d_t, late = outs[:10]
    early = list(outs[10 : 10 + EARLY])
    (
        lse, inner, slot_k, slot_kt, slot_v, slot_q, slot_qt, mem, stats, dwo, dgain2,
    ) = outs[10 + EARLY :]

    sizes = [blocks] * (chunks - EARLY) + [3 * half]
    n_sum = len(sizes)
    outs = pl.pallas_call(
        lambda *refs: back_kernel(count, group, orders, sizes, *refs),
        in_specs=[anywhere] * 17 + [vm] * 15,
        out_specs=[anywhere] * (1 + n_sum) + [vm] * 7,
        out_shape=[struct(segments, F32)]
        + [struct((n, TILE, width), BF16) for n in sizes]
        + [struct(square, BF16)] * 4
        + [
            struct((32, width), F32), struct((slots_here, width), F32), struct((slots_here, width), F32),
        ],
        scratch_shapes=[
            pltpu.VMEM(segments, BF16), pltpu.VMEM(segments, BF16), pltpu.VMEM(by_lanes, BF16),
            pltpu.VMEM(by_rows, BF16), pltpu.VMEM(by_lanes, BF16), pltpu.VMEM(by_rows, BF16),
            pltpu.VMEM(by_lanes, BF16), pltpu.VMEM(by_lanes, BF16), pltpu.VMEM(segments, F32),
            pltpu.VMEM(square, BF16), pltpu.VMEM(square, BF16), pltpu.VMEM(square, BF16),
            pltpu.VMEM(square, BF16), pltpu.VMEM(square, BF16), pltpu.VMEM(square, BF16),
            pltpu.VMEM((count, SEG, SEG), F32), pltpu.VMEM((count, pairs, 3 * two_heads, SEG), BF16),
            pltpu.VMEM((3 * two_heads, width), F32), pltpu.VMEM((width, 3 * width), BF16),
            pltpu.VMEM(slot_wide, F32), pltpu.VMEM(slot_wide, F32), pltpu.VMEM(slot_wide, F32),
            pltpu.VMEM(slot_tall, BF16), pltpu.VMEM(slot_wide, BF16), pltpu.VMEM(slot_tall, F32),
            pltpu.VMEM(slot_tall, F32), pltpu.VMEM((slots, width), F32),
            pltpu.VMEM((group, slots_here, width), F32), pltpu.VMEM((slots, width), BF16),
            pltpu.VMEM((1, width), F32), pltpu.VMEM((1, width), F32), pltpu.VMEM((1, width), F32),
            pltpu.VMEM((group, slots_here, width), F32), pltpu.VMEM((group, slots_here, width), F32),
            pltpu.SemaphoreType.DMA((2, group)), pltpu.SemaphoreType.DMA((9, count)),
            pltpu.SemaphoreType.DMA((6 + n_sum,)), pltpu.SemaphoreType.DMA((n_sum,)),
        ]
        + reduction_scratch(sizes + [4 * two_heads // TILE] * pairs + [2], orders, width),
        compiler_params=params(1),
        name="back",
    )(
        tokens, low, q_t, k, k_t, v, v_t, d_t.reshape(by_lanes), res_grad,
        query_weight, key_weight, value_weight, slot_query_weight, gate_weight, write_weight,
        late, tiles(dwo),
        lse, inner, doc, pad, gain1, gain3, slot_k, slot_kt, slot_v, slot_q, slot_qt, mem, stats,
        gate_bias[None, :], dgain2,
    )
    input_grad = outs[0].reshape(rows, width)
    sums = outs[1 : 1 + n_sum]
    dwq, dwk, dwv, dwsq, gains, memory_grad, new_memory = outs[1 + n_sum :]
    ffn = early + list(sums[:-1])
    dwup = jnp.concatenate([f[:half].reshape(width, SEG) for f in ffn], 1)
    dwdown = jnp.concatenate([f[half:].reshape(SEG, width) for f in ffn], 0)
    dwo, dwgate, dwwrite = (
        sums[-1][n * half : (n + 1) * half].reshape(width, width) for n in range(3)
    )

    return (
        layer_out.reshape(rows, width),
        new_memory[None],
        input_grad,
        memory_grad[None],
        gains[0],
        dwq.astype(F32),
        dwk.astype(F32),
        dwv.astype(F32),
        dwo.astype(F32),
        gains[16],
        dwup.astype(F32),
        dwdown.astype(F32),
        gains[8],
        dwsq.astype(F32),
        dwgate.astype(F32),
        gains[24],
        dwwrite.astype(F32),
    )


def solution(mesh):
    token = P(("dp", "slot"), None)
    slot = P("dp", "slot", None)
    in_specs = (
        (token, slot, P(("dp", "slot"))) + (P(),) * 14 + (token, slot)
    )
    out_specs = (token, slot, token, slot) + (P(),) * 13
    return jax.shard_map(body, mesh=mesh, in_specs=in_specs, out_specs=out_specs, check_vma=False)
```

time: 301 us -> 262 us (0.87)
  Pallas kernels: 244 us -> 230 us
  between operations: 14.1 us -> 0.74 us
  blocking collectives: 6.49 us -> 0 us
  local copies, waits for them, and re-layouts: 14.5 us -> 11 us
    pallas_call x5 -> x2, Pallas kernels: 244 us -> 230 us  [the longest x1 120 us: body(): pl.pallas_call(lambda *refs: back_kernel(count, group, orders, sizes, *re...]
    all_gather x1 -> x0, blocking collectives: 6.49 us -> none  [body(): lax.all_gather(jnp.concatenate([memory[0], memory_cotangent[0]], 1), 'slo...]
    concatenate x3 -> x0, other arithmetic: 3.88 us -> none  [the longest x1 2.54 us: body(): jnp.concatenate([tiles(dwo), tiles(dwgate), tiles(dwwrite)], 0)]
    squeeze x1 -> x0, local copies, waits for them, and re-layouts: 3.17 us -> none  [body(): late[n]]
    unnamed x29 -> x28, local copies, waits for them, and re-layouts: 6.51 us -> 6.52 us
  transfers between devices with their start and end apart: 1 -> 0, of which waited for: 0 -> 0; matrix products, arithmetic and copies ran while one was open for 2% -> 0% of each run, Pallas kernels for 35% -> 0%
where the time goes in v3:
time: 262 us; the launch traced here: 261 us
  Pallas kernels  230 us (88%)
  other arithmetic  19.4 us (7%)
  local copies, waits for them, and re-layouts  11 us (4%)
    pallas_call x1, Pallas kernels, body(): pl.pallas_call(lambda *refs: back_kernel(count, group, orders, sizes, *re...  120 us
    pallas_call x1, Pallas kernels, body(): pl.pallas_call(lambda *refs: front_kernel(count, chunks, group, orders, *...  111 us
    unnamed x28, local copies, waits for them, and re-layouts  6.52 us

profile of v3, /device:TPU:0, one launch (start us, length us, event | category | flops | bytes accessed | tf_op | source)
XLA Modules:
  0.0 261.3 jit_solution(3963488205247704985)
XLA Ops:
  0.7 0.8 reduce-window.8
  1.5 0.1 convert_reduce_fusion
  1.6 0.6 convert_element_type.56
  2.2 1.3 convert_element_type.58
  3.5 1.4 pad_maximum_fusion.refs_1_
  4.9 110.7 %front.1 = (bf16[4,512,512]{2,1,0:T(8,128)(2,1)}, f32[4,512,512]{2,1,0:T(8,128)}, bf16[4,512,512]{2,1,0:T(8,128)(2,1)}, bf16[4,4,128,512]{3,2,1,0:T(8,128)(2,1)}...) custom-call(bf16[4,512,512]{2,1,0:T(8,128)(2,1)} %bitcast.38, ...), custom_call_target="tpu_custom_call" | custom-call | tf_op jit(solution)/shard_map/front/pallas_call | solution.py:863
  115.5 2.7 %fusion.1 = (bf16[32,16,512]{2,1,0:T(8,128)(2,1)S(1)}, bf16[32,16,512]{2,1,0:T(8,128)(2,1)}, bf16[32,16,512]{2,1,0:T(8,128)(2,1)}, bf16[32,16,512]{2,1,0:T(8,128)(2,1)}) fusion(bf16[64,16,512]{2,1,0:T(8,128)(2,1)} %get-tuple-element.80, bf16[64,16,512]{2,1,0:T(8,128)(2,1)} %get-tuple-element.81), kind=kLoop, calls=%fused_computation.9 | loop fusion | bytes 4194304 | tf_op jit(solution)/shard_map/slice | solution.py:956
  118.2 119.5 %back.1 = (f32[4,512,512]{2,1,0:T(8,128)}, bf16[64,16,512]{2,1,0:T(8,128)(2,1)}, bf16[64,16,512]{2,1,0:T(8,128)(2,1)}, bf16[96,16,512]{2,1,0:T(8,128)(2,1)}, bf1...) custom-call(bf16[4,512,512]{2,1,0:T(8,128)(2,1)} %bitcast.39, ...), custom_call_target="tpu_custom_call" | custom-call | tf_op jit(solution)/shard_map/back/pallas_call | solution.py:914
  237.7 0.0 copy-start.9
  237.7 1.4 fusion.5
  239.2 0.0 copy-start.8
  239.2 2.2 convert_element_type.59
  241.4 0.0 copy-start.7
  241.4 2.2 convert_element_type.60
  243.6 0.0 copy-done.9
  243.6 1.1 convert_element_type.61
  244.7 0.0 copy-done.8
  244.7 0.0 copy-start.5
  244.7 0.0 copy-start.6
  244.7 1.1 convert_element_type.66
  245.8 0.0 copy-done.7
  245.8 0.1 fusion.4
  245.9 0.6 copy-done.5
  246.5 0.3 copy-done.6
  246.8 0.3 fusion
  247.1 0.0 copy-start.3
  247.1 0.0 copy-start.4
  247.1 1.1 bitcast_convert_fusion
  248.2 1.1 bitcast_convert_fusion.1
  249.4 1.1 bitcast_convert_fusion.2
  250.5 0.0 copy-done.3
  250.5 0.0 copy-done.4
  250.5 0.0 copy-start.2
  250.5 2.6 maximum_convert_fusion
  253.1 0.0 copy-done.2
  253.1 0.0 copy-start.1
  253.1 0.0 copy-start.11
  253.1 2.6 maximum_convert_fusion.1
  255.7 0.0 copy-done.1
  255.7 0.0 copy-start
  255.7 1.3 copy.40
  257.0 0.0 copy-done.11
  257.0 0.6 copy.41
  257.6 1.0 copy-done
  258.7 0.0 copy-start.10
  258.7 2.0 copy.42
  260.7 0.0 copy-done.10
  260.7 0.6 copy.43
  (1 shorter events, 0.0 us)
Async XLA Ops:
  237.7 5.9 %copy-start.9 = (bf16[512,512]{1,0:T(8,128)(2,1)S(1)}, bf16[512,512]{1,0:T(8,128)(2,1)}, u32[]{:S(2)}) copy-start(bf16[512,512]{1,0:T(8,128)(2,1)} %get-tuple-element.78) | copy-start | bytes 1572868
  239.2 5.5 %copy-start.8 = (bf16[512,512]{1,0:T(8,128)(2,1)S(1)}, bf16[512,512]{1,0:T(8,128)(2,1)}, u32[]{:S(2)}) copy-start(bf16[512,512]{1,0:T(8,128)(2,1)} %get-tuple-element.84) | copy-start | bytes 1572868
  241.4 4.4 %copy-start.7 = (bf16[64,16,512]{2,1,0:T(8,128)(2,1)S(1)}, bf16[64,16,512]{2,1,0:T(8,128)(2,1)}, u32[]{:S(2)}) copy-start(bf16[64,16,512]{2,1,0:T(8,128)(2,1)} %get-tuple-element.83) | copy-start | bytes 3145732
  244.7 1.8 copy-start.5
  244.7 2.1 copy-start.6
  247.1 3.4 %copy-start.3 = (bf16[32,16,512]{2,1,0:T(8,128)(2,1)S(1)}, bf16[32,16,512]{2,1,0:T(8,128)(2,1)}, u32[]{:S(2)}) copy-start(bf16[32,16,512]{2,1,0:T(8,128)(2,1)} %get-tuple-element.89) | copy-start | bytes 1572868
  247.1 3.4 %copy-start.4 = (bf16[32,16,512]{2,1,0:T(8,128)(2,1)S(1)}, bf16[32,16,512]{2,1,0:T(8,128)(2,1)}, u32[]{:S(2)}) copy-start(bf16[32,16,512]{2,1,0:T(8,128)(2,1)} %get-tuple-element.100) | copy-start | bytes 1572868
  250.5 2.6 copy-start.2
  253.1 2.6 %copy-start.1 = (bf16[4,512,512]{2,1,0:T(8,128)(2,1)S(1)}, bf16[4,512,512]{2,1,0:T(8,128)(2,1)}, u32[]{:S(2)}) copy-start(bf16[4,512,512]{2,1,0:T(8,128)(2,1)} %get-tuple-element.51) | copy-start | bytes 6291460
  253.1 3.9 %copy-start.11 = (f32[16,512]{1,0:T(8,128)S(1)}, f32[16,512]{1,0:T(8,128)}, u32[]{:S(2)}) copy-start(f32[16,512]{1,0:T(8,128)} %get-tuple-element.72) | copy-start | bytes 98308
  255.7 3.0 %copy-start = (f32[4,512,512]{2,1,0:T(8,128)S(1)}, f32[4,512,512]{2,1,0:T(8,128)}, u32[]{:S(2)}) copy-start(f32[4,512,512]{2,1,0:T(8,128)} %get-tuple-element.73) | copy-start | bytes 12582916
  258.7 2.0 copy-start.10

commit v4 on v3

--- a/solution.py
+++ b/solution.py
@@ -71,6 +71,16 @@
     columns = lax.broadcasted_iota(jnp.int32, (SEG, SEG), 1)
     seen = (rows <= columns) & (key_code == doc_row)
     return jnp.where(seen, 0.0, FILL)
+
+
+def documents(lengths, index, group, rows):
+    place = lax.broadcasted_iota(jnp.int32, (1, rows), 1)
+    place = place + (index["dp"] * group + index["slot"]) * rows
+    end, doc = 0, jnp.zeros((1, rows), F32)
+    for n in range(lengths.shape[0]):
+        end = end + lengths[n]
+        doc = doc + jnp.where(place >= end, 1.0, 0.0)
+    return doc
 
 
 def head_rows(pair, odd):
@@ -265,19 +275,19 @@
 
 def front_kernel(
     count, chunks, group, orders,
-    x_in, mem_in, wq_in, wk_in, wv_in, wsq_in, wo_in, wup_in, wdown_in, cot_in,
-    doc, pad, gain1, gain2, gain3,
+    x_in, mem_in, mem_cot_in, wq_in, wk_in, wv_in, wsq_in, wo_in, wup_in, wdown_in, cot_in,
+    lengths, pad, gain1, gain2, gain3,
     out, res_out, low_out, q_out, k_out, kt_out, v_out, vt_out, d_out, late, *rest,
 ):
     sums, rest = rest[:EARLY], rest[EARLY:]
     (lse, inner, slot_k, slot_kt, slot_v, slot_q, slot_qt, mem, stats, dwo_out, dgain) = rest[:11]
     (
         x, cot, low, q_t, k, k_t, v, v_t, o_t, second, second_t, cot_t, ffn, grad,
-        wq, wk, wv, wsq, wo, wup, wdown, slot_vt, bias, dwo, dwup, dwdown_t, out_low, late_buf,
+        wq, wk, wv, wsq, wo, wup, wdown, slot_vt, bias, dwo, dwup, dwdown_t, out_low, late_buf, doc,
         loads, stores, gathers, late_sems,
-    ) = rest[11:43]
+    ) = rest[11:44]
     index = here()
-    work = reductions(rest[43:], EARLY, orders, index)
+    work = reductions(rest[44:], EARLY, orders, index)
     pairs = H // 2
 
     def load(n):
@@ -289,7 +299,7 @@
                 (wup_in.at[:, c * SEG : (c + 1) * SEG], wup.at[c]) for c in range(chunks)
             ]
             + [(wdown_in.at[c], wdown.at[c]) for c in range(chunks)]
-            + [(mem_in, mem.at[index["slot"]])]
+            + [(mem_in, mem.at[index["slot"], 0]), (mem_cot_in, mem.at[index["slot"], 1])]
         )
         return pltpu.make_async_copy(*pairs_of[n], loads.at[n])
 
@@ -299,7 +309,7 @@
     down_at = up_at + chunks
     mem_at = down_at + chunks
     order = (
-        [mem_at, 0, weights_at, weights_at + 1, weights_at + 2]
+        [mem_at, mem_at + 1, 0, weights_at, weights_at + 1, weights_at + 2]
         + list(range(1, count))
         + [weights_at + 3, weights_at + 4]
         + list(range(cot_at, mem_at))
@@ -308,8 +318,10 @@
         load(n).start()
     greet(orders, index, group)
     load(mem_at).wait()
+    load(mem_at + 1).wait()
     for copy in gather(mem, gathers.at[0], index, group):
         copy.start()
+    doc[...] = documents(lengths, index, group, doc.shape[1])
     dwo[...] = jnp.zeros_like(dwo)
     dwup[...] = jnp.zeros_like(dwup)
     dwdown_t[...] = jnp.zeros_like(dwdown_t)
@@ -567,7 +579,7 @@
     count, group, orders, sizes,
     x_in, low_in, q_in, k_in, kt_in, v_in, vt_in, d_in, res_in,
     wq_in, wk_in, wv_in, wsq_in, wgate_in, wwrite_in, late, dwo_in,
-    lse, inner, doc, pad, gain1, mgain, slot_k, slot_kt, slot_v, slot_q, slot_qt, mem, stats, bgate,
+    lse, inner, lengths, pad, gain1, mgain, slot_k, slot_kt, slot_v, slot_q, slot_qt, mem, stats, bgate,
     dgain2, *rest,
 ):
     early = len(sizes)
@@ -577,11 +589,11 @@
         dwq_out, dwk_out, dwv_out, dwsq_out, gains_out, memory_grad, new_memory,
         x, low, q_t, k, k_t, v, v_t, d_t, res, wq, wk, wv, wsq, wgate, wwrite,
         bias, grads, acc, w_all, sq_acc, sk_acc, sv_acc, g, g_t, wlse, winner, direct, fresh,
-        slot_low, dgain, dgain3, dbias, part, part_in, part_sems, block_loads, loads, stores,
-    ) = rest[1 + early : 46 + early]
+        slot_low, dgain, dgain3, dbias, part, part_in, doc, part_sems, block_loads, loads, stores,
+    ) = rest[1 + early : 47 + early]
     pairs = H // 2
     index = here()
-    work = reductions(rest[46 + early :], early + pairs + 1, orders, index)
+    work = reductions(rest[47 + early :], early + pairs + 1, orders, index)
     wide = 2 * DH
     third = wo_blocks = wq.shape[0] // TILE
 
@@ -616,6 +628,7 @@
         for n in range(used, len(blocks)):
             block(n, i).start()
     greet(orders, index, group)
+    doc[...] = documents(lengths, index, group, doc.shape[1])
     load(0).wait()
     load(1).wait()
     update(
@@ -800,6 +813,67 @@
         pltpu.make_async_copy(work[n].buf, sums[n], stores.at[n]).wait()
 
 
+def widen_kernel(chunks, half, *refs):
+    ffn, rest = refs[:chunks], refs[chunks:]
+    own, dwq, dwk, dwv, dwsq, layer_in, grad_in, new_in, mem_in, gains_in = rest[:10]
+    (
+        layer_out, new_out, grad_out, mem_out,
+        dwq_out, dwk_out, dwv_out, dwo_out, dwsq_out, dwgate_out, dwwrite_out, dwup_out, dwdown_out,
+    ) = rest[10:23]
+    gain_outs = rest[23:27]
+    layer, grad, slots, gains, low, wide = rest[27:33]
+    rows, loads, stores = rest[33:37], rest[37], rest[38]
+    count, seg = layer.shape[:2]
+
+    jobs = [(dwq, dwq_out), (dwk, dwk_out), (dwv, dwv_out), (dwsq, dwsq_out)]
+    for n, out in enumerate((dwo_out, dwgate_out, dwwrite_out)):
+        jobs.append((own.at[n * half : (n + 1) * half], out))
+    for c in range(chunks):
+        jobs.append((ffn[c].at[:half], dwup_out.at[:, c * seg : (c + 1) * seg]))
+        jobs.append((ffn[c].at[half:], dwdown_out.at[c * seg : (c + 1) * seg, :]))
+    passed = [(gains_in, gains, None)]
+    passed += [(new_in, slots.at[0], new_out), (mem_in, slots.at[1], mem_out)]
+    for i in range(count):
+        passed += [
+            (grad_in.at[i], grad.at[i], grad_out.at[i]),
+            (layer_in.at[i], layer.at[i], layer_out.at[i]),
+        ]
+    moves = [(source, low.at[n], wide.at[n], target) for n, (source, target) in enumerate(jobs)]
+    todo = []
+    for n in range(max(len(moves), len(passed))):
+        todo += moves[n : n + 1] + passed[n : n + 1]
+    copies = [pltpu.make_async_copy(t[0], t[1], loads.at[n]) for n, t in enumerate(todo)]
+    for copy in copies:
+        copy.start()
+    sent = []
+
+    def send(source, target):
+        copy = pltpu.make_async_copy(source, target, stores.at[len(sent)])
+        copy.start()
+        sent.append(copy)
+
+    for copy, t in zip(copies, todo):
+        copy.wait()
+        if len(t) == 4:
+            _, narrow, full, target = t
+            per = 4
+
+            @pl.loop(0, half // per)
+            def _(b):
+                at = pl.ds(pl.multiple_of(b * per * TILE, per * TILE), per * TILE)
+                full[at, :] = narrow[pl.ds(b * per, per)].reshape(per * TILE, full.shape[1]).astype(F32)
+
+            send(full, target)
+        elif t[2] is None:
+            for n, at in enumerate((0, 16, 8, 24)):
+                rows[n][...] = gains[at : at + 1, :]
+                send(rows[n], gain_outs[n])
+        else:
+            send(t[1], t[2])
+    for copy in sent:
+        copy.wait()
+
+
 def struct(shape, dtype):
     return jax.ShapeDtypeStruct(shape, dtype)
 
@@ -840,17 +914,13 @@
     slots_here = memory.shape[1]
     group = lax.axis_size("slot")
     slots = slots_here * group
-    begin = (lax.axis_index("dp") * group + lax.axis_index("slot")) * rows
-    places = begin + jnp.arange(rows, dtype=jnp.int32)
-    ends = jnp.cumsum(doc_lengths)
-    document = jnp.sum((places[:, None] >= ends[None, :]).astype(jnp.int32), 1)
-    doc = document.astype(F32)[None, :]
-    pad = pad_mask.astype(F32)[None, :]
+    pad = pad_mask[None, :]
     gain1, gain2, gain3 = (g[None, :] for g in (first_gain, second_gain, memory_gain))
     orders = bit_orders({"dp": lax.axis_size("dp"), "slot": group})
 
     anywhere = pl.BlockSpec(memory_space=pl.ANY)
     vm = pl.BlockSpec(memory_space=pltpu.VMEM)
+    sm = pl.BlockSpec(memory_space=pltpu.SMEM)
     tokens = tokens.reshape(count, SEG, width)
     segments = (count, SEG, width)
     by_rows = (count, pairs, SEG, two_heads)
@@ -862,7 +932,7 @@
     per_head = (count, pairs, 2, SEG)
     outs = pl.pallas_call(
         lambda *refs: front_kernel(count, chunks, group, orders, *refs),
-        in_specs=[anywhere] * 10 + [vm] * 5,
+        in_specs=[anywhere] * 11 + [sm] + [vm] * 4,
         out_specs=[anywhere] * (10 + EARLY) + [vm] * 11,
         out_shape=[
             struct(segments, BF16), struct(segments, F32), struct(segments, BF16),
@@ -890,7 +960,8 @@
             pltpu.VMEM(slot_wide, BF16), pltpu.VMEM((SEG, SEG), F32), pltpu.VMEM(square, F32),
             pltpu.VMEM((width, SEG), F32), pltpu.VMEM((width, SEG), F32),
             pltpu.VMEM(segments, BF16), pltpu.VMEM((chunks - EARLY, blocks, TILE, width), BF16),
-            pltpu.SemaphoreType.DMA((2 * count + 6 + 2 * chunks,)),
+            pltpu.VMEM((1, rows), F32),
+            pltpu.SemaphoreType.DMA((2 * count + 7 + 2 * chunks,)),
             pltpu.SemaphoreType.DMA((9, count)),
             pltpu.SemaphoreType.DMA((2, 2, group)),
             pltpu.SemaphoreType.DMA((chunks,)),
@@ -899,9 +970,9 @@
         compiler_params=params(0),
         name="front",
     )(
-        tokens, jnp.stack([memory[0], memory_cotangent[0]]), query_weight, key_weight, value_weight,
+        tokens, memory[0], memory_cotangent[0], query_weight, key_weight, value_weight,
         slot_query_weight, out_weight, up_weight, down_weight.reshape(chunks, SEG, width),
-        out_cotangent.reshape(segments), doc, pad, gain1, gain2, gain3,
+        out_cotangent.reshape(segments), doc_lengths, pad, gain1, gain2, gain3,
     )
     layer_out, res_grad, low, q_t, k, k_t, v, v_t, d_t, late = outs[:10]
     early = list(outs[10 : 10 + EARLY])
@@ -913,7 +984,7 @@
     n_sum = len(sizes)
     outs = pl.pallas_call(
         lambda *refs: back_kernel(count, group, orders, sizes, *refs),
-        in_specs=[anywhere] * 17 + [vm] * 15,
+        in_specs=[anywhere] * 17 + [vm] * 2 + [sm] + [vm] * 12,
         out_specs=[anywhere] * (1 + n_sum) + [vm] * 7,
         out_shape=[struct(segments, F32)]
         + [struct((n, TILE, width), BF16) for n in sizes]
@@ -935,6 +1006,7 @@
             pltpu.VMEM((group, slots_here, width), F32), pltpu.VMEM((slots, width), BF16),
             pltpu.VMEM((1, width), F32), pltpu.VMEM((1, width), F32), pltpu.VMEM((1, width), F32),
             pltpu.VMEM((group, slots_here, width), F32), pltpu.VMEM((group, slots_here, width), F32),
+            pltpu.VMEM((1, rows), F32),
             pltpu.SemaphoreType.DMA((2, group)), pltpu.SemaphoreType.DMA((9, count)),
             pltpu.SemaphoreType.DMA((6 + n_sum,)), pltpu.SemaphoreType.DMA((n_sum,)),
         ]
@@ -945,37 +1017,48 @@
         tokens, low, q_t, k, k_t, v, v_t, d_t.reshape(by_lanes), res_grad,
         query_weight, key_weight, value_weight, slot_query_weight, gate_weight, write_weight,
         late, tiles(dwo),
-        lse, inner, doc, pad, gain1, gain3, slot_k, slot_kt, slot_v, slot_q, slot_qt, mem, stats,
+        lse, inner, doc_lengths, pad, gain1, gain3, slot_k, slot_kt, slot_v, slot_q, slot_qt, mem, stats,
         gate_bias[None, :], dgain2,
     )
-    input_grad = outs[0].reshape(rows, width)
-    sums = outs[1 : 1 + n_sum]
+    input_grad = outs[0]
+    sums = list(outs[1 : 1 + n_sum])
     dwq, dwk, dwv, dwsq, gains, memory_grad, new_memory = outs[1 + n_sum :]
-    ffn = early + list(sums[:-1])
-    dwup = jnp.concatenate([f[:half].reshape(width, SEG) for f in ffn], 1)
-    dwdown = jnp.concatenate([f[half:].reshape(SEG, width) for f in ffn], 0)
-    dwo, dwgate, dwwrite = (
-        sums[-1][n * half : (n + 1) * half].reshape(width, width) for n in range(3)
-    )
-
+    ffn = early + sums[:-1]
+    low_jobs = 7 + 2 * chunks
+    outs = pl.pallas_call(
+        lambda *refs: widen_kernel(chunks, half, *refs),
+        in_specs=[anywhere] * (chunks + 10),
+        out_specs=[anywhere] * 17,
+        out_shape=[
+            struct(segments, BF16), struct((slots_here, width), F32), struct(segments, F32),
+            struct((slots_here, width), F32),
+        ]
+        + [struct(square, F32)] * 7
+        + [struct((width, hidden), F32), struct((hidden, width), F32)]
+        + [struct((1, width), F32)] * 4,
+        scratch_shapes=[
+            pltpu.VMEM(segments, BF16), pltpu.VMEM(segments, F32),
+            pltpu.VMEM((2, slots_here, width), F32), pltpu.VMEM((32, width), F32),
+            pltpu.VMEM((low_jobs, half, TILE, width), BF16), pltpu.VMEM((low_jobs, width, width), F32),
+        ]
+        + [pltpu.VMEM((1, width), F32)] * 4
+        + [
+            pltpu.SemaphoreType.DMA((2 * count + 3 + low_jobs,)),
+            pltpu.SemaphoreType.DMA((2 * count + 6 + low_jobs,)),
+        ],
+        compiler_params=pltpu.CompilerParams(vmem_limit_bytes=63 << 20),
+        name="widen",
+    )(
+        *ffn, sums[-1], tiles(dwq), tiles(dwk), tiles(dwv), tiles(dwsq),
+        layer_out, input_grad, new_memory, memory_grad, gains,
+    )
+    layer_out, new_memory, input_grad, memory_grad = outs[:4]
+    dwq, dwk, dwv, dwo, dwsq, dwgate, dwwrite, dwup, dwdown = outs[4:13]
+    gain1, gain2, gain3, bias = (r[0] for r in outs[13:])
     return (
-        layer_out.reshape(rows, width),
-        new_memory[None],
-        input_grad,
-        memory_grad[None],
-        gains[0],
-        dwq.astype(F32),
-        dwk.astype(F32),
-        dwv.astype(F32),
-        dwo.astype(F32),
-        gains[16],
-        dwup.astype(F32),
-        dwdown.astype(F32),
-        gains[8],
-        dwsq.astype(F32),
-        dwgate.astype(F32),
-        gains[24],
-        dwwrite.astype(F32),
+        layer_out.reshape(rows, width), new_memory[None], input_grad.reshape(rows, width),
+        memory_grad[None], gain1, dwq, dwk, dwv, dwo, gain2, dwup, dwdown, gain3, dwsq, dwgate,
+        bias, dwwrite,
     )
 
 

time: 262 us -> 244 us (0.931)
  other arithmetic: 19.4 us -> 0 us
  Pallas kernels: 230 us -> 243 us
  local copies, waits for them, and re-layouts: 11 us -> 0 us
    convert_element_type x11 -> x0, other arithmetic: 17.1 us -> none  [the longest x1 2.61 us: body(): dwdown.astype(F32)]
    pallas_call x0 -> x1, Pallas kernels: none -> 12.5 us  [body(): pl.pallas_call(lambda *refs: widen_kernel(chunks, half, *refs), in_specs=...]
    unnamed x28 -> x0, local copies, waits for them, and re-layouts: 6.52 us -> none
    slice x4 -> x0, local copies, waits for them, and re-layouts: 4.46 us -> none  [the longest x2 2.76 us: body(): dwdown = jnp.concatenate([f[half:].reshape(SEG, width) for f in ffn], 0)]
where the time goes in v4:
time: 244 us
  Pallas kernels  243 us (100%)
    pallas_call x1, Pallas kernels, body(): pl.pallas_call(lambda *refs: back_kernel(count, group, orders, sizes, *re...  119 us
    pallas_call x1, Pallas kernels, body(): pl.pallas_call(lambda *refs: front_kernel(count, chunks, group, orders, *...  111 us
    pallas_call x1, Pallas kernels, body(): pl.pallas_call(lambda *refs: widen_kernel(chunks, half, *refs), in_specs=...  12.5 us

profile of v4, /device:TPU:0, one launch (start us, length us, event | category | flops | bytes accessed | tf_op | source)
XLA Modules:
  0.0 243.8 jit_solution(5736529845189143040)
XLA Ops:
  0.7 111.1 %front.1 = (bf16[4,512,512]{2,1,0:T(8,128)(2,1)}, f32[4,512,512]{2,1,0:T(8,128)}, bf16[4,512,512]{2,1,0:T(8,128)(2,1)}, bf16[4,4,128,512]{3,2,1,0:T(8,128)(2,1)}...) custom-call(bf16[4,512,512]{2,1,0:T(8,128)(2,1)} %bitcast.24, ...), custom_call_target="tpu_custom_call" | custom-call | tf_op jit(solution)/shard_map/front/pallas_call | solution.py:933
  111.8 119.3 %back.1 = (f32[4,512,512]{2,1,0:T(8,128)}, bf16[64,16,512]{2,1,0:T(8,128)(2,1)}, bf16[64,16,512]{2,1,0:T(8,128)(2,1)}, bf16[96,16,512]{2,1,0:T(8,128)(2,1)}, bf1...) custom-call(bf16[4,512,512]{2,1,0:T(8,128)(2,1)} %bitcast.25, ...), custom_call_target="tpu_custom_call" | custom-call | tf_op jit(solution)/shard_map/back/pallas_call | solution.py:985
  231.1 12.5 %widen.1 = (bf16[4,512,512]{2,1,0:T(8,128)(2,1)}, f32[16,512]{1,0:T(8,128)}, f32[4,512,512]{2,1,0:T(8,128)}, f32[16,512]{1,0:T(8,128)}, f32[512,512]{1,0:T(8,128...) custom-call(bf16[64,16,512]{2,1,0:T(8,128)(2,1)} %get-tuple-element., ...), custom_call_target="tpu_custom_call" | custom-call | tf_op jit(solution)/shard_map/widen/pallas_call | solution.py:1028

commit v5 on v4

--- a/solution.py
+++ b/solution.py
@@ -111,6 +111,10 @@
 MESH = pl.DeviceIdType.MESH
 
 
+PARTS = 2
+WHOLE = 2
+
+
 def bit_orders(sizes):
     dp = [("dp", 1 << n) for n in range(sizes["dp"].bit_length() - 1)]
     slot = [("slot", 1 << n) for n in range(sizes["slot"].bit_length() - 1)]
@@ -119,17 +123,17 @@
 
 
 def plan(blocks, orders):
-    half = blocks // 2
+    parts = min(blocks, len(orders))
     steps, recv = [], 0
-    for n, order in enumerate(orders):
-        size, row = half, []
-        for axis, stride in order:
-            halves = size % 2 == 0
+    for n, order in enumerate(orders[:parts]):
+        size, row = blocks // parts, []
+        for level, (axis, stride) in enumerate(order):
+            halves = size % 2 == 0 and level < len(order) - WHOLE
             sent = size // 2 if halves else size
             row.append((axis, stride, halves, sent, recv))
             recv += sent
             size = sent
-        steps.append((n * half, row))
+        steps.append((n * (blocks // parts), row))
     return steps, recv
 
 
@@ -252,8 +256,8 @@
         [pltpu.VMEM((s, TILE, width), BF16) for s in sizes]
         + [pltpu.VMEM((plan(s, orders)[1], TILE, width), BF16) for s in sizes]
         + [
-            pltpu.SemaphoreType.DMA((4, len(sizes) * 2 * depth)),
-            pltpu.SemaphoreType.REGULAR((len(sizes) * 2 * depth,)),
+            pltpu.SemaphoreType.DMA((4, len(sizes) * PARTS * depth)),
+            pltpu.SemaphoreType.REGULAR((len(sizes) * PARTS * depth,)),
         ]
     )
 
@@ -261,7 +265,7 @@
 def reductions(refs, count, orders, index):
     bufs, recvs, (sems, free) = refs[:count], refs[count : 2 * count], refs[2 * count :]
     return [
-        Reduction(bufs[n], recvs[n], sems, free, n * 2 * len(orders[0]), orders, index)
+        Reduction(bufs[n], recvs[n], sems, free, n * PARTS * len(orders[0]), orders, index)
         for n in range(count)
     ]
 
@@ -426,7 +430,7 @@
             pltpu.make_async_copy(work[n].buf, sums[n], late_sems.at[n]).start()
 
     events = [
-        ((n + 1) * count - 1 + stage, summed, (n, stage))
+        ((n + 1) * count - 1 + ((4 - n) * stage) // 2, summed, (n, stage))
         for n in range(EARLY)
         for stage in range(work[n].stages)
     ]
@@ -615,11 +619,11 @@
     def load(n):
         return pltpu.make_async_copy(*whole[n], loads.at[n])
 
-    for n in (0, 1):
+    for n in (*range(6, 5 + early), 0, 1):
         load(n).start()
     for n in range(used):
         block(n, 0).start()
-    for n in range(2, len(whole)):
+    for n in (*range(2, 6), 5 + early):
         load(n).start()
     for i in range(1, count):
         for n in range(used):
@@ -628,6 +632,9 @@
         for n in range(used, len(blocks)):
             block(n, i).start()
     greet(orders, index, group)
+    for n in range(early - 1):
+        load(6 + n).wait()
+        work[n].tick(0)
     doc[...] = documents(lengths, index, group, doc.shape[1])
     load(0).wait()
     load(1).wait()
@@ -636,6 +643,8 @@
         new_memory, g, g_t, wlse, winner, sq_acc, sk_acc, sv_acc, direct,
         work[early - 1].buf.at[third : 2 * third], work[early - 1].buf.at[2 * third :], dbias, fresh,
     )
+    for n in range(early - 1):
+        work[n].tick(1)
     for n in range(2, 6):
         load(n).wait()
     for n in range(pairs):
@@ -697,7 +706,7 @@
 
     def summed(n, stage):
         item = work[n]
-        if n < early and stage == 0:
+        if n == early - 1 and stage == 0:
             load(6 + n).wait()
         item.tick(stage)
         if stage < item.stages - 1:
@@ -713,15 +722,20 @@
     busy = pairs * count
     last = busy + count - 1
     events = []
-    for n in range(early):
-        events += [(n // 2 + stage, summed, (n, stage)) for stage in range(work[n].stages)]
+    for n in range(early - 1):
+        events += [
+            (1 + n + 3 * (stage - 2) // 2, summed, (n, stage)) for stage in range(2, work[n].stages)
+        ]
+    events += [
+        (1 + 3 * stage // 2, summed, (early - 1, stage)) for stage in range(work[early - 1].stages)
+    ]
     for n in range(pairs):
         events += [
-            ((n + 1) * count - 1 + stage, summed, (early + n, stage))
+            ((n + 1) * count - 1 + (stage if n else 3 * stage // 2), summed, (early + n, stage))
             for stage in range(work[early + n].stages)
         ]
     events += [(busy + stage, slot_grads, (stage,)) for stage in range(len(strides) + 1)]
-    events += [(last + stage, gains, (stage,)) for stage in range(work[early + pairs].stages)]
+    events += [(busy + stage, gains, (stage,)) for stage in range(work[early + pairs].stages)]
 
     @pl.loop(0, busy)
     def _(step):
@@ -785,12 +799,15 @@
                 ],
                 0,
             )
+            rows = tiles(rows.astype(BF16))
+            token = acc[...]
             acc[...] = jnp.zeros_like(acc)
-            rows = tiles(rows.astype(BF16))
             for n in range(pairs):
 
                 @pl.when(p == n)
                 def _():
+                    w = jnp.transpose(w_all[:, n * 3 * wide : (n + 1) * 3 * wide]).astype(F32)
+                    dgain[...] += jnp.sum(token * w, 0, keepdims=True) / gain1[...]
                     work[early + n].buf[...] = rows
 
         run_events(step, last, [e for e in events if e[0] < busy])
@@ -801,8 +818,7 @@
         block(used + 1, i).wait()
         unit, inverse = norm(x[i].astype(F32))
         grad_t = nn(w_all[...], grads[i].reshape(3 * pairs * wide, SEG))
-        back, gain_part = norm_back(jnp.transpose(grad_t), unit, inverse, gain1[...])
-        dgain[...] += gain_part
+        back, _ = norm_back(jnp.transpose(grad_t), unit, inverse, gain1[...])
         res[i] += back
         pltpu.make_async_copy(res.at[i], input_grad.at[i], block_loads.at[0, i]).start()
         run_events(i + busy, last, [e for e in events if e[0] >= busy])

time: 244 us -> 231 us (0.947)
  Pallas kernels: 243 us -> 230 us
    pallas_call x1, Pallas kernels: 119 us -> 109 us  [body(): pl.pallas_call(lambda *refs: back_kernel(count, group, orders, sizes, *re...]
    pallas_call x1, Pallas kernels: 111 us -> 108 us  [body(): pl.pallas_call(lambda *refs: front_kernel(count, chunks, group, orders, *...]
where the time goes in v5:
time: 231 us; the launch traced here: 230 us
  Pallas kernels  230 us (100%)
    pallas_call x1, Pallas kernels, body(): pl.pallas_call(lambda *refs: back_kernel(count, group, orders, sizes, *re...  109 us
    pallas_call x1, Pallas kernels, body(): pl.pallas_call(lambda *refs: front_kernel(count, chunks, group, orders, *...  108 us
    pallas_call x1, Pallas kernels, body(): pl.pallas_call(lambda *refs: widen_kernel(chunks, half, *refs), in_specs=...  12.5 us

profile of v5, /device:TPU:0, one launch (start us, length us, event | category | flops | bytes accessed | tf_op | source)
XLA Modules:
  0.0 230.4 jit_solution(16334186375995629937)
XLA Ops:
  0.7 108.0 %front.1 = (bf16[4,512,512]{2,1,0:T(8,128)(2,1)}, f32[4,512,512]{2,1,0:T(8,128)}, bf16[4,512,512]{2,1,0:T(8,128)(2,1)}, bf16[4,4,128,512]{3,2,1,0:T(8,128)(2,1)}...) custom-call(bf16[4,512,512]{2,1,0:T(8,128)(2,1)} %bitcast.24, ...), custom_call_target="tpu_custom_call" | custom-call | tf_op jit(solution)/shard_map/front/pallas_call | solution.py:949
  108.6 109.0 %back.1 = (f32[4,512,512]{2,1,0:T(8,128)}, bf16[64,16,512]{2,1,0:T(8,128)(2,1)}, bf16[64,16,512]{2,1,0:T(8,128)(2,1)}, bf16[96,16,512]{2,1,0:T(8,128)(2,1)}, bf1...) custom-call(bf16[4,512,512]{2,1,0:T(8,128)(2,1)} %bitcast.25, ...), custom_call_target="tpu_custom_call" | custom-call | tf_op jit(solution)/shard_map/back/pallas_call | solution.py:1001
  217.7 12.5 %widen.1 = (bf16[4,512,512]{2,1,0:T(8,128)(2,1)}, f32[16,512]{1,0:T(8,128)}, f32[4,512,512]{2,1,0:T(8,128)}, f32[16,512]{1,0:T(8,128)}, f32[512,512]{1,0:T(8,128...) custom-call(bf16[64,16,512]{2,1,0:T(8,128)(2,1)} %get-tuple-element., ...), custom_call_target="tpu_custom_call" | custom-call | tf_op jit(solution)/shard_map/widen/pallas_call | solution.py:1044

commit v6 on v5

--- a/solution.py
+++ b/solution.py
@@ -724,14 +724,14 @@
     events = []
     for n in range(early - 1):
         events += [
-            (1 + n + 3 * (stage - 2) // 2, summed, (n, stage)) for stage in range(2, work[n].stages)
+            (1 + n + 5 * (stage - 2) // 2, summed, (n, stage)) for stage in range(2, work[n].stages)
         ]
     events += [
-        (1 + 3 * stage // 2, summed, (early - 1, stage)) for stage in range(work[early - 1].stages)
+        (2 + 2 * stage, summed, (early - 1, stage)) for stage in range(work[early - 1].stages)
     ]
     for n in range(pairs):
         events += [
-            ((n + 1) * count - 1 + (stage if n else 3 * stage // 2), summed, (early + n, stage))
+            ((n + 1) * count - 1 + (stage if n > 1 else (4 - n) * stage // 2), summed, (early + n, stage))
             for stage in range(work[early + n].stages)
         ]
     events += [(busy + stage, slot_grads, (stage,)) for stage in range(len(strides) + 1)]

time: 231 us -> 220 us (0.952)
  Pallas kernels: 230 us -> 219 us
    pallas_call x1, Pallas kernels: 109 us -> 98.9 us  [body(): pl.pallas_call(lambda *refs: back_kernel(count, group, orders, sizes, *re...]
where the time goes in v6:
time: 220 us
  Pallas kernels  219 us (100%)
    pallas_call x1, Pallas kernels, body(): pl.pallas_call(lambda *refs: front_kernel(count, chunks, group, orders, *...  108 us
    pallas_call x1, Pallas kernels, body(): pl.pallas_call(lambda *refs: back_kernel(count, group, orders, sizes, *re...  98.9 us
    pallas_call x1, Pallas kernels, body(): pl.pallas_call(lambda *refs: widen_kernel(chunks, half, *refs), in_specs=...  12.5 us

profile of v6, /device:TPU:0, one launch (start us, length us, event | category | flops | bytes accessed | tf_op | source)
XLA Modules:
  0.0 220.3 jit_solution(17734393736557341297)
XLA Ops:
  0.7 108.0 %front.1 = (bf16[4,512,512]{2,1,0:T(8,128)(2,1)}, f32[4,512,512]{2,1,0:T(8,128)}, bf16[4,512,512]{2,1,0:T(8,128)(2,1)}, bf16[4,4,128,512]{3,2,1,0:T(8,128)(2,1)}...) custom-call(bf16[4,512,512]{2,1,0:T(8,128)(2,1)} %bitcast.24, ...), custom_call_target="tpu_custom_call" | custom-call | tf_op jit(solution)/shard_map/front/pallas_call | solution.py:949
  108.6 98.9 %back.1 = (f32[4,512,512]{2,1,0:T(8,128)}, bf16[64,16,512]{2,1,0:T(8,128)(2,1)}, bf16[64,16,512]{2,1,0:T(8,128)(2,1)}, bf16[96,16,512]{2,1,0:T(8,128)(2,1)}, bf1...) custom-call(bf16[4,512,512]{2,1,0:T(8,128)(2,1)} %bitcast.25, ...), custom_call_target="tpu_custom_call" | custom-call | tf_op jit(solution)/shard_map/back/pallas_call | solution.py:1001
  207.6 12.5 %widen.1 = (bf16[4,512,512]{2,1,0:T(8,128)(2,1)}, f32[16,512]{1,0:T(8,128)}, f32[4,512,512]{2,1,0:T(8,128)}, f32[16,512]{1,0:T(8,128)}, f32[512,512]{1,0:T(8,128...) custom-call(bf16[64,16,512]{2,1,0:T(8,128)(2,1)} %get-tuple-element., ...), custom_call_target="tpu_custom_call" | custom-call | tf_op jit(solution)/shard_map/widen/pallas_call | solution.py:1044

commit v7 on v6

--- a/solution.py
+++ b/solution.py
@@ -724,7 +724,7 @@
     events = []
     for n in range(early - 1):
         events += [
-            (1 + n + 5 * (stage - 2) // 2, summed, (n, stage)) for stage in range(2, work[n].stages)
+            (1 + n + (6 - n) * (stage - 2) // 2, summed, (n, stage)) for stage in range(2, work[n].stages)
         ]
     events += [
         (2 + 2 * stage, summed, (early - 1, stage)) for stage in range(work[early - 1].stages)

time: 220 us -> 225 us (1.023)
  Pallas kernels: 219 us -> 224 us
    pallas_call x1, Pallas kernels: 98.9 us -> 103 us  [body(): pl.pallas_call(lambda *refs: back_kernel(count, group, orders, sizes, *re...]
where the time goes in v7:
time: 225 us
  Pallas kernels  224 us (100%)
    pallas_call x1, Pallas kernels, body(): pl.pallas_call(lambda *refs: front_kernel(count, chunks, group, orders, *...  108 us
    pallas_call x1, Pallas kernels, body(): pl.pallas_call(lambda *refs: back_kernel(count, group, orders, sizes, *re...  103 us
    pallas_call x1, Pallas kernels, body(): pl.pallas_call(lambda *refs: widen_kernel(chunks, half, *refs), in_specs=...  12.5 us

profile of v7, /device:TPU:0, one launch (start us, length us, event | category | flops | bytes accessed | tf_op | source)
XLA Modules:
  0.0 224.7 jit_solution(868610919532492824)
XLA Ops:
  0.7 108.0 %front.1 = (bf16[4,512,512]{2,1,0:T(8,128)(2,1)}, f32[4,512,512]{2,1,0:T(8,128)}, bf16[4,512,512]{2,1,0:T(8,128)(2,1)}, bf16[4,4,128,512]{3,2,1,0:T(8,128)(2,1)}...) custom-call(bf16[4,512,512]{2,1,0:T(8,128)(2,1)} %bitcast.24, ...), custom_call_target="tpu_custom_call" | custom-call | tf_op jit(solution)/shard_map/front/pallas_call | solution.py:949
  108.6 103.4 %back.1 = (f32[4,512,512]{2,1,0:T(8,128)}, bf16[64,16,512]{2,1,0:T(8,128)(2,1)}, bf16[64,16,512]{2,1,0:T(8,128)(2,1)}, bf16[96,16,512]{2,1,0:T(8,128)(2,1)}, bf1...) custom-call(bf16[4,512,512]{2,1,0:T(8,128)(2,1)} %bitcast.25, ...), custom_call_target="tpu_custom_call" | custom-call | tf_op jit(solution)/shard_map/back/pallas_call | solution.py:1001
  212.0 12.5 %widen.1 = (bf16[4,512,512]{2,1,0:T(8,128)(2,1)}, f32[16,512]{1,0:T(8,128)}, f32[4,512,512]{2,1,0:T(8,128)}, f32[16,512]{1,0:T(8,128)}, f32[512,512]{1,0:T(8,128...) custom-call(bf16[64,16,512]{2,1,0:T(8,128)(2,1)} %get-tuple-element., ...), custom_call_target="tpu_custom_call" | custom-call | tf_op jit(solution)/shard_map/widen/pallas_call | solution.py:1044
